TPU v7x, 128 devices: a whole 4x4x4 slice. The times are simulated.
128 devices in a mesh: row: 8 (over x_lo, z), col: 16 (over x_hi, y, core).
Axes of the slice: x: 4 (x_hi: 2, x_lo: 2; x = x_hi * 2 + x_lo), y: 4, z: 4, core: 2. Of those that a mesh axis runs over, the one named last changes fastest.
Arguments:
- tokens: bfloat16 [2048, 4096], P('row', 'col'), may hold values from -6 to 6
- norm_gain: float32 [4096], replicated, may hold values from 0.1 to 1.9
- expert_ids: int32 [2048, 2], P('row'), may hold values from 0 to 7, all different within a row; in each aligned block of 256 rows (0 to 255, 256 to 511, ...) at most 128 rows name the same one
- gate_weights: float32 [2048, 2], P('row'), may hold values from 0.1 to 1
- w_gate: bfloat16 [8, 4096, 14336], P('row', None, 'col'), may hold values from -0.09375 to 0.09375
- w_up: bfloat16 [8, 4096, 14336], P('row', None, 'col'), may hold values from -0.09375 to 0.09375
- w_down: bfloat16 [8, 14336, 4096], P('row', 'col'), may hold values from -0.046875 to 0.046875
Outputs:
- layer_output: bfloat16 [2048, 4096], P('row', 'col')
Inputs may be any that keep to these rules, and one draw needn't show every extreme that they name: `expert_ids`: the 2 experts of a token differ. In each aligned block of 256 tokens no expert is chosen by more than 128 tokens, a bound that some block reaches.
All inputs are finite; a program needn't handle non-finite values.
Results may differ from a plain program's by a relative error of at most 0.0043.
Values may be sent and summed in bfloat16 or wider, within the bound.
A program may use at most 128 MiB of HBM per device.

v0:
```python
import jax
import jax.numpy as jnp
from jax import lax
from jax.sharding import PartitionSpec as P

EXPERTS = 8
CAP = 128


def normalize(rows, norm_gain):
    values = rows.astype(jnp.float32)
    inverse_norm = lax.rsqrt(jnp.mean(values * values, axis=-1, keepdims=True) + 1e-05)
    return (values * inverse_norm * norm_gain).astype(jnp.bfloat16)


def route_tables(expert_ids, expert_count, capacity):
    token_count = expert_ids.shape[0]
    flat_ids = expert_ids.reshape(-1)
    expert_range = jnp.arange(expert_count, dtype=jnp.int32)
    expert_hits = (flat_ids[:, None] == expert_range[None, :]).astype(jnp.int32)
    earlier = jnp.cumsum(expert_hits, axis=0) - expert_hits
    ranks = jnp.sum(earlier * expert_hits, axis=1)
    slot_index = (flat_ids * capacity + ranks).reshape(token_count, -1)
    slot_ids = jnp.arange(expert_count * capacity, dtype=jnp.int32)
    matches = (slot_index[:, :, None] == slot_ids[None, None, :]).astype(jnp.float32)
    picker = jnp.sum(matches, axis=1)
    return (picker.astype(jnp.bfloat16), slot_index)


def combine_rows(slot_rows, slot_index, gate_weights):
    picked = slot_rows[slot_index]
    return jnp.sum(picked * gate_weights[:, :, None], axis=1)


def run_experts(normed, gate_block, up_block, down_block):
    local_count = gate_block.shape[0]
    sources = normed.shape[0] // local_count
    grouped = normed.reshape(sources, local_count, normed.shape[1], normed.shape[2])
    gate_part = jnp.einsum(
        "slcd,ldf->slcf", grouped, gate_block, preferred_element_type=jnp.float32
    )
    up_part = jnp.einsum("slcd,ldf->slcf", grouped, up_block, preferred_element_type=jnp.float32)
    hidden = (jax.nn.silu(gate_part) * up_part).astype(jnp.bfloat16)
    outputs = jnp.einsum("slcf,lfd->slcd", hidden, down_block, preferred_element_type=jnp.float32)
    return outputs.reshape(normed.shape[0], normed.shape[1], down_block.shape[2])


def body(tokens, norm_gain, expert_ids, gate_weights, w_gate, w_up, w_down):
    picker, slot_index = route_tables(expert_ids, EXPERTS, CAP)
    packed = jnp.einsum("ts,td->sd", picker, tokens, preferred_element_type=jnp.float32).astype(
        jnp.bfloat16
    )
    packed = packed.reshape(EXPERTS, CAP, tokens.shape[1])
    arrived = lax.all_to_all(packed, "row", split_axis=0, concat_axis=0, tiled=True)
    widened = lax.all_gather(arrived, "col", axis=2, tiled=True)
    normed = normalize(widened, norm_gain)
    outputs = run_experts(normed, w_gate, w_up, w_down)
    shares = lax.psum_scatter(outputs, "col", scatter_dimension=2, tiled=True)
    returned = lax.all_to_all(shares, "row", split_axis=0, concat_axis=0, tiled=True)
    mixed = combine_rows(returned.reshape(-1, shares.shape[2]), slot_index, gate_weights)
    return (tokens.astype(jnp.float32) + mixed).astype(jnp.bfloat16)


def solution(mesh):
    placed = (
        P("row", "col"),
        P(),
        P("row", None),
        P("row", None),
        P("row", None, "col"),
        P("row", None, "col"),
        P("row", "col", None),
    )
    return jax.shard_map(
        body, mesh=mesh, in_specs=placed, out_specs=P("row", "col"), check_vma=False
    )
```

profile of v0, /device:TPU:0, one launch (start us, length us, event | category | flops | bytes accessed | tf_op | source)
XLA Modules:
  0.0 323.9 jit_solution(4479239125791643411)
XLA Ops:
  6.5 0.0 copy-start.3
  6.5 0.0 all-gather.2.cloned.1.call-start
  6.5 0.8 copy.21
  7.4 0.1 eq.42
  7.5 0.1 eq.38
  7.7 1.1 reduce-window.6
  8.8 0.2 slice_reduce_fusion
  9.1 0.1 fusion.30
  9.2 0.1 reduce_sum.39
  9.3 0.1 copy.23
  9.4 0.7 compare_select_fusion
  10.1 0.3 convert_reduce_fusion
  10.4 1.3 convolution_convert_fusion
  11.6 16.3 %all_to_all.10 = bf16[8,128,256]{2,1,0:T(8,128)(2,1)} all-to-all(bf16[8,128,256]{2,1,0:T(8,128)(2,1)S(1)} %bitcast.67), channel_id=1, replica_groups=mesh['row'=8,'col'=16] {'row'}, dimensions={0} | all-to-all | bytes 1048576 | tf_op jit(solution)/shard_map/all_to_all | solution.py:54
  27.9 0.0 all-gather.2.cloned.1.call-update
  27.9 0.0 reduce-scatter.2.cloned.1.call-start
  28.0 76.0 %all-gather.2.cloned.1.call-done = bf16[8,128,4096]{2,1,0:T(8,128)(2,1)} async-done(((bf16[8,128,256]{2,1,0:T(8,128)(2,1)}), bf16[8,128,4096]{2,1,0:T(8,128)(2,1)}) %all-gather.2.cloned.1.call-update) | async-done | bytes 8388624 | tf_op jit(solution)/shard_map/all_gather | solution.py:55
  104.0 0.0 copy-start
  104.0 5.2 %fusion = f32[8,128]{1,0:T(8,128)S(1)} fusion(bf16[8,128,4096]{2,1,0:T(8,128)(2,1)} %all-gather.2.cloned.1.call-done), kind=kLoop, calls=%fused_computation.3 | loop fusion | flops 12581888 | bytes 8392704 | tf_op jit(solution)/shard_map/reduce_sum | solution.py:12
  109.3 0.0 copy-done.3
  109.3 0.5 copy-done
  109.8 12.5 %fusion.7 = f32[8,128,896]{2,1,0:T(8,128)} fusion(bf16[1,4096,896]{2,1,0:T(8,128)(2,1)} %param.11, bf16[8,128,4096]{2,1,0:T(8,128)(2,1)S(1)} %copy-done, f32[4096]{0:T(1024)S(1)} %copy-done.3, f32[8,128]{1,0:T(8,128)S(1)} %add_rsqrt_fusion), kind=kOutput, calls=%fused_computation.10 | convolution fusion | flops 7532969984 | bytes 19419136 | tf_op jit(solution)/shard_map/slcd,ldf->slcf/dot_general | solution.py:39
  122.3 28.0 %fusion.3 = f32[8,128,4096]{2,1,0:T(8,128)} fusion(bf16[1,896,4096]{2,1,0:T(8,128)(2,1)} %param.13, f32[8,128,896]{2,1,0:T(8,128)} %fusion.7, bf16[1,4096,896]{2,1,0:T(8,128)(2,1)} %param.12, bf16[8,128,4096]{2,1,0:T(8,128)(2,1)} %all-gather.2.cloned.1.call-done, f32[4096]{0:T(1024)S(1)} %copy-done.3, f32[8,128]{1,0:T(8,128)S(1)} %add_rsqrt_fusion), kind=kOutput, calls=%fused_computation.6 | convolution fusion | flops 15054667776 | bytes 43536384 | tf_op jit(solution)/shard_map/slcf,lfd->slcd/dot_general | solution.py:44
  150.4 0.0 copy-start.2
  150.4 0.0 reduce-scatter.2.cloned.1.call-update
  150.4 0.0 copy-start.1
  150.4 144.8 %reduce-scatter.2.cloned.1.call-done = f32[8,128,256]{2,1,0:T(8,128)} async-done(((f32[8,128,4096]{2,1,0:T(8,128)}), f32[8,128,256]{2,1,0:T(8,128)}) %reduce-scatter.2.cloned.1.call-update) | async-done | bytes 1048592 | tf_op jit(solution)/shard_map/reduce_scatter | solution.py:58
  295.2 4.4 %all-to-all-start.1 = ((f32[8,128,256]{2,1,0:T(8,128)}), f32[8,128,256]{2,1,0:T(8,128)S(1)}, u32[]{:S(2)}, u32[]{:S(2)}) async-start(f32[8,128,256]{2,1,0:T(8,128)} %reduce-scatter.2.cloned.1.call-done), calls=%async_computation.2 | async-start | bytes 2097152 | tf_op jit(solution)/shard_map/all_to_all | solution.py:59
  299.6 0.1 copy.24
  299.7 0.1 reshape.72
  299.9 0.0 copy-done.2
  299.9 0.1 copy.25
  300.1 13.7 %all-to-all-done.1 = f32[8,128,256]{2,1,0:T(8,128)S(1)} async-done(((f32[8,128,256]{2,1,0:T(8,128)}), f32[8,128,256]{2,1,0:T(8,128)S(1)}, u32[]{:S(2)}, u32[]{:S(2)}) %all-to-all-start.1) | async-done | bytes 1048608 | tf_op jit(solution)/shard_map/all_to_all | solution.py:59
  313.8 1.6 gather_fusion
  315.4 0.3 reshape.71
  315.7 0.7 multiply_reduce_fusion
  316.4 0.0 copy-done.1
  316.4 0.7 add_convert_fusion
  (5 shorter events, 0.1 us)
Async XLA Ops:
  6.5 102.7 %copy-start.3 = (f32[4096]{0:T(1024)S(1)}, f32[4096]{0:T(1024)}, u32[]{:S(2)}) copy-start(f32[4096]{0:T(1024)} %param.8) | copy-start | bytes 49156
  6.5 97.5 %all-gather.2.cloned.1.call-start = ((), (), s32[]{:S(2)}) async-start(), calls=%async_computation.3 | async-start | bytes 8912896 | tf_op jit(solution)/shard_map/all_gather | solution.py:55
  27.9 267.2 %reduce-scatter.2.cloned.1.call-start = ((), (), s32[]{:S(2)}) async-start(), calls=%async_computation.4 | async-start | bytes 17825792 | tf_op jit(solution)/shard_map/reduce_scatter | solution.py:58
  104.0 5.8 %copy-start = (bf16[8,128,4096]{2,1,0:T(8,128)(2,1)S(1)}, bf16[8,128,4096]{2,1,0:T(8,128)(2,1)}, u32[]{:S(2)}) copy-start(bf16[8,128,4096]{2,1,0:T(8,128)(2,1)} %all-gather.2.cloned.1.call-done) | copy-start | bytes 25165828
  150.4 149.5 %copy-start.2 = (f32[256,2]{0,1:T(2,128)S(1)}, f32[256,2]{0,1:T(2,128)}, u32[]{:S(2)}) copy-start(f32[256,2]{0,1:T(2,128)} %param.10) | copy-start | bytes 6148
  150.4 166.0 %copy-start.1 = (bf16[256,256]{1,0:T(8,128)(2,1)S(1)}, bf16[256,256]{1,0:T(8,128)(2,1)}, u32[]{:S(2)}) copy-start(bf16[256,256]{1,0:T(8,128)(2,1)} %param.7) | copy-start | bytes 393220
  295.2 18.6 %all-to-all-start.1 = ((f32[8,128,256]{2,1,0:T(8,128)}), f32[8,128,256]{2,1,0:T(8,128)S(1)}, u32[]{:S(2)}, u32[]{:S(2)}) async-start(f32[8,128,256]{2,1,0:T(8,128)} %reduce-scatter.2.cloned.1.call-done), calls=%async_computation.2 | async-start | bytes 2097152 | tf_op jit(solution)/shard_map/all_to_all | solution.py:59
Sparse Core Ops, SparseCore 0:
  28.1 75.9 all-gather.1
  150.5 144.6 reduce-scatter.1
where the time goes:
time: 324 us
  waiting for transfers between devices  235 us (73%)
  matrix products  41.8 us (13%)
  blocking collectives  16.3 us (5%)
  between operations  13.5 us (4%)
  other arithmetic  8.85 us (3%)
  starting transfers between devices  4.49 us (1%)
  local copies, waits for them, and re-layouts  4.36 us (1%)
    reduce_scatter x1, waiting for transfers between devices, body(): shares = lax.psum_scatter(outputs, 'col', scatter_dimension=2, tiled=True)  145 us
    all_gather x1, waiting for transfers between devices, body(): widened = lax.all_gather(arrived, 'col', axis=2, tiled=True)  76 us
    dot_general x1, matrix products, run_experts(): jnp.einsum('slcf,lfd->slcd', hidden, down_block, preferred_element_type=j...  28 us
    all_to_all x1, blocking collectives, body(): lax.all_to_all(packed, 'row', split_axis=0, concat_axis=0, tiled=True)  16.3 us
    all_to_all x1, waiting for transfers between devices, body(): lax.all_to_all(shares, 'row', split_axis=0, concat_axis=0, tiled=True)  13.7 us
    dot_general x1, matrix products, run_experts(): jnp.einsum('slcd,ldf->slcf', grouped, gate_block, preferred_element_type=...  12.5 us
  transfers between devices with their start and end apart: 3, of which 3 were waited for; matrix products, arithmetic and copies ran while one was open for 0% of the time, Pallas kernels for 0%

commit v1 on v0

v1 whole, which is shorter than its diff:
```python
import jax
import jax.numpy as jnp
from jax import lax
from jax.sharding import Mesh
from jax.sharding import PartitionSpec as P

EXPERTS = 8
CAP = 128
COL = ("chip", "core")


def route_tables(expert_ids, expert_count, capacity):
    token_count = expert_ids.shape[0]
    flat_ids = expert_ids.reshape(-1)
    expert_range = jnp.arange(expert_count, dtype=jnp.int32)
    expert_hits = (flat_ids[:, None] == expert_range[None, :]).astype(jnp.int32)
    earlier = jnp.cumsum(expert_hits, axis=0) - expert_hits
    ranks = jnp.sum(earlier * expert_hits, axis=1)
    slot_index = (flat_ids * capacity + ranks).reshape(token_count, -1)
    slot_ids = jnp.arange(expert_count * capacity, dtype=jnp.int32)
    matches = (slot_index[:, :, None] == slot_ids[None, None, :]).astype(jnp.float32)
    picker = jnp.sum(matches, axis=1)
    return (picker.astype(jnp.bfloat16), slot_index)


def combine_rows(slot_rows, slot_index, gate_weights):
    picked = slot_rows[slot_index]
    return jnp.sum(picked * gate_weights[:, :, None], axis=1)


def swap_cores(value):
    return lax.ppermute(value, "core", perm=[(0, 1), (1, 0)])


def body(tokens, norm_gain, expert_ids, gate_weights, w_gate, w_up, w_down):
    chips = lax.psum(1, "chip")
    width = tokens.shape[1]
    core = lax.axis_index("core")
    block = lax.axis_index("chip") * 2 + core

    values = tokens.astype(jnp.float32)
    squares = lax.psum(jnp.sum(values * values, axis=-1, keepdims=True), COL)
    inverse_norm = lax.rsqrt(squares / (width * chips * 2) + 1e-05)
    gain = lax.dynamic_slice_in_dim(norm_gain, block * width, width)
    normed = (values * inverse_norm * gain).astype(jnp.bfloat16)

    picker, slot_index = route_tables(expert_ids, EXPERTS, CAP)
    packed = jnp.einsum("ts,td->sd", picker, normed, preferred_element_type=jnp.float32).astype(
        jnp.bfloat16
    )
    packed = packed.reshape(EXPERTS, CAP, width)
    arrived = lax.all_to_all(packed, "row", split_axis=0, concat_axis=0, tiled=True)
    arrived = arrived.reshape(EXPERTS * CAP, width)

    mine = lax.all_gather(arrived, "chip", axis=0, tiled=False)
    other = swap_cores(mine)
    pair = jnp.where(core == 0, jnp.stack([mine, other], 1), jnp.stack([other, mine], 1))
    slots = arrived.shape[0]
    widened = jnp.transpose(pair, (2, 0, 1, 3)).reshape(slots, chips * 2 * width)

    gate_part = jnp.dot(widened, w_gate[0], preferred_element_type=jnp.float32)
    up_part = jnp.dot(widened, w_up[0], preferred_element_type=jnp.float32)
    hidden = (jax.nn.silu(gate_part) * up_part).astype(jnp.bfloat16)
    outputs = jnp.dot(hidden, w_down[0], preferred_element_type=jnp.float32)

    split = outputs.reshape(slots, chips, 2, width)
    keep = jnp.where(core == 0, split[:, :, 0], split[:, :, 1])
    give = jnp.where(core == 0, split[:, :, 1], split[:, :, 0])
    summed = keep + swap_cores(give)
    shares = lax.psum_scatter(summed, "chip", scatter_dimension=1, tiled=True)
    shares = shares.reshape(EXPERTS, CAP, width)
    returned = lax.all_to_all(shares, "row", split_axis=0, concat_axis=0, tiled=True)
    mixed = combine_rows(returned.reshape(-1, width), slot_index, gate_weights)
    return (tokens.astype(jnp.float32) + mixed).astype(jnp.bfloat16)


def solution(mesh):
    rows, cols = mesh.devices.shape
    split_mesh = Mesh(mesh.devices.reshape(rows, cols // 2, 2), ("row", "chip", "core"))
    placed = (
        P("row", COL),
        P(),
        P("row", None),
        P("row", None),
        P("row", None, COL),
        P("row", None, COL),
        P("row", COL, None),
    )
    return jax.shard_map(
        body, mesh=split_mesh, in_specs=placed, out_specs=P("row", COL), check_vma=False
    )
```

time: 324 us -> 372 us (1.15)
  blocking collectives: 16.3 us -> 52 us
  waiting for transfers between devices: 235 us -> 206 us
  other arithmetic: 8.85 us -> 32.7 us
  local copies, waits for them, and re-layouts: 4.36 us -> 21.9 us
    psum x0 -> x1, blocking collectives: none -> 38.1 us  [body(): squares = lax.psum(jnp.sum(values * values, axis=-1, keepdims=True), COL)]
    reduce_scatter x1, waiting for transfers between devices: 145 us -> 113 us  [body(): shares = lax.psum_scatter(summed, 'chip', scatter_dimension=1, tiled=True)]
    select_n x0 -> x2, other arithmetic: none -> 18 us  [the longest x1 10.1 us: body(): give = jnp.where(core == 0, split[:, :, 1], split[:, :, 0])]
    ppermute x0 -> x2, waiting for transfers between devices: none -> 13 us  [swap_cores(): return lax.ppermute(value, 'core', perm=[(0, 1), (1, 0)])]
    dot_general x0 -> x1, local copies, waits for them, and re-layouts: none -> 10.8 us  [body(): outputs = jnp.dot(hidden, w_down[0], preferred_element_type=jnp.float32)]
    add x0 -> x1, other arithmetic: none -> 10 us  [body(): summed = keep + swap_cores(give)]
    all_gather x1, waiting for transfers between devices: 76 us -> 67 us  [body(): mine = lax.all_gather(arrived, 'chip', axis=0, tiled=False)]
    all_gather x0 -> x1, local copies, waits for them, and re-layouts: none -> 6.45 us  [body(): mine = lax.all_gather(arrived, 'chip', axis=0, tiled=False)]
  transfers between devices with their start and end apart: 3 -> 5, of which waited for: 3 -> 4; matrix products, arithmetic and copies ran while one was open for 0% -> 3% of each run, Pallas kernels for 0% -> 0%
where the time goes in v1:
time: 372 us; the launch traced here: 371 us
  waiting for transfers between devices  206 us (55%)
  blocking collectives  52 us (14%)
  matrix products  39.2 us (11%)
  other arithmetic  32.7 us (9%)
  local copies, waits for them, and re-layouts  21.9 us (6%)
  between operations  13.6 us (4%)
  starting transfers between devices  4.98 us (1%)
    reduce_scatter x1, waiting for transfers between devices, body(): shares = lax.psum_scatter(summed, 'chip', scatter_dimension=1, tiled=True)  113 us
    all_gather x1, waiting for transfers between devices, body(): mine = lax.all_gather(arrived, 'chip', axis=0, tiled=False)  67 us
    psum x1, blocking collectives, body(): squares = lax.psum(jnp.sum(values * values, axis=-1, keepdims=True), COL)  38.1 us
    all_to_all x1, blocking collectives, body(): lax.all_to_all(packed, 'row', split_axis=0, concat_axis=0, tiled=True)  13.9 us
    dot_general x1, matrix products, body(): outputs = jnp.dot(hidden, w_down[0], preferred_element_type=jnp.float32)  13.8 us
    all_to_all x1, waiting for transfers between devices, body(): lax.all_to_all(shares, 'row', split_axis=0, concat_axis=0, tiled=True)  13.7 us
    dot_general x1, matrix products, body(): up_part = jnp.dot(widened, w_up[0], preferred_element_type=jnp.float32)  13 us
    ppermute x2, waiting for transfers between devices, swap_cores(): return lax.ppermute(value, 'core', perm=[(0, 1), (1, 0)])  13 us
  transfers between devices with their start and end apart: 5, of which 4 were waited for; matrix products, arithmetic and copies ran while one was open for 3% of the time, Pallas kernels for 0%

profile of v1, /device:TPU:0, one launch (start us, length us, event | category | flops | bytes accessed | tf_op | source)
XLA Modules:
  0.0 370.8 jit_solution(8695487437753940584)
XLA Ops:
  6.5 0.0 all-gather.2.cloned.1.call-start
  6.5 0.8 copy.51
  7.4 0.1 eq.48
  7.5 0.1 eq.44
  7.7 1.1 reduce-window.6
  8.8 0.2 slice_reduce_fusion
  9.1 0.1 fusion.17
  9.2 0.1 reduce_sum.39
  9.3 0.1 copy.53
  9.4 0.7 compare_select_fusion
  10.1 0.3 convert_reduce_fusion
  10.4 1.0 fusion.9
  11.4 38.1 %psum.7 = f32[256,1]{0,1:T(1,128)S(1)} all-reduce(f32[256,1]{0,1:T(1,128)S(1)} %bitcast.67), channel_id=1, replica_groups=mesh['row'=8,'chip'=8,'core'=2] {'chip','core'}, use_global_device_ids=true, to_apply=%region_5.6 | all-reduce | flops 256 | bytes 2048 | tf_op jit(solution)/shard_map/psum | solution.py:42
  49.5 0.8 dynamic_slice.3
  50.3 1.3 convolution_convert_fusion
  51.6 13.9 %all_to_all.10 = bf16[8,128,256]{2,1,0:T(8,128)(2,1)} all-to-all(bf16[8,128,256]{2,1,0:T(8,128)(2,1)S(1)} %bitcast.66), channel_id=1, replica_groups=mesh['row'=8,'chip'=8,'core'=2] {'row'}, dimensions={0} | all-to-all | bytes 1048576 | tf_op jit(solution)/shard_map/all_to_all | solution.py:52
  65.5 0.0 all-gather.2.cloned.1.call-update
  65.5 0.0 reduce-scatter.2.cloned.1.call-start
  65.5 67.0 %all-gather.2.cloned.1.call-done = bf16[8,1024,256]{2,1,0:T(8,128)(2,1)} async-done(((bf16[1,1024,256]{2,1,0:T(8,128)(2,1)}), bf16[8,1024,256]{2,1,0:T(8,128)(2,1)}) %all-gather.2.cloned.1.call-update) | async-done | bytes 4194320 | tf_op jit(solution)/shard_map/all_gather | solution.py:55
  132.6 6.4 %copy.54 = bf16[8,1024,256]{1,2,0:T(8,128)(2,1)} copy(bf16[8,1024,256]{2,1,0:T(8,128)(2,1)} %all-gather.2.cloned.1.call-done) | data formatting | bytes 8388608 | tf_op jit(solution)/shard_map/all_gather | solution.py:55
  139.0 0.0 collective-permute-start
  139.0 10.8 %copy.64 = bf16[4096,896]{1,0:T(8,128)(2,1)} copy(bf16[4096,896]{0,1:T(8,128)(2,1)} %bitcast.60) | data formatting | bytes 14680064 | tf_op jit(solution)/shard_map/dot_general | solution.py:64
  149.8 0.0 collective-permute-done
  149.8 7.9 %maximum_select_fusion = bf16[8,2,1024,256]{2,3,1,0:T(8,128)(2,1)S(1)} fusion(bf16[8,1,1024,256]{2,3,1,0:T(8,128)(2,1)} %bitcast.7, bf16[8,1,1024,256]{2,3,1,0:T(8,128)(2,1)} %bitcast.57, pred[]{:T(512)S(6)} %eq.43), kind=kLoop, calls=%fused_computation.1 | loop fusion | flops 12582912 | bytes 16777216 | tf_op jit(solution)/shard_map/jit(_where)/select_n | solution.py:57
  157.8 0.0 slice-start.3
  157.8 0.0 slice-start
  157.8 13.0 %fusion.2 = f32[1024,896]{1,0:T(8,128)S(1)} fusion(bf16[1024,4096]{0,1:T(8,128)(2,1)S(1)} %bitcast.58, bf16[1,4096,896]{2,1,0:T(8,128)(2,1)} %param.12), kind=kOutput, calls=%fused_computation.6 | convolution fusion | flops 7516192768 | bytes 19398656 | tf_op jit(solution)/shard_map/dot_general | solution.py:62
  170.8 0.0 slice-done.2
  170.8 0.0 slice-done.3
  170.9 0.0 slice-start.1
  170.9 11.1 %fusion.4 = f32[1024,896]{1,0:T(8,128)} fusion(bf16[1024,4096]{0,1:T(8,128)(2,1)S(1)} %bitcast.59, bf16[1,4096,896]{2,1,0:T(8,128)(2,1)S(1)} %bitcast.70), kind=kOutput, calls=%fused_computation.8 | convolution fusion | flops 7516192768 | bytes 19398656 | tf_op jit(solution)/shard_map/dot_general | solution.py:61
  182.0 0.0 slice-done.1
  182.0 13.8 %fusion.6 = f32[1024,8,2,256]{3,0,2,1:T(8,128)} fusion(bf16[8,2,256,896]{3,2,1,0:T(8,128)(2,1)S(1)} %bitcast.63, f32[1024,896]{1,0:T(8,128)S(1)} %fusion.2, f32[1024,896]{1,0:T(8,128)} %fusion.4), kind=kOutput, calls=%fused_computation.13 | convolution fusion | flops 7521697792 | bytes 31457280 | tf_op jit(solution)/shard_map/dot_general | solution.py:64
  195.8 10.1 %select_bitcast_fusion = f32[1024,8,256]{2,0,1:T(8,128)} fusion(f32[1024,8,2,256]{3,0,2,1:T(8,128)} %fusion.6, pred[]{:T(512)S(6)} %eq.43), kind=kLoop, calls=%fused_computation.5 | loop fusion | flops 2097152 | bytes 25165824 | tf_op jit(solution)/shard_map/jit(_where)/select_n | solution.py:68
  205.8 0.5 collective-permute-start.1
  206.3 13.0 %collective-permute-done.1 = f32[1024,8,256]{2,0,1:T(8,128)S(1)} collective-permute-done((f32[1024,8,256]{2,0,1:T(8,128)}, f32[1024,8,256]{2,0,1:T(8,128)S(1)}, u32[]{:S(2)}, u32[]{:S(2)}) %collective-permute-start.1) | collective-permute-done | bytes 8388640 | tf_op jit(solution)/shard_map/ppermute | solution.py:32
  219.3 10.0 %fusion.1 = f32[1024,8,256]{2,0,1:T(8,128)} fusion(f32[1024,8,256]{2,0,1:T(8,128)S(1)} %collective-permute-done.1, f32[1024,8,2,256]{3,0,2,1:T(8,128)} %fusion.6, pred[]{:T(512)S(6)} %eq.43), kind=kLoop, calls=%fused_computation.4 | loop fusion | flops 4194304 | bytes 33554432 | tf_op jit(solution)/shard_map/add | solution.py:69
  229.4 0.0 reduce-scatter.2.cloned.1.call-update
  229.4 112.7 %reduce-scatter.2.cloned.1.call-done = f32[1024,1,256]{2,0,1:T(8,128)} async-done(((f32[1024,8,256]{2,0,1:T(8,128)}), f32[1024,1,256]{2,0,1:T(8,128)}) %reduce-scatter.2.cloned.1.call-update) | async-done | bytes 1048592 | tf_op jit(solution)/shard_map/reduce_scatter | solution.py:70
  342.1 4.4 %all-to-all-start.1 = ((f32[8,128,256]{2,1,0:T(8,128)}), f32[8,128,256]{2,1,0:T(8,128)S(1)}, u32[]{:S(2)}, u32[]{:S(2)}) async-start(f32[8,128,256]{2,1,0:T(8,128)} %bitcast.65), calls=%async_computation.2 | async-start | bytes 2097152 | tf_op jit(solution)/shard_map/all_to_all | solution.py:72
  346.5 0.1 copy.61
  346.6 0.1 reshape.53
  346.8 0.1 copy.62
  347.0 13.7 %all-to-all-done.1 = f32[8,128,256]{2,1,0:T(8,128)S(1)} async-done(((f32[8,128,256]{2,1,0:T(8,128)}), f32[8,128,256]{2,1,0:T(8,128)S(1)}, u32[]{:S(2)}, u32[]{:S(2)}) %all-to-all-start.1) | async-done | bytes 1048608 | tf_op jit(solution)/shard_map/all_to_all | solution.py:72
  360.7 1.6 gather_fusion
  362.3 0.3 reshape.52
  362.6 0.7 multiply_reduce_fusion
  363.3 0.7 fusion.12
  (13 shorter events, 0.1 us)
Async XLA Ops:
  6.5 126.0 %all-gather.2.cloned.1.call-start = ((), (), s32[]{:S(2)}) async-start(), calls=%async_computation.3 | async-start | bytes 4718592 | tf_op jit(solution)/shard_map/all_gather | solution.py:55
  65.5 276.6 %reduce-scatter.2.cloned.1.call-start = ((), (), s32[]{:S(2)}) async-start(), calls=%async_computation.4 | async-start | bytes 9437184 | tf_op jit(solution)/shard_map/reduce_scatter | solution.py:70
  139.0 10.8 %collective-permute-start = (bf16[8,1024,256]{1,2,0:T(8,128)(2,1)}, bf16[8,1024,256]{1,2,0:T(8,128)(2,1)}, u32[]{:S(2)}, u32[]{:S(2)}) collective-permute-start(bf16[8,1024,256]{1,2,0:T(8,128)(2,1)} %copy.54), channel_id=1, source_target_pairs={{0,1},{1,0},{2,3},{3,2},{4,5},{5,4},{6,7},{7,6},{8,9},{9,8},{10,11... | collective-permute-start | bytes 12582920 | tf_op jit(solution)/shard_map/ppermute | solution.py:32
  149.8 21.0 %slice-start.2 = ((s8[7340032]{0:T(1024)(128)(4,1)}), s8[4194304]{0:T(1024)(128)(4,1)S(1)}, s32[]{:S(2)}) async-start(s8[7340032]{0:T(1024)(128)(4,1)} %bitcast.69), calls=%async_computation.7 | async-start | bytes 8388608
  157.8 13.1 %slice-start.3 = ((s8[7340032]{0:T(1024)(128)(4,1)}), s8[3145728]{0:T(1024)(128)(4,1)S(1)}, s32[]{:S(2)}) async-start(s8[7340032]{0:T(1024)(128)(4,1)} %bitcast.69), calls=%async_computation.8 | async-start | bytes 6291456
  157.8 24.2 %slice-start = ((s8[7340032]{0:T(1024)(128)(4,1)}), s8[4194304]{0:T(1024)(128)(4,1)S(1)}, s32[]{:S(2)}) async-start(s8[7340032]{0:T(1024)(128)(4,1)} %bitcast.61), calls=%async_computation.5 | async-start | bytes 8388608
  170.9 11.1 %slice-start.1 = ((s8[7340032]{0:T(1024)(128)(4,1)}), s8[3145728]{0:T(1024)(128)(4,1)S(1)}, s32[]{:S(2)}) async-start(s8[7340032]{0:T(1024)(128)(4,1)} %bitcast.61), calls=%async_computation.6 | async-start | bytes 6291456
  205.8 13.5 %collective-permute-start.1 = (f32[1024,8,256]{2,0,1:T(8,128)}, f32[1024,8,256]{2,0,1:T(8,128)S(1)}, u32[]{:S(2)}, u32[]{:S(2)}) collective-permute-start(f32[1024,8,256]{2,0,1:T(8,128)} %select_bitcast_fusion), channel_id=1, source_target_pairs={{0,1},{1,0},{2,3},{3,2},{4,5},{5,4},{6,7},{7,6},{8,9},{9,8},{10,11... | collective-permute-start | bytes 25165832 | tf_op jit(solution)/shard_map/ppermute | solution.py:32
  229.3 117.4 %copy-start.1 = (f32[256,2]{0,1:T(2,128)S(1)}, f32[256,2]{0,1:T(2,128)}, u32[]{:S(2)}) copy-start(f32[256,2]{0,1:T(2,128)} %param.10) | copy-start | bytes 6148
  229.3 134.0 %copy-start = (bf16[256,256]{1,0:T(8,128)(2,1)S(1)}, bf16[256,256]{1,0:T(8,128)(2,1)}, u32[]{:S(2)}) copy-start(bf16[256,256]{1,0:T(8,128)(2,1)} %param.7) | copy-start | bytes 393220
  342.1 18.6 %all-to-all-start.1 = ((f32[8,128,256]{2,1,0:T(8,128)}), f32[8,128,256]{2,1,0:T(8,128)S(1)}, u32[]{:S(2)}, u32[]{:S(2)}) async-start(f32[8,128,256]{2,1,0:T(8,128)} %bitcast.65), calls=%async_computation.2 | async-start | bytes 2097152 | tf_op jit(solution)/shard_map/all_to_all | solution.py:72
Sparse Core Ops, SparseCore 0:
  65.6 66.8 all-gather.1
  229.5 112.5 reduce-scatter.1

commit v2 on v1

v2 whole, which is shorter than its diff:
```python
import functools

import jax
import jax.numpy as jnp
from jax import lax
from jax.experimental import pallas as pl
from jax.experimental.pallas import tpu as pltpu
from jax.sharding import Mesh
from jax.sharding import PartitionSpec as P

EXPERTS = 8
CAP = 128
COL = ("chip", "core")
MESH = pl.DeviceIdType.MESH


def normalize(rows, norm_gain):
    values = rows.astype(jnp.float32)
    inverse_norm = lax.rsqrt(jnp.mean(values * values, axis=-1, keepdims=True) + 1e-05)
    return (values * inverse_norm * norm_gain).astype(jnp.bfloat16)


def route_tables(expert_ids, expert_count, capacity):
    token_count = expert_ids.shape[0]
    flat_ids = expert_ids.reshape(-1)
    expert_range = jnp.arange(expert_count, dtype=jnp.int32)
    expert_hits = (flat_ids[:, None] == expert_range[None, :]).astype(jnp.int32)
    earlier = jnp.cumsum(expert_hits, axis=0) - expert_hits
    ranks = jnp.sum(earlier * expert_hits, axis=1)
    slot_index = (flat_ids * capacity + ranks).reshape(token_count, -1)
    slot_ids = jnp.arange(expert_count * capacity, dtype=jnp.int32)
    matches = (slot_index[:, :, None] == slot_ids[None, None, :]).astype(jnp.float32)
    picker = jnp.sum(matches, axis=1)
    return (picker.astype(jnp.bfloat16), slot_index)


def combine_rows(slot_rows, slot_index, gate_weights):
    picked = slot_rows[slot_index]
    return jnp.sum(picked * gate_weights[:, :, None], axis=1)


def entry_barrier(chips, row, me, core):
    barrier = pltpu.get_barrier_semaphore()
    for d in range(1, chips):
        peer = lax.rem(me + d, chips)
        pl.semaphore_signal(barrier, inc=1, device_id=(row, peer, core), device_id_type=MESH)
    pl.semaphore_signal(barrier, inc=1, device_id=(row, me, 1 - core), device_id_type=MESH)
    pl.semaphore_wait(barrier, chips)


def gather_kernel(chips, width, src, out, send_sem, recv_sem, fwd_send, fwd_recv, local_sem):
    row, me, core = lax.axis_index("row"), lax.axis_index("chip"), lax.axis_index("core")
    entry_barrier(chips, row, me, core)

    def window(chip, half):
        start = pl.multiple_of((chip * 2 + half) * width, width)
        return out.at[:, pl.ds(start, width)]

    local = pltpu.make_async_copy(src, window(me, core), local_sem)
    local.start()
    copies = []
    for d in range(1, chips):
        peer = lax.rem(me + d, chips)
        copy = pltpu.make_async_remote_copy(
            src_ref=src, dst_ref=window(me, core), send_sem=send_sem.at[d],
            recv_sem=recv_sem.at[d], device_id=(row, peer, core), device_id_type=MESH,
        )
        copy.start()
        copies.append(copy)
    forwards = []
    for d in range(chips):
        source = lax.rem(me - d + chips, chips)
        if d == 0:
            local.wait()
        else:
            copies[d - 1].wait_recv()
        fwd = pltpu.make_async_remote_copy(
            src_ref=window(source, core), dst_ref=window(source, core), send_sem=fwd_send.at[d],
            recv_sem=fwd_recv.at[d], device_id=(row, me, 1 - core), device_id_type=MESH,
        )
        fwd.start()
        forwards.append(fwd)
    for copy in copies:
        copy.wait_send()
    for fwd in forwards:
        fwd.wait()


def gather_cols(block, chips):
    slots, width = block.shape
    return pl.pallas_call(
        functools.partial(gather_kernel, chips, width),
        out_shape=jax.ShapeDtypeStruct((slots, chips * 2 * width), block.dtype),
        in_specs=[pl.BlockSpec(memory_space=pl.ANY)],
        out_specs=pl.BlockSpec(memory_space=pl.ANY),
        scratch_shapes=[
            pltpu.SemaphoreType.DMA((chips,)),
            pltpu.SemaphoreType.DMA((chips,)),
            pltpu.SemaphoreType.DMA((chips,)),
            pltpu.SemaphoreType.DMA((chips,)),
            pltpu.SemaphoreType.DMA(()),
        ],
        compiler_params=pltpu.CompilerParams(collective_id=0, has_side_effects=True),
    )(block)


def scatter_kernel(chips, src, out, send_sem, recv_sem, local_sem):
    row, me, core = lax.axis_index("row"), lax.axis_index("chip"), lax.axis_index("core")
    barrier = pltpu.get_barrier_semaphore()
    for d in range(1, chips):
        peer = lax.rem(me + d, chips)
        pl.semaphore_signal(barrier, inc=1, device_id=(row, peer, core), device_id_type=MESH)
    pl.semaphore_wait(barrier, chips - 1)
    local = pltpu.make_async_copy(src.at[me], out.at[me], local_sem)
    local.start()
    copies = []
    for d in range(1, chips):
        peer = lax.rem(me + d, chips)
        copy = pltpu.make_async_remote_copy(
            src_ref=src.at[peer], dst_ref=out.at[me], send_sem=send_sem.at[d],
            recv_sem=recv_sem.at[d], device_id=(row, peer, core), device_id_type=MESH,
        )
        copy.start()
        copies.append(copy)
    for copy in copies:
        copy.wait()
    local.wait()


def scatter_chips(parts):
    chips = parts.shape[0]
    return pl.pallas_call(
        functools.partial(scatter_kernel, chips),
        out_shape=jax.ShapeDtypeStruct(parts.shape, parts.dtype),
        in_specs=[pl.BlockSpec(memory_space=pl.ANY)],
        out_specs=pl.BlockSpec(memory_space=pl.ANY),
        scratch_shapes=[
            pltpu.SemaphoreType.DMA((chips,)),
            pltpu.SemaphoreType.DMA((chips,)),
            pltpu.SemaphoreType.DMA(()),
        ],
        compiler_params=pltpu.CompilerParams(collective_id=1, has_side_effects=True),
    )(parts)


def body(tokens, norm_gain, expert_ids, gate_weights, w_gate, w_up, w_down):
    chips = lax.psum(1, "chip")
    width = tokens.shape[1]
    core = lax.axis_index("core")

    picker, slot_index = route_tables(expert_ids, EXPERTS, CAP)
    packed = jnp.einsum("ts,td->sd", picker, tokens, preferred_element_type=jnp.float32).astype(
        jnp.bfloat16
    )
    packed = packed.reshape(EXPERTS, CAP, width)
    arrived = lax.all_to_all(packed, "row", split_axis=0, concat_axis=0, tiled=True)
    arrived = arrived.reshape(EXPERTS * CAP, width)
    slots = arrived.shape[0]

    widened = gather_cols(arrived, chips)
    normed = normalize(widened, norm_gain)
    gate_part = jnp.dot(normed, w_gate[0], preferred_element_type=jnp.float32)
    up_part = jnp.dot(normed, w_up[0], preferred_element_type=jnp.float32)
    hidden = (jax.nn.silu(gate_part) * up_part).astype(jnp.bfloat16)
    down = w_down[0].reshape(w_down.shape[1], chips, 2, width)
    split = jnp.einsum("sf,fkjw->jksw", hidden, down, preferred_element_type=jnp.float32)

    keep = lax.dynamic_index_in_dim(split, core, 0, keepdims=False)
    give = lax.dynamic_index_in_dim(split, 1 - core, 0, keepdims=False)
    summed = keep + lax.ppermute(give, "core", perm=[(0, 1), (1, 0)])
    arrived_parts = scatter_chips(summed.astype(jnp.bfloat16))
    shares = jnp.sum(arrived_parts.astype(jnp.float32), axis=0)
    shares = shares.reshape(EXPERTS, CAP, width)
    returned = lax.all_to_all(shares, "row", split_axis=0, concat_axis=0, tiled=True)
    mixed = combine_rows(returned.reshape(-1, width), slot_index, gate_weights)
    return (tokens.astype(jnp.float32) + mixed).astype(jnp.bfloat16)


def solution(mesh):
    rows, cols = mesh.devices.shape
    split_mesh = Mesh(mesh.devices.reshape(rows, cols // 2, 2), ("row", "chip", "core"))
    placed = (
        P("row", COL),
        P(),
        P("row", None),
        P("row", None),
        P("row", None, COL),
        P("row", None, COL),
        P("row", COL, None),
    )
    return jax.shard_map(
        body, mesh=split_mesh, in_specs=placed, out_specs=P("row", COL), check_vma=False
    )
```

time: 372 us -> 267 us (0.72)
  the two profiles are of different devices: /device:TPU:0 before, /device:TPU:24 now
where the time goes in v2:
time: 267 us; the launch traced here: 266 us
  Pallas kernels  141 us (53%)
  matrix products  38.8 us (15%)
  waiting for transfers between devices  26.9 us (10%)
  local copies, waits for them, and re-layouts  26.2 us (10%)
  other arithmetic  21.5 us (8%)
  starting transfers between devices  11.8 us (4%)
    pallas_call x1, Pallas kernels, scatter_chips(): pl.pallas_call(functools.partial(scatter_kernel, chips), out_shape=jax.Sh...  71.4 us
    pallas_call x1, Pallas kernels, gather_cols(): pl.pallas_call(functools.partial(gather_kernel, chips, width), out_shape=...  69.6 us
    dot_general x1, matrix products, body(): up_part = jnp.dot(normed, w_up[0], preferred_element_type=jnp.float32)  15.9 us
    all_to_all x1, waiting for transfers between devices, body(): lax.all_to_all(shares, 'row', split_axis=0, concat_axis=0, tiled=True)  13.8 us
    ppermute x1, waiting for transfers between devices, body(): summed = keep + lax.ppermute(give, 'core', perm=[(0, 1), (1, 0)])  13.1 us
    another operation x1, local copies, waits for them, and re-layouts, body(): down = w_down[0].reshape(w_down.shape[1], chips, 2, width)  12.8 us
    dot_general x1, matrix products, body(): jnp.einsum('sf,fkjw->jksw', hidden, down, preferred_element_type=jnp.floa...  11.6 us
    dot_general x1, matrix products, body(): gate_part = jnp.dot(normed, w_gate[0], preferred_element_type=jnp.float32)  9.24 us
  transfers between devices with their start and end apart: 3, of which 2 were waited for; matrix products, arithmetic and copies ran while one was open for 5% of the time, Pallas kernels for 0%

profile of v2, /device:TPU:24, one launch (start us, length us, event | category | flops | bytes accessed | tf_op | source)
XLA Modules:
  0.0 266.4 jit_solution(7899378033153083874)
XLA Ops:
  0.0 0.8 copy.30
  0.8 0.1 eq.42
  1.0 0.1 eq.38
  1.1 1.1 reduce-window.6
  2.3 0.2 slice_reduce_fusion
  2.5 0.1 fusion.17
  2.6 0.1 reduce_sum.48
  2.8 0.1 copy.32
  2.8 0.7 compare_select_fusion
  3.5 0.3 convert_reduce_fusion.1
  3.8 2.0 convolution_convert_fusion
  5.9 6.2 %all-to-all-start = ((bf16[8,128,256]{2,1,0:T(8,128)(2,1)}), bf16[8,128,256]{2,1,0:T(8,128)(2,1)S(1)}, u32[]{:S(2)}, u32[]{:S(2)}) async-start(bf16[8,128,256]{2,1,0:T(8,128)(2,1)} %bitcast.2), calls=%async_computation | async-start | bytes 1048576 | tf_op jit(solution)/shard_map/all_to_all | solution.py:156
  12.1 12.8 %reshape_squeeze.3 = bf16[896,8,2,256]{3,2,1,0:T(2,128)(2,1)} reshape(bf16[1,896,4096]{2,1,0:T(8,128)(2,1)} %param.13) | data formatting | bytes 14680064 | tf_op jit(solution)/shard_map/reshape;squeeze | solution.py:165
  24.9 0.0 all-to-all-done
  24.9 0.0 copy-start.2
  24.9 0.8 copy-done.2
  25.7 69.6 %shard_map.73 = bf16[1024,4096]{1,0:T(8,128)(2,1)} custom-call(bf16[1024,256]{1,0:T(8,128)(2,1)} %bitcast.36), custom_call_target="tpu_custom_call" | custom-call | tf_op jit(solution)/shard_map/pallas_call | solution.py:91
  95.4 0.0 copy-start
  95.4 0.0 slice-start
  95.4 5.2 %fusion = f32[1024]{0:T(1024)S(1)} fusion(bf16[1024,4096]{1,0:T(8,128)(2,1)} %shard_map.73), kind=kLoop, calls=%fused_computation.3 | loop fusion | flops 12581888 | bytes 8392704 | tf_op jit(solution)/shard_map/reduce_sum | solution.py:19
  100.6 0.0 copy-done.5
  100.7 0.5 copy-done
  101.2 0.0 slice-start.1
  101.2 15.9 %fusion.6 = f32[1024,896]{1,0:T(8,128)S(1)} fusion(bf16[1,4096,896]{2,1,0:T(8,128)(2,1)} %param.12, bf16[1024,4096]{1,0:T(8,128)(2,1)S(1)} %copy-done, f32[4096]{0:T(1024)S(1)} %copy-done.5, f32[1024]{0:T(1024)S(1)} %add_rsqrt_fusion), kind=kOutput, calls=%fused_computation.12 | convolution fusion | flops 7532969984 | bytes 19419136 | tf_op jit(solution)/shard_map/dot_general | solution.py:163
  117.1 0.0 slice-done
  117.1 0.0 slice-done.1
  117.1 9.2 %multiply_convert_fusion = bf16[1024,896]{1,0:T(8,128)(2,1)S(1)} fusion(f32[1024,896]{1,0:T(8,128)S(1)} %fusion.6, bf16[1,4096,896]{2,1,0:T(8,128)(2,1)S(1)} %bitcast.38, bf16[1024,4096]{1,0:T(8,128)(2,1)S(1)} %copy-done, f32[4096]{0:T(1024)S(1)} %copy-done.5, f32[1024]{0:T(1024)S(1)} %add_rsqrt_fusion), kind=kOutput, calls=%fused_computation.16 | convolution fusion | flops 7538475008 | bytes 21254144 | tf_op jit(solution)/shard_map/dot_general | solution.py:162
  126.3 11.6 %fusion.4 = f32[1024,8,2,256]{3,0,1,2:T(8,128)S(1)} fusion(bf16[896,8,2,256]{3,2,1,0:T(2,128)(2,1)} %reshape_squeeze.3, bf16[1024,896]{1,0:T(8,128)(2,1)S(1)} %multiply_convert_fusion), kind=kOutput, calls=%fused_computation.10 | convolution fusion | flops 7516192768 | bytes 25952256 | tf_op jit(solution)/shard_map/sf,fkjw->jksw/dot_general | solution.py:166
  137.9 0.0 copy-start.1
  137.9 4.1 %dynamic-slice_bitcast_fusion = f32[8,1024,256]{2,1,0:T(8,128)} fusion(f32[1024,8,2,256]{3,0,1,2:T(8,128)S(1)} %fusion.4, s32[]{:T(128)S(6)} %select_n.11), kind=kLoop, calls=%fused_computation.9 | loop fusion | bytes 16777220 | tf_op jit(solution)/shard_map/jit(dynamic_index_in_dim)/squeeze | solution.py:169
  142.0 4.1 %copy-done.1 = f32[1024,8,2,256]{3,0,1,2:T(8,128)} copy-done((f32[1024,8,2,256]{3,0,1,2:T(8,128)}, f32[1024,8,2,256]{3,0,1,2:T(8,128)S(1)}, u32[]{:S(2)}) %copy-start.1) | copy-done | bytes 16777240
  146.1 0.4 collective-permute-start
  146.5 13.1 %collective-permute-done = f32[8,1024,256]{2,1,0:T(8,128)} collective-permute-done((f32[8,1024,256]{2,1,0:T(8,128)}, f32[8,1024,256]{2,1,0:T(8,128)}, u32[]{:S(2)}, u32[]{:S(2)}) %collective-permute-start) | collective-permute-done | bytes 8388640 | tf_op jit(solution)/shard_map/ppermute | solution.py:170
  159.6 8.8 %fusion.3.src = bf16[8,1024,256]{2,1,0:T(8,128)(2,1)} fusion(f32[8,1024,256]{2,1,0:T(8,128)} %collective-permute-done, f32[1024,8,2,256]{3,0,1,2:T(8,128)} %copy-done.1, s32[]{:T(128)S(6)} %select_n.10), kind=kLoop, calls=%fused_computation.7 | loop fusion | flops 4194304 | bytes 20971524 | tf_op jit(solution)/shard_map/convert_element_type | solution.py:171
  168.4 71.4 %shard_map.74 = bf16[8,1024,256]{2,1,0:T(8,128)(2,1)} custom-call(bf16[8,1024,256]{2,1,0:T(8,128)(2,1)} %fusion.3.src), custom_call_target="tpu_custom_call" | custom-call | tf_op jit(solution)/shard_map/pallas_call | solution.py:132
  239.9 0.0 copy-start.3
  239.9 3.8 %convert_reduce_fusion = f32[1024,256]{1,0:T(8,128)} fusion(bf16[8,1024,256]{2,1,0:T(8,128)(2,1)} %shard_map.74), kind=kLoop, calls=%fused_computation.8 | loop fusion | flops 3932160 | bytes 5242880 | tf_op jit(solution)/shard_map/reduce_sum | solution.py:172
  243.7 5.1 %all-to-all-start.1 = ((f32[8,128,256]{2,1,0:T(8,128)}), f32[8,128,256]{2,1,0:T(8,128)S(1)}, u32[]{:S(2)}, u32[]{:S(2)}) async-start(f32[8,128,256]{2,1,0:T(8,128)} %bitcast.11), calls=%async_computation.1 | async-start | bytes 2097152 | tf_op jit(solution)/shard_map/all_to_all | solution.py:174
  248.9 0.1 copy.36
  249.0 0.1 reshape.55
  249.2 0.0 copy-done.4
  249.2 0.1 copy.37
  249.3 13.8 %all-to-all-done.1 = f32[8,128,256]{2,1,0:T(8,128)S(1)} async-done(((f32[8,128,256]{2,1,0:T(8,128)}), f32[8,128,256]{2,1,0:T(8,128)S(1)}, u32[]{:S(2)}, u32[]{:S(2)}) %all-to-all-start.1) | async-done | bytes 1048608 | tf_op jit(solution)/shard_map/all_to_all | solution.py:174
  263.1 1.6 gather_fusion
  264.7 0.3 reshape.54
  265.0 0.7 multiply_reduce_fusion
  265.7 0.0 copy-done.3
  265.7 0.7 add_convert_fusion
  (8 shorter events, 0.1 us)
Async XLA Ops:
  5.9 19.1 %all-to-all-start = ((bf16[8,128,256]{2,1,0:T(8,128)(2,1)}), bf16[8,128,256]{2,1,0:T(8,128)(2,1)S(1)}, u32[]{:S(2)}, u32[]{:S(2)}) async-start(bf16[8,128,256]{2,1,0:T(8,128)(2,1)} %bitcast.2), calls=%async_computation | async-start | bytes 1048576 | tf_op jit(solution)/shard_map/all_to_all | solution.py:156
  24.9 0.8 copy-start.2
  25.7 74.9 %copy-start.5 = (f32[4096]{0:T(1024)S(1)}, f32[4096]{0:T(1024)}, u32[]{:S(2)}) copy-start(f32[4096]{0:T(1024)} %param.8) | copy-start | bytes 49156
  95.4 5.8 %copy-start = (bf16[1024,4096]{1,0:T(8,128)(2,1)S(1)}, bf16[1024,4096]{1,0:T(8,128)(2,1)}, u32[]{:S(2)}) copy-start(bf16[1024,4096]{1,0:T(8,128)(2,1)} %shard_map.73) | copy-start | bytes 25165828
  95.4 21.7 %slice-start = ((s8[7340032]{0:T(1024)(128)(4,1)}), s8[3145728]{0:T(1024)(128)(4,1)S(1)}, s32[]{:S(2)}) async-start(s8[7340032]{0:T(1024)(128)(4,1)} %bitcast.37), calls=%async_computation.2 | async-start | bytes 6291456
  101.2 15.9 %slice-start.1 = ((s8[7340032]{0:T(1024)(128)(4,1)}), s8[4194304]{0:T(1024)(128)(4,1)S(1)}, s32[]{:S(2)}) async-start(s8[7340032]{0:T(1024)(128)(4,1)} %bitcast.37), calls=%async_computation.3 | async-start | bytes 8388608
  137.9 8.2 %copy-start.1 = (f32[1024,8,2,256]{3,0,1,2:T(8,128)}, f32[1024,8,2,256]{3,0,1,2:T(8,128)S(1)}, u32[]{:S(2)}) copy-start(f32[1024,8,2,256]{3,0,1,2:T(8,128)S(1)} %fusion.4) | copy-start | bytes 50331652
  146.1 13.5 %collective-permute-start = (f32[8,1024,256]{2,1,0:T(8,128)}, f32[8,1024,256]{2,1,0:T(8,128)}, u32[]{:S(2)}, u32[]{:S(2)}) collective-permute-start(f32[8,1024,256]{2,1,0:T(8,128)} %dynamic-slice_bitcast_fusion), channel_id=1, source_target_pairs={{0,1},{1,0},{2,3},{3,2},{4,5},{5,4},{6,7},{7,6},{8,9},{9,8},{10,11... | collective-permute-start | bytes 25165832 | tf_op jit(solution)/shard_map/ppermute | solution.py:170
  168.4 80.7 %copy-start.4 = (f32[256,2]{0,1:T(2,128)S(1)}, f32[256,2]{0,1:T(2,128)}, u32[]{:S(2)}) copy-start(f32[256,2]{0,1:T(2,128)} %param.10) | copy-start | bytes 6148
  239.9 25.8 %copy-start.3 = (bf16[256,256]{1,0:T(8,128)(2,1)S(1)}, bf16[256,256]{1,0:T(8,128)(2,1)}, u32[]{:S(2)}) copy-start(bf16[256,256]{1,0:T(8,128)(2,1)} %param.7) | copy-start | bytes 393220
  243.7 19.4 %all-to-all-start.1 = ((f32[8,128,256]{2,1,0:T(8,128)}), f32[8,128,256]{2,1,0:T(8,128)S(1)}, u32[]{:S(2)}, u32[]{:S(2)}) async-start(f32[8,128,256]{2,1,0:T(8,128)} %bitcast.11), calls=%async_computation.1 | async-start | bytes 2097152 | tf_op jit(solution)/shard_map/all_to_all | solution.py:174

commit v3 on v2

--- a/solution.py
+++ b/solution.py
@@ -39,65 +39,90 @@
     return jnp.sum(picked * gate_weights[:, :, None], axis=1)
 
 
-def entry_barrier(chips, row, me, core):
+def gather_kernel(width, src, out, send_sem, recv_sem, local_sem):
+    row, me, core = lax.axis_index("row"), lax.axis_index("chip"), lax.axis_index("core")
+    side, y = me // 4, me % 4
+    partner = lax.rem(me + 4, 8)
+    up = side * 4 + lax.rem(y + 1, 4)
+    down = side * 4 + lax.rem(y + 3, 4)
+    across = side * 4 + lax.rem(y + 2, 4)
+    sister = 1 - core
+
     barrier = pltpu.get_barrier_semaphore()
-    for d in range(1, chips):
-        peer = lax.rem(me + d, chips)
-        pl.semaphore_signal(barrier, inc=1, device_id=(row, peer, core), device_id_type=MESH)
-    pl.semaphore_signal(barrier, inc=1, device_id=(row, me, 1 - core), device_id_type=MESH)
-    pl.semaphore_wait(barrier, chips)
-
-
-def gather_kernel(chips, width, src, out, send_sem, recv_sem, fwd_send, fwd_recv, local_sem):
-    row, me, core = lax.axis_index("row"), lax.axis_index("chip"), lax.axis_index("core")
-    entry_barrier(chips, row, me, core)
-
-    def window(chip, half):
-        start = pl.multiple_of((chip * 2 + half) * width, width)
+    for chip, half in ((partner, core), (up, core), (down, core), (me, sister)):
+        pl.semaphore_signal(barrier, inc=1, device_id=(row, chip, half), device_id_type=MESH)
+    pl.semaphore_wait(barrier, 4)
+
+    def window(chip):
+        start = pl.multiple_of((chip * 2 + core) * width, width)
         return out.at[:, pl.ds(start, width)]
 
-    local = pltpu.make_async_copy(src, window(me, core), local_sem)
-    local.start()
-    copies = []
-    for d in range(1, chips):
-        peer = lax.rem(me + d, chips)
+    def send(tag, origin, chip, half, source=None):
         copy = pltpu.make_async_remote_copy(
-            src_ref=src, dst_ref=window(me, core), send_sem=send_sem.at[d],
-            recv_sem=recv_sem.at[d], device_id=(row, peer, core), device_id_type=MESH,
+            src_ref=window(origin) if source is None else source, dst_ref=window(origin),
+            send_sem=send_sem.at[tag], recv_sem=recv_sem.at[tag],
+            device_id=(row, chip, half), device_id_type=MESH,
         )
         copy.start()
-        copies.append(copy)
-    forwards = []
-    for d in range(chips):
-        source = lax.rem(me - d + chips, chips)
-        if d == 0:
-            local.wait()
-        else:
-            copies[d - 1].wait_recv()
-        fwd = pltpu.make_async_remote_copy(
-            src_ref=window(source, core), dst_ref=window(source, core), send_sem=fwd_send.at[d],
-            recv_sem=fwd_recv.at[d], device_id=(row, me, 1 - core), device_id_type=MESH,
-        )
-        fwd.start()
-        forwards.append(fwd)
-    for copy in copies:
+        return copy
+
+    sent = [
+        send(0, me, partner, core, src),
+        send(1, me, up, core, src),
+        send(2, me, down, core, src),
+        send(7, me, me, sister, src),
+    ]
+    local = pltpu.make_async_copy(src, window(me), local_sem)
+    local.start()
+
+    def arrive(tag, origin):
+        pltpu.make_async_remote_copy(
+            src_ref=window(origin), dst_ref=window(origin), send_sem=send_sem.at[tag],
+            recv_sem=recv_sem.at[tag], device_id=(row, me, sister), device_id_type=MESH,
+        ).wait_recv()
+
+    other = lax.rem(partner, 8)
+    arrive(0, other)
+    sent += [send(3, other, up, core), send(4, other, down, core), send(8, other, me, sister)]
+    arrive(1, down)
+    sent += [send(5, down, up, core), send(9, down, me, sister)]
+    arrive(2, up)
+    sent.append(send(10, up, me, sister))
+    arrive(3, lax.rem(down + 4, 8))
+    sent.append(send(11, lax.rem(down + 4, 8), me, sister))
+    arrive(4, lax.rem(up + 4, 8))
+    sent += [send(6, lax.rem(up + 4, 8), down, core), send(12, lax.rem(up + 4, 8), me, sister)]
+    arrive(5, across)
+    sent.append(send(13, across, me, sister))
+    arrive(6, lax.rem(across + 4, 8))
+    sent.append(send(14, lax.rem(across + 4, 8), me, sister))
+    local.wait()
+
+    def sister_window(origin):
+        start = pl.multiple_of((origin * 2 + sister) * width, width)
+        return out.at[:, pl.ds(start, width)]
+
+    for tag, origin in ((7, me), (8, partner), (9, down), (10, up), (11, lax.rem(down + 4, 8)),
+                        (12, lax.rem(up + 4, 8)), (13, across), (14, lax.rem(across + 4, 8))):
+        pltpu.make_async_remote_copy(
+            src_ref=sister_window(origin), dst_ref=sister_window(origin),
+            send_sem=send_sem.at[tag], recv_sem=recv_sem.at[tag],
+            device_id=(row, me, sister), device_id_type=MESH,
+        ).wait_recv()
+    for copy in sent:
         copy.wait_send()
-    for fwd in forwards:
-        fwd.wait()
 
 
 def gather_cols(block, chips):
     slots, width = block.shape
     return pl.pallas_call(
-        functools.partial(gather_kernel, chips, width),
+        functools.partial(gather_kernel, width),
         out_shape=jax.ShapeDtypeStruct((slots, chips * 2 * width), block.dtype),
         in_specs=[pl.BlockSpec(memory_space=pl.ANY)],
         out_specs=pl.BlockSpec(memory_space=pl.ANY),
         scratch_shapes=[
-            pltpu.SemaphoreType.DMA((chips,)),
-            pltpu.SemaphoreType.DMA((chips,)),
-            pltpu.SemaphoreType.DMA((chips,)),
-            pltpu.SemaphoreType.DMA((chips,)),
+            pltpu.SemaphoreType.DMA((15,)),
+            pltpu.SemaphoreType.DMA((15,)),
             pltpu.SemaphoreType.DMA(()),
         ],
         compiler_params=pltpu.CompilerParams(collective_id=0, has_side_effects=True),

time: 267 us -> 239 us (0.90)
  Pallas kernels: 141 us -> 114 us
    pallas_call x1, Pallas kernels: 69.6 us -> 43.5 us  [gather_cols(): pl.pallas_call(functools.partial(gather_kernel, width), out_shape=jax.Sha...]
  transfers between devices with their start and end apart: 3 -> 3, of which waited for: 2 -> 2; matrix products, arithmetic and copies ran while one was open for 5% -> 6% of each run, Pallas kernels for 0% -> 0%
where the time goes in v3:
time: 239 us
  Pallas kernels  114 us (48%)
  matrix products  38.8 us (16%)
  waiting for transfers between devices  26.7 us (11%)
  local copies, waits for them, and re-layouts  26.2 us (11%)
  other arithmetic  21.5 us (9%)
  starting transfers between devices  11.5 us (5%)
    pallas_call x1, Pallas kernels, scatter_chips(): pl.pallas_call(functools.partial(scatter_kernel, chips), out_shape=jax.Sh...  70.3 us
    pallas_call x1, Pallas kernels, gather_cols(): pl.pallas_call(functools.partial(gather_kernel, width), out_shape=jax.Sha...  43.5 us
    dot_general x1, matrix products, body(): up_part = jnp.dot(normed, w_up[0], preferred_element_type=jnp.float32)  15.9 us
    all_to_all x1, waiting for transfers between devices, body(): lax.all_to_all(shares, 'row', split_axis=0, concat_axis=0, tiled=True)  13.5 us
    ppermute x1, waiting for transfers between devices, body(): summed = keep + lax.ppermute(give, 'core', perm=[(0, 1), (1, 0)])  13.1 us
    another operation x1, local copies, waits for them, and re-layouts, body(): down = w_down[0].reshape(w_down.shape[1], chips, 2, width)  12.8 us
    dot_general x1, matrix products, body(): jnp.einsum('sf,fkjw->jksw', hidden, down, preferred_element_type=jnp.floa...  11.6 us
    dot_general x1, matrix products, body(): gate_part = jnp.dot(normed, w_gate[0], preferred_element_type=jnp.float32)  9.24 us
  transfers between devices with their start and end apart: 3, of which 2 were waited for; matrix products, arithmetic and copies ran while one was open for 6% of the time, Pallas kernels for 0%

profile of v3, /device:TPU:24, one launch (start us, length us, event | category | flops | bytes accessed | tf_op | source)
XLA Modules:
  0.0 238.5 jit_solution(9277113154420418896)
XLA Ops:
  0.0 0.8 copy.30
  0.8 0.1 eq.42
  1.0 0.1 eq.38
  1.1 1.1 reduce-window.6
  2.3 0.2 slice_reduce_fusion
  2.5 0.1 fusion.17
  2.6 0.1 reduce_sum.48
  2.8 0.1 copy.32
  2.8 0.7 compare_select_fusion
  3.5 0.3 convert_reduce_fusion.1
  3.8 2.0 convolution_convert_fusion
  5.9 6.2 %all-to-all-start = ((bf16[8,128,256]{2,1,0:T(8,128)(2,1)}), bf16[8,128,256]{2,1,0:T(8,128)(2,1)S(1)}, u32[]{:S(2)}, u32[]{:S(2)}) async-start(bf16[8,128,256]{2,1,0:T(8,128)(2,1)} %bitcast.2), calls=%async_computation | async-start | bytes 1048576 | tf_op jit(solution)/shard_map/all_to_all | solution.py:181
  12.1 12.8 %reshape_squeeze.3 = bf16[896,8,2,256]{3,2,1,0:T(2,128)(2,1)} reshape(bf16[1,896,4096]{2,1,0:T(8,128)(2,1)} %param.13) | data formatting | bytes 14680064 | tf_op jit(solution)/shard_map/reshape;squeeze | solution.py:190
  24.9 0.0 all-to-all-done
  24.9 0.0 copy-start.2
  24.9 0.8 copy-done.2
  25.7 43.5 %shard_map.73 = bf16[1024,4096]{1,0:T(8,128)(2,1)} custom-call(bf16[1024,256]{1,0:T(8,128)(2,1)} %bitcast.36), custom_call_target="tpu_custom_call" | custom-call | tf_op jit(solution)/shard_map/pallas_call | solution.py:118
  69.2 0.0 copy-start
  69.2 0.0 slice-start
  69.2 5.2 %fusion = f32[1024]{0:T(1024)S(1)} fusion(bf16[1024,4096]{1,0:T(8,128)(2,1)} %shard_map.73), kind=kLoop, calls=%fused_computation.3 | loop fusion | flops 12581888 | bytes 8392704 | tf_op jit(solution)/shard_map/reduce_sum | solution.py:19
  74.5 0.0 copy-done.5
  74.5 0.5 copy-done
  75.0 0.0 slice-start.1
  75.0 15.9 %fusion.6 = f32[1024,896]{1,0:T(8,128)S(1)} fusion(bf16[1,4096,896]{2,1,0:T(8,128)(2,1)} %param.12, bf16[1024,4096]{1,0:T(8,128)(2,1)S(1)} %copy-done, f32[4096]{0:T(1024)S(1)} %copy-done.5, f32[1024]{0:T(1024)S(1)} %add_rsqrt_fusion), kind=kOutput, calls=%fused_computation.12 | convolution fusion | flops 7532969984 | bytes 19419136 | tf_op jit(solution)/shard_map/dot_general | solution.py:188
  90.9 0.0 slice-done
  90.9 0.0 slice-done.1
  90.9 9.2 %multiply_convert_fusion = bf16[1024,896]{1,0:T(8,128)(2,1)S(1)} fusion(f32[1024,896]{1,0:T(8,128)S(1)} %fusion.6, bf16[1,4096,896]{2,1,0:T(8,128)(2,1)S(1)} %bitcast.38, bf16[1024,4096]{1,0:T(8,128)(2,1)S(1)} %copy-done, f32[4096]{0:T(1024)S(1)} %copy-done.5, f32[1024]{0:T(1024)S(1)} %add_rsqrt_fusion), kind=kOutput, calls=%fused_computation.16 | convolution fusion | flops 7538475008 | bytes 21254144 | tf_op jit(solution)/shard_map/dot_general | solution.py:187
  100.2 11.6 %fusion.4 = f32[1024,8,2,256]{3,0,1,2:T(8,128)S(1)} fusion(bf16[896,8,2,256]{3,2,1,0:T(2,128)(2,1)} %reshape_squeeze.3, bf16[1024,896]{1,0:T(8,128)(2,1)S(1)} %multiply_convert_fusion), kind=kOutput, calls=%fused_computation.10 | convolution fusion | flops 7516192768 | bytes 25952256 | tf_op jit(solution)/shard_map/sf,fkjw->jksw/dot_general | solution.py:191
  111.7 0.0 copy-start.1
  111.7 4.1 %dynamic-slice_bitcast_fusion = f32[8,1024,256]{2,1,0:T(8,128)} fusion(f32[1024,8,2,256]{3,0,1,2:T(8,128)S(1)} %fusion.4, s32[]{:T(128)S(6)} %select_n.11), kind=kLoop, calls=%fused_computation.9 | loop fusion | bytes 16777220 | tf_op jit(solution)/shard_map/jit(dynamic_index_in_dim)/squeeze | solution.py:194
  115.9 4.1 %copy-done.1 = f32[1024,8,2,256]{3,0,1,2:T(8,128)} copy-done((f32[1024,8,2,256]{3,0,1,2:T(8,128)}, f32[1024,8,2,256]{3,0,1,2:T(8,128)S(1)}, u32[]{:S(2)}) %copy-start.1) | copy-done | bytes 16777240
  120.0 0.4 collective-permute-start
  120.4 13.1 %collective-permute-done = f32[8,1024,256]{2,1,0:T(8,128)} collective-permute-done((f32[8,1024,256]{2,1,0:T(8,128)}, f32[8,1024,256]{2,1,0:T(8,128)}, u32[]{:S(2)}, u32[]{:S(2)}) %collective-permute-start) | collective-permute-done | bytes 8388640 | tf_op jit(solution)/shard_map/ppermute | solution.py:195
  133.5 8.8 %fusion.3.src = bf16[8,1024,256]{2,1,0:T(8,128)(2,1)} fusion(f32[8,1024,256]{2,1,0:T(8,128)} %collective-permute-done, f32[1024,8,2,256]{3,0,1,2:T(8,128)} %copy-done.1, s32[]{:T(128)S(6)} %select_n.10), kind=kLoop, calls=%fused_computation.7 | loop fusion | flops 4194304 | bytes 20971524 | tf_op jit(solution)/shard_map/convert_element_type | solution.py:196
  142.3 70.3 %shard_map.74 = bf16[8,1024,256]{2,1,0:T(8,128)(2,1)} custom-call(bf16[8,1024,256]{2,1,0:T(8,128)(2,1)} %fusion.3.src), custom_call_target="tpu_custom_call" | custom-call | tf_op jit(solution)/shard_map/pallas_call | solution.py:157
  212.6 0.0 copy-start.3
  212.6 3.8 %convert_reduce_fusion = f32[1024,256]{1,0:T(8,128)} fusion(bf16[8,1024,256]{2,1,0:T(8,128)(2,1)} %shard_map.74), kind=kLoop, calls=%fused_computation.8 | loop fusion | flops 3932160 | bytes 5242880 | tf_op jit(solution)/shard_map/reduce_sum | solution.py:197
  216.4 4.8 %all-to-all-start.1 = ((f32[8,128,256]{2,1,0:T(8,128)}), f32[8,128,256]{2,1,0:T(8,128)S(1)}, u32[]{:S(2)}, u32[]{:S(2)}) async-start(f32[8,128,256]{2,1,0:T(8,128)} %bitcast.11), calls=%async_computation.1 | async-start | bytes 2097152 | tf_op jit(solution)/shard_map/all_to_all | solution.py:199
  221.2 0.1 copy.36
  221.4 0.1 reshape.55
  221.5 0.0 copy-done.4
  221.5 0.1 copy.37
  221.7 13.5 %all-to-all-done.1 = f32[8,128,256]{2,1,0:T(8,128)S(1)} async-done(((f32[8,128,256]{2,1,0:T(8,128)}), f32[8,128,256]{2,1,0:T(8,128)S(1)}, u32[]{:S(2)}, u32[]{:S(2)}) %all-to-all-start.1) | async-done | bytes 1048608 | tf_op jit(solution)/shard_map/all_to_all | solution.py:199
  235.2 1.6 gather_fusion
  236.8 0.3 reshape.54
  237.1 0.7 multiply_reduce_fusion
  237.8 0.0 copy-done.3
  237.8 0.7 add_convert_fusion
  (8 shorter events, 0.1 us)
Async XLA Ops:
  5.9 19.1 %all-to-all-start = ((bf16[8,128,256]{2,1,0:T(8,128)(2,1)}), bf16[8,128,256]{2,1,0:T(8,128)(2,1)S(1)}, u32[]{:S(2)}, u32[]{:S(2)}) async-start(bf16[8,128,256]{2,1,0:T(8,128)(2,1)} %bitcast.2), calls=%async_computation | async-start | bytes 1048576 | tf_op jit(solution)/shard_map/all_to_all | solution.py:181
  24.9 0.8 copy-start.2
  25.7 48.7 %copy-start.5 = (f32[4096]{0:T(1024)S(1)}, f32[4096]{0:T(1024)}, u32[]{:S(2)}) copy-start(f32[4096]{0:T(1024)} %param.8) | copy-start | bytes 49156
  69.2 5.8 %copy-start = (bf16[1024,4096]{1,0:T(8,128)(2,1)S(1)}, bf16[1024,4096]{1,0:T(8,128)(2,1)}, u32[]{:S(2)}) copy-start(bf16[1024,4096]{1,0:T(8,128)(2,1)} %shard_map.73) | copy-start | bytes 25165828
  69.2 21.7 %slice-start = ((s8[7340032]{0:T(1024)(128)(4,1)}), s8[3145728]{0:T(1024)(128)(4,1)S(1)}, s32[]{:S(2)}) async-start(s8[7340032]{0:T(1024)(128)(4,1)} %bitcast.37), calls=%async_computation.2 | async-start | bytes 6291456
  75.0 15.9 %slice-start.1 = ((s8[7340032]{0:T(1024)(128)(4,1)}), s8[4194304]{0:T(1024)(128)(4,1)S(1)}, s32[]{:S(2)}) async-start(s8[7340032]{0:T(1024)(128)(4,1)} %bitcast.37), calls=%async_computation.3 | async-start | bytes 8388608
  111.7 8.2 %copy-start.1 = (f32[1024,8,2,256]{3,0,1,2:T(8,128)}, f32[1024,8,2,256]{3,0,1,2:T(8,128)S(1)}, u32[]{:S(2)}) copy-start(f32[1024,8,2,256]{3,0,1,2:T(8,128)S(1)} %fusion.4) | copy-start | bytes 50331652
  120.0 13.5 %collective-permute-start = (f32[8,1024,256]{2,1,0:T(8,128)}, f32[8,1024,256]{2,1,0:T(8,128)}, u32[]{:S(2)}, u32[]{:S(2)}) collective-permute-start(f32[8,1024,256]{2,1,0:T(8,128)} %dynamic-slice_bitcast_fusion), channel_id=1, source_target_pairs={{0,1},{1,0},{2,3},{3,2},{4,5},{5,4},{6,7},{7,6},{8,9},{9,8},{10,11... | collective-permute-start | bytes 25165832 | tf_op jit(solution)/shard_map/ppermute | solution.py:195
  142.3 79.2 %copy-start.4 = (f32[256,2]{0,1:T(2,128)S(1)}, f32[256,2]{0,1:T(2,128)}, u32[]{:S(2)}) copy-start(f32[256,2]{0,1:T(2,128)} %param.10) | copy-start | bytes 6148
  212.6 25.2 %copy-start.3 = (bf16[256,256]{1,0:T(8,128)(2,1)S(1)}, bf16[256,256]{1,0:T(8,128)(2,1)}, u32[]{:S(2)}) copy-start(bf16[256,256]{1,0:T(8,128)(2,1)} %param.7) | copy-start | bytes 393220
  216.4 18.8 %all-to-all-start.1 = ((f32[8,128,256]{2,1,0:T(8,128)}), f32[8,128,256]{2,1,0:T(8,128)S(1)}, u32[]{:S(2)}, u32[]{:S(2)}) async-start(f32[8,128,256]{2,1,0:T(8,128)} %bitcast.11), calls=%async_computation.1 | async-start | bytes 2097152 | tf_op jit(solution)/shard_map/all_to_all | solution.py:199

commit v4 on v3

--- a/solution.py
+++ b/solution.py
@@ -129,42 +129,91 @@
     )(block)
 
 
-def scatter_kernel(chips, src, out, send_sem, recv_sem, local_sem):
+def add_blocks(dst, *sources):
+    rows = dst.shape[0]
+    step = 128
+
+    def one(i, carry):
+        part = pl.ds(pl.multiple_of(i * step, step), step)
+        total = sources[0][part, :].astype(jnp.float32)
+        for source in sources[1:]:
+            total = total + source[part, :].astype(jnp.float32)
+        dst[part, :] = total.astype(dst.dtype)
+        return carry
+
+    lax.fori_loop(0, rows // step, one, 0)
+
+
+def scatter_kernel(parts, out, sending, landed, send_sem, recv_sem):
     row, me, core = lax.axis_index("row"), lax.axis_index("chip"), lax.axis_index("core")
+    side, y = me // 4, me % 4
+    partner = lax.rem(me + 4, 8)
+    up = side * 4 + lax.rem(y + 1, 4)
+    down = side * 4 + lax.rem(y + 3, 4)
+    across = side * 4 + lax.rem(y + 2, 4)
+
+    def far(chip):
+        return lax.rem(chip + 4, 8)
+
     barrier = pltpu.get_barrier_semaphore()
-    for d in range(1, chips):
-        peer = lax.rem(me + d, chips)
-        pl.semaphore_signal(barrier, inc=1, device_id=(row, peer, core), device_id_type=MESH)
-    pl.semaphore_wait(barrier, chips - 1)
-    local = pltpu.make_async_copy(src.at[me], out.at[me], local_sem)
-    local.start()
-    copies = []
-    for d in range(1, chips):
-        peer = lax.rem(me + d, chips)
+    for chip in (partner, up, down):
+        pl.semaphore_signal(barrier, inc=1, device_id=(row, chip, core), device_id_type=MESH)
+    pl.semaphore_wait(barrier, 3)
+
+    def send(tag, chip):
         copy = pltpu.make_async_remote_copy(
-            src_ref=src.at[peer], dst_ref=out.at[me], send_sem=send_sem.at[d],
-            recv_sem=recv_sem.at[d], device_id=(row, peer, core), device_id_type=MESH,
+            src_ref=sending.at[tag], dst_ref=landed.at[tag], send_sem=send_sem.at[tag],
+            recv_sem=recv_sem.at[tag], device_id=(row, chip, core), device_id_type=MESH,
         )
         copy.start()
-        copies.append(copy)
-    for copy in copies:
-        copy.wait()
-    local.wait()
+        return copy
+
+    def arrive(tag):
+        pltpu.make_async_remote_copy(
+            src_ref=sending.at[tag], dst_ref=landed.at[tag], send_sem=send_sem.at[tag],
+            recv_sem=recv_sem.at[tag], device_id=(row, me, core), device_id_type=MESH,
+        ).wait_recv()
+
+    sent = []
+    for tag, chip, target in ((0, down, far(down)), (1, down, across), (2, up, up),
+                              (3, up, far(across))):
+        add_blocks(sending.at[tag], parts.at[target])
+        sent.append(send(tag, chip))
+    arrive(1)
+    add_blocks(sending.at[4], parts.at[down], landed.at[1])
+    sent.append(send(4, down))
+    arrive(3)
+    add_blocks(sending.at[5], parts.at[far(up)], landed.at[3])
+    sent.append(send(5, up))
+    arrive(0)
+    arrive(5)
+    add_blocks(sending.at[6], parts.at[partner], landed.at[0], landed.at[5])
+    sent.append(send(6, partner))
+    arrive(2)
+    arrive(4)
+    add_blocks(out, parts.at[me], landed.at[2], landed.at[4])
+    arrive(6)
+    add_blocks(out, out, landed.at[6])
+    for copy in sent:
+        copy.wait_send()
 
 
 def scatter_chips(parts):
-    chips = parts.shape[0]
+    chips, slots, width = parts.shape
     return pl.pallas_call(
-        functools.partial(scatter_kernel, chips),
-        out_shape=jax.ShapeDtypeStruct(parts.shape, parts.dtype),
-        in_specs=[pl.BlockSpec(memory_space=pl.ANY)],
-        out_specs=pl.BlockSpec(memory_space=pl.ANY),
+        scatter_kernel,
+        out_shape=jax.ShapeDtypeStruct((slots, width), jnp.float32),
+        in_specs=[pl.BlockSpec(memory_space=pltpu.VMEM)],
+        out_specs=pl.BlockSpec(memory_space=pltpu.VMEM),
         scratch_shapes=[
-            pltpu.SemaphoreType.DMA((chips,)),
-            pltpu.SemaphoreType.DMA((chips,)),
-            pltpu.SemaphoreType.DMA(()),
+            pltpu.VMEM((7, slots, width), jnp.bfloat16),
+            pltpu.VMEM((7, slots, width), jnp.bfloat16),
+            pltpu.SemaphoreType.DMA((7,)),
+            pltpu.SemaphoreType.DMA((7,)),
         ],
-        compiler_params=pltpu.CompilerParams(collective_id=1, has_side_effects=True),
+        compiler_params=pltpu.CompilerParams(
+            collective_id=1, has_side_effects=True, vmem_limit_bytes=48 * 1024 * 1024
+        ),
     )(parts)
 
 
@@ -193,8 +242,7 @@
     keep = lax.dynamic_index_in_dim(split, core, 0, keepdims=False)
     give = lax.dynamic_index_in_dim(split, 1 - core, 0, keepdims=False)
     summed = keep + lax.ppermute(give, "core", perm=[(0, 1), (1, 0)])
-    arrived_parts = scatter_chips(summed.astype(jnp.bfloat16))
-    shares = jnp.sum(arrived_parts.astype(jnp.float32), axis=0)
+    shares = scatter_chips(summed)
     shares = shares.reshape(EXPERTS, CAP, width)
     returned = lax.all_to_all(shares, "row", split_axis=0, concat_axis=0, tiled=True)
     mixed = combine_rows(returned.reshape(-1, width), slot_index, gate_weights)

time: 239 us -> 225 us (0.941)
  the two profiles are of different devices: /device:TPU:24 before, /device:TPU:0 now
where the time goes in v4:
time: 225 us; the launch traced here: 224 us
  Pallas kernels  102 us (45%)
  matrix products  38.8 us (17%)
  local copies, waits for them, and re-layouts  26.2 us (12%)
  waiting for transfers between devices  26 us (12%)
  other arithmetic  18.9 us (8%)
  starting transfers between devices  11.5 us (5%)
    pallas_call x1, Pallas kernels, scatter_chips(): pl.pallas_call(scatter_kernel, out_shape=jax.ShapeDtypeStruct((slots, wid...  58 us
    pallas_call x1, Pallas kernels, gather_cols(): pl.pallas_call(functools.partial(gather_kernel, width), out_shape=jax.Sha...  44.3 us
    dot_general x1, matrix products, body(): up_part = jnp.dot(normed, w_up[0], preferred_element_type=jnp.float32)  15.9 us
    ppermute x1, waiting for transfers between devices, body(): summed = keep + lax.ppermute(give, 'core', perm=[(0, 1), (1, 0)])  13.1 us
    another operation x1, local copies, waits for them, and re-layouts, body(): down = w_down[0].reshape(w_down.shape[1], chips, 2, width)  12.8 us
    all_to_all x1, waiting for transfers between devices, body(): lax.all_to_all(shares, 'row', split_axis=0, concat_axis=0, tiled=True)  12.8 us
    dot_general x1, matrix products, body(): jnp.einsum('sf,fkjw->jksw', hidden, down, preferred_element_type=jnp.floa...  11.6 us
    add x1, other arithmetic, body(): summed = keep + lax.ppermute(give, 'core', perm=[(0, 1), (1, 0)])  10.1 us
  transfers between devices with their start and end apart: 3, of which 2 were waited for; matrix products, arithmetic and copies ran while one was open for 6% of the time, Pallas kernels for 0%

profile of v4, /device:TPU:0, one launch (start us, length us, event | category | flops | bytes accessed | tf_op | source)
XLA Modules:
  0.0 223.9 jit_solution(14603437270507567175)
XLA Ops:
  0.0 0.8 copy.30
  0.8 0.1 eq.42
  1.0 0.1 eq.38
  1.1 1.1 reduce-window.6
  2.3 0.2 slice_reduce_fusion
  2.5 0.1 fusion.16
  2.6 0.1 reduce_sum.39
  2.8 0.1 copy.32
  2.8 0.7 compare_select_fusion
  3.5 0.3 convert_reduce_fusion
  3.8 2.0 convolution_convert_fusion
  5.9 6.3 %all-to-all-start = ((bf16[8,128,256]{2,1,0:T(8,128)(2,1)}), bf16[8,128,256]{2,1,0:T(8,128)(2,1)S(1)}, u32[]{:S(2)}, u32[]{:S(2)}) async-start(bf16[8,128,256]{2,1,0:T(8,128)(2,1)} %bitcast.2), calls=%async_computation | async-start | bytes 1048576 | tf_op jit(solution)/shard_map/all_to_all | solution.py:230
  12.2 12.8 %reshape_squeeze.3 = bf16[896,8,2,256]{3,2,1,0:T(2,128)(2,1)} reshape(bf16[1,896,4096]{2,1,0:T(8,128)(2,1)} %param.13) | data formatting | bytes 14680064 | tf_op jit(solution)/shard_map/reshape;squeeze | solution.py:239
  25.0 0.0 all-to-all-done
  25.0 0.0 copy-start.2
  25.0 0.8 copy-done.2
  25.8 0.0 copy-start.5
  25.8 44.3 %shard_map.73 = bf16[1024,4096]{1,0:T(8,128)(2,1)} custom-call(bf16[1024,256]{1,0:T(8,128)(2,1)} %bitcast.34), custom_call_target="tpu_custom_call" | custom-call | tf_op jit(solution)/shard_map/pallas_call | solution.py:118
  70.2 0.0 copy-start
  70.2 0.0 slice-start
  70.2 5.2 %fusion = f32[1024]{0:T(1024)S(1)} fusion(bf16[1024,4096]{1,0:T(8,128)(2,1)} %shard_map.73), kind=kLoop, calls=%fused_computation.3 | loop fusion | flops 12581888 | bytes 8392704 | tf_op jit(solution)/shard_map/reduce_sum | solution.py:19
  75.4 0.0 copy-done.5
  75.4 0.5 copy-done
  75.9 0.0 slice-start.1
  75.9 15.9 %fusion.5 = f32[1024,896]{1,0:T(8,128)S(1)} fusion(bf16[1,4096,896]{2,1,0:T(8,128)(2,1)} %param.12, bf16[1024,4096]{1,0:T(8,128)(2,1)S(1)} %copy-done, f32[4096]{0:T(1024)S(1)} %copy-done.5, f32[1024]{0:T(1024)S(1)} %add_rsqrt_fusion), kind=kOutput, calls=%fused_computation.10 | convolution fusion | flops 7532969984 | bytes 19419136 | tf_op jit(solution)/shard_map/dot_general | solution.py:237
  91.8 0.0 slice-done
  91.8 0.0 slice-done.1
  91.9 9.2 %multiply_convert_fusion = bf16[1024,896]{1,0:T(8,128)(2,1)S(1)} fusion(f32[1024,896]{1,0:T(8,128)S(1)} %fusion.5, bf16[1,4096,896]{2,1,0:T(8,128)(2,1)S(1)} %bitcast.36, bf16[1024,4096]{1,0:T(8,128)(2,1)S(1)} %copy-done, f32[4096]{0:T(1024)S(1)} %copy-done.5, f32[1024]{0:T(1024)S(1)} %add_rsqrt_fusion), kind=kOutput, calls=%fused_computation.14 | convolution fusion | flops 7538475008 | bytes 21254144 | tf_op jit(solution)/shard_map/dot_general | solution.py:236
  101.1 11.6 %fusion.3 = f32[1024,8,2,256]{3,0,1,2:T(8,128)S(1)} fusion(bf16[896,8,2,256]{3,2,1,0:T(2,128)(2,1)} %reshape_squeeze.3, bf16[1024,896]{1,0:T(8,128)(2,1)S(1)} %multiply_convert_fusion), kind=kOutput, calls=%fused_computation.8 | convolution fusion | flops 7516192768 | bytes 25952256 | tf_op jit(solution)/shard_map/sf,fkjw->jksw/dot_general | solution.py:240
  112.7 0.0 copy-start.1
  112.7 4.1 %dynamic-slice_bitcast_fusion = f32[8,1024,256]{2,1,0:T(8,128)} fusion(f32[1024,8,2,256]{3,0,1,2:T(8,128)S(1)} %fusion.3, s32[]{:T(128)S(6)} %select_n.11), kind=kLoop, calls=%fused_computation.7 | loop fusion | bytes 16777220 | tf_op jit(solution)/shard_map/jit(dynamic_index_in_dim)/squeeze | solution.py:243
  116.8 4.1 %copy-done.1 = f32[1024,8,2,256]{3,0,1,2:T(8,128)} copy-done((f32[1024,8,2,256]{3,0,1,2:T(8,128)}, f32[1024,8,2,256]{3,0,1,2:T(8,128)S(1)}, u32[]{:S(2)}) %copy-start.1) | copy-done | bytes 16777240
  120.9 0.4 collective-permute-start
  121.3 13.1 %collective-permute-done = f32[8,1024,256]{2,1,0:T(8,128)} collective-permute-done((f32[8,1024,256]{2,1,0:T(8,128)}, f32[8,1024,256]{2,1,0:T(8,128)}, u32[]{:S(2)}, u32[]{:S(2)}) %collective-permute-start) | collective-permute-done | bytes 8388640 | tf_op jit(solution)/shard_map/ppermute | solution.py:244
  134.4 10.1 %bitcast_add_fusion.parts = f32[8,1024,256]{2,1,0:T(8,128)} fusion(f32[8,1024,256]{2,1,0:T(8,128)} %collective-permute-done, f32[1024,8,2,256]{3,0,1,2:T(8,128)} %copy-done.1, s32[]{:T(128)S(6)} %select_n.10), kind=kLoop, calls=%fused_computation.6 | loop fusion | flops 2097152 | bytes 25165828 | tf_op jit(solution)/shard_map/add | solution.py:244
  144.5 0.0 copy-start.4
  144.5 58.0 %shard_map.74 = f32[1024,256]{1,0:T(8,128)} custom-call(f32[8,1024,256]{2,1,0:T(8,128)} %bitcast_add_fusion.parts), custom_call_target="tpu_custom_call" | custom-call | tf_op jit(solution)/shard_map/pallas_call | solution.py:203
  202.5 4.8 %all-to-all-start.1 = ((f32[8,128,256]{2,1,0:T(8,128)}), f32[8,128,256]{2,1,0:T(8,128)S(1)}, u32[]{:S(2)}, u32[]{:S(2)}) async-start(f32[8,128,256]{2,1,0:T(8,128)} %bitcast.11), calls=%async_computation.1 | async-start | bytes 2097152 | tf_op jit(solution)/shard_map/all_to_all | solution.py:247
  207.3 0.1 copy.36
  207.5 0.1 reshape.55
  207.6 0.0 copy-done.4
  207.6 0.1 copy.37
  207.8 12.8 %all-to-all-done.1 = f32[8,128,256]{2,1,0:T(8,128)S(1)} async-done(((f32[8,128,256]{2,1,0:T(8,128)}), f32[8,128,256]{2,1,0:T(8,128)S(1)}, u32[]{:S(2)}, u32[]{:S(2)}) %all-to-all-start.1) | async-done | bytes 1048608 | tf_op jit(solution)/shard_map/all_to_all | solution.py:247
  220.6 1.6 gather_fusion
  222.2 0.3 reshape.54
  222.5 0.7 multiply_reduce_fusion
  223.2 0.0 copy-done.3
  223.2 0.7 add_convert_fusion
  (7 shorter events, 0.1 us)
Async XLA Ops:
  5.9 19.2 %all-to-all-start = ((bf16[8,128,256]{2,1,0:T(8,128)(2,1)}), bf16[8,128,256]{2,1,0:T(8,128)(2,1)S(1)}, u32[]{:S(2)}, u32[]{:S(2)}) async-start(bf16[8,128,256]{2,1,0:T(8,128)(2,1)} %bitcast.2), calls=%async_computation | async-start | bytes 1048576 | tf_op jit(solution)/shard_map/all_to_all | solution.py:230
  25.0 0.8 copy-start.2
  25.8 49.6 %copy-start.5 = (f32[4096]{0:T(1024)S(1)}, f32[4096]{0:T(1024)}, u32[]{:S(2)}) copy-start(f32[4096]{0:T(1024)} %param.8) | copy-start | bytes 49156
  70.2 5.8 %copy-start = (bf16[1024,4096]{1,0:T(8,128)(2,1)S(1)}, bf16[1024,4096]{1,0:T(8,128)(2,1)}, u32[]{:S(2)}) copy-start(bf16[1024,4096]{1,0:T(8,128)(2,1)} %shard_map.73) | copy-start | bytes 25165828
  70.2 21.7 %slice-start = ((s8[7340032]{0:T(1024)(128)(4,1)}), s8[3145728]{0:T(1024)(128)(4,1)S(1)}, s32[]{:S(2)}) async-start(s8[7340032]{0:T(1024)(128)(4,1)} %bitcast.35), calls=%async_computation.2 | async-start | bytes 6291456
  75.9 15.9 %slice-start.1 = ((s8[7340032]{0:T(1024)(128)(4,1)}), s8[4194304]{0:T(1024)(128)(4,1)S(1)}, s32[]{:S(2)}) async-start(s8[7340032]{0:T(1024)(128)(4,1)} %bitcast.35), calls=%async_computation.3 | async-start | bytes 8388608
  112.7 8.2 %copy-start.1 = (f32[1024,8,2,256]{3,0,1,2:T(8,128)}, f32[1024,8,2,256]{3,0,1,2:T(8,128)S(1)}, u32[]{:S(2)}) copy-start(f32[1024,8,2,256]{3,0,1,2:T(8,128)S(1)} %fusion.3) | copy-start | bytes 50331652
  120.9 13.5 %collective-permute-start = (f32[8,1024,256]{2,1,0:T(8,128)}, f32[8,1024,256]{2,1,0:T(8,128)}, u32[]{:S(2)}, u32[]{:S(2)}) collective-permute-start(f32[8,1024,256]{2,1,0:T(8,128)} %dynamic-slice_bitcast_fusion), channel_id=1, source_target_pairs={{0,1},{1,0},{2,3},{3,2},{4,5},{5,4},{6,7},{7,6},{8,9},{9,8},{10,11... | collective-permute-start | bytes 25165832 | tf_op jit(solution)/shard_map/ppermute | solution.py:244
  144.5 63.1 %copy-start.4 = (f32[256,2]{0,1:T(2,128)S(1)}, f32[256,2]{0,1:T(2,128)}, u32[]{:S(2)}) copy-start(f32[256,2]{0,1:T(2,128)} %param.10) | copy-start | bytes 6148
  144.5 78.7 %copy-start.3 = (bf16[256,256]{1,0:T(8,128)(2,1)S(1)}, bf16[256,256]{1,0:T(8,128)(2,1)}, u32[]{:S(2)}) copy-start(bf16[256,256]{1,0:T(8,128)(2,1)} %param.7) | copy-start | bytes 393220
  202.5 18.1 %all-to-all-start.1 = ((f32[8,128,256]{2,1,0:T(8,128)}), f32[8,128,256]{2,1,0:T(8,128)S(1)}, u32[]{:S(2)}, u32[]{:S(2)}) async-start(f32[8,128,256]{2,1,0:T(8,128)} %bitcast.11), calls=%async_computation.1 | async-start | bytes 2097152 | tf_op jit(solution)/shard_map/all_to_all | solution.py:247

commit v5 on v4

--- a/solution.py
+++ b/solution.py
@@ -217,6 +217,39 @@
     )(parts)
 
 
+def exchange_kernel(rows, src, out, send_sem, recv_sem):
+    me, chip, core = lax.axis_index("row"), lax.axis_index("chip"), lax.axis_index("core")
+    barrier = pltpu.get_barrier_semaphore()
+    for d in range(1, rows):
+        peer = lax.rem(me + d, rows)
+        pl.semaphore_signal(barrier, inc=1, device_id=(peer, chip, core), device_id_type=MESH)
+    pl.semaphore_wait(barrier, rows - 1)
+    out[me] = src[me]
+    copies = []
+    for d in range(1, rows):
+        peer = lax.rem(me + d, rows)
+        copy = pltpu.make_async_remote_copy(
+            src_ref=src.at[peer], dst_ref=out.at[me], send_sem=send_sem.at[d],
+            recv_sem=recv_sem.at[d], device_id=(peer, chip, core), device_id_type=MESH,
+        )
+        copy.start()
+        copies.append(copy)
+    for copy in copies:
+        copy.wait()
+
+
+def exchange_rows(blocks, collective_id):
+    rows = blocks.shape[0]
+    return pl.pallas_call(
+        functools.partial(exchange_kernel, rows),
+        out_shape=jax.ShapeDtypeStruct(blocks.shape, blocks.dtype),
+        in_specs=[pl.BlockSpec(memory_space=pltpu.VMEM)],
+        out_specs=pl.BlockSpec(memory_space=pltpu.VMEM),
+        scratch_shapes=[pltpu.SemaphoreType.DMA((rows,)), pltpu.SemaphoreType.DMA((rows,))],
+        compiler_params=pltpu.CompilerParams(collective_id=collective_id, has_side_effects=True),
+    )(blocks)
+
+
 def body(tokens, norm_gain, expert_ids, gate_weights, w_gate, w_up, w_down):
     chips = lax.psum(1, "chip")
     width = tokens.shape[1]
@@ -227,7 +260,7 @@
         jnp.bfloat16
     )
     packed = packed.reshape(EXPERTS, CAP, width)
-    arrived = lax.all_to_all(packed, "row", split_axis=0, concat_axis=0, tiled=True)
+    arrived = exchange_rows(packed, 2)
     arrived = arrived.reshape(EXPERTS * CAP, width)
     slots = arrived.shape[0]
 
@@ -244,7 +277,7 @@
     summed = keep + lax.ppermute(give, "core", perm=[(0, 1), (1, 0)])
     shares = scatter_chips(summed)
     shares = shares.reshape(EXPERTS, CAP, width)
-    returned = lax.all_to_all(shares, "row", split_axis=0, concat_axis=0, tiled=True)
+    returned = exchange_rows(shares, 3)
     mixed = combine_rows(returned.reshape(-1, width), slot_index, gate_weights)
     return (tokens.astype(jnp.float32) + mixed).astype(jnp.bfloat16)
 

time: 225 us -> 239 us (1.062)
  Pallas kernels: 102 us -> 132 us
  waiting for transfers between devices: 26 us -> 12.7 us
  starting transfers between devices: 11.5 us -> 0.38 us
  matrix products: 38.8 us -> 46.9 us
    pallas_call x0 -> x2, Pallas kernels: none -> 30.5 us  [exchange_rows(): pl.pallas_call(functools.partial(exchange_kernel, rows), out_shape=jax.Sh...]
    all_to_all x2 -> x0, waiting for transfers between devices: 12.8 us -> none  [the longest x1 12.8 us: body(): lax.all_to_all(shares, 'row', split_axis=0, concat_axis=0, tiled=True)]
    all_to_all x2 -> x0, starting transfers between devices: 11.1 us -> none  [the longest x1 6.32 us: body(): lax.all_to_all(packed, 'row', split_axis=0, concat_axis=0, tiled=True)]
    dot_general x1, matrix products: 11.6 us -> 18.2 us  [body(): jnp.einsum('sf,fkjw->jksw', hidden, down, preferred_element_type=jnp.floa...]
    dot_general x1, matrix products: 9.24 us -> 14.1 us  [body(): gate_part = jnp.dot(normed, w_gate[0], preferred_element_type=jnp.float32)]
    unnamed x18 -> x14, local copies, waits for them, and re-layouts: 6.35 us -> 1.94 us
    dot_general x1, matrix products: 15.9 us -> 12.6 us  [body(): up_part = jnp.dot(normed, w_up[0], preferred_element_type=jnp.float32)]
    squeeze x1, local copies, waits for them, and re-layouts: 4.11 us -> 7.14 us  [body(): give = lax.dynamic_index_in_dim(split, 1 - core, 0, keepdims=False)]
  transfers between devices with their start and end apart: 3 -> 1, of which waited for: 2 -> 1; matrix products, arithmetic and copies ran while one was open for 6% -> 0% of each run, Pallas kernels for 0% -> 0%
where the time goes in v5:
time: 239 us; the launch traced here: 237 us
  Pallas kernels  132 us (55%)
  matrix products  46.9 us (20%)
  local copies, waits for them, and re-layouts  26 us (11%)
  other arithmetic  18.8 us (8%)
  waiting for transfers between devices  12.7 us (5%)
    pallas_call x1, Pallas kernels, scatter_chips(): pl.pallas_call(scatter_kernel, out_shape=jax.ShapeDtypeStruct((slots, wid...  57 us
    pallas_call x1, Pallas kernels, gather_cols(): pl.pallas_call(functools.partial(gather_kernel, width), out_shape=jax.Sha...  44.5 us
    pallas_call x2, Pallas kernels, exchange_rows(): pl.pallas_call(functools.partial(exchange_kernel, rows), out_shape=jax.Sh...  30.5 us
    dot_general x1, matrix products, body(): jnp.einsum('sf,fkjw->jksw', hidden, down, preferred_element_type=jnp.floa...  18.2 us
    dot_general x1, matrix products, body(): gate_part = jnp.dot(normed, w_gate[0], preferred_element_type=jnp.float32)  14.1 us
    another operation x1, local copies, waits for them, and re-layouts, body(): down = w_down[0].reshape(w_down.shape[1], chips, 2, width)  12.9 us
    ppermute x1, waiting for transfers between devices, body(): summed = keep + lax.ppermute(give, 'core', perm=[(0, 1), (1, 0)])  12.7 us
    dot_general x1, matrix products, body(): up_part = jnp.dot(normed, w_up[0], preferred_element_type=jnp.float32)  12.6 us
  transfers between devices with their start and end apart: 1, of which 1 were waited for; matrix products, arithmetic and copies ran while one was open for 0% of the time, Pallas kernels for 0%

profile of v5, /device:TPU:0, one launch (start us, length us, event | category | flops | bytes accessed | tf_op | source)
XLA Modules:
  0.0 237.1 jit_solution(12072904588580132891)
XLA Ops:
  0.0 0.8 copy.30
  0.8 0.1 eq.42
  1.0 0.1 eq.38
  1.1 1.1 reduce-window.6
  2.3 0.2 slice_reduce_fusion
  2.5 0.1 fusion.16
  2.6 0.1 reduce_sum.39
  2.8 0.1 copy.32
  2.8 0.7 compare_select_fusion
  3.5 0.3 convert_reduce_fusion
  3.8 2.0 convolution_convert_fusion
  5.9 13.9 %shard_map.73 = bf16[8,128,256]{2,1,0:T(8,128)(2,1)} custom-call(bf16[8,128,256]{2,1,0:T(8,128)(2,1)} %bitcast.38), custom_call_target="tpu_custom_call" | custom-call | tf_op jit(solution)/shard_map/pallas_call | solution.py:243
  19.7 44.5 %shard_map.74 = bf16[1024,4096]{1,0:T(8,128)(2,1)} custom-call(bf16[1024,256]{1,0:T(8,128)(2,1)} %bitcast.37), custom_call_target="tpu_custom_call" | custom-call | tf_op jit(solution)/shard_map/pallas_call | solution.py:118
  64.2 5.1 %fusion = f32[1024]{0:T(1024)S(1)} fusion(bf16[1024,4096]{1,0:T(8,128)(2,1)} %shard_map.74), kind=kLoop, calls=%fused_computation.3 | loop fusion | flops 12581888 | bytes 8392704 | tf_op jit(solution)/shard_map/reduce_sum | solution.py:19
  69.3 0.0 copy-start.3
  69.3 12.9 %reshape_squeeze.3 = bf16[896,8,2,256]{3,2,1,0:T(2,128)(2,1)} reshape(bf16[1,896,4096]{2,1,0:T(8,128)(2,1)} %param.13) | data formatting | bytes 14680064 | tf_op jit(solution)/shard_map/reshape;squeeze | solution.py:272
  82.2 0.0 copy-done.3
  82.2 0.0 slice-start
  82.2 12.6 %fusion.5 = f32[1024,896]{1,0:T(8,128)S(1)} fusion(bf16[1,4096,896]{2,1,0:T(8,128)(2,1)} %param.12, bf16[1024,4096]{1,0:T(8,128)(2,1)} %shard_map.74, f32[4096]{0:T(1024)S(1)} %copy-done.3, f32[1024]{0:T(1024)S(1)} %add_rsqrt_fusion), kind=kOutput, calls=%fused_computation.10 | convolution fusion | flops 7532969984 | bytes 19419136 | tf_op jit(solution)/shard_map/dot_general | solution.py:270
  94.8 0.0 slice-start.1
  94.8 14.1 %multiply_convert_fusion = bf16[1024,896]{1,0:T(8,128)(2,1)S(1)} fusion(f32[1024,896]{1,0:T(8,128)S(1)} %fusion.5, bf16[1,4096,896]{2,1,0:T(8,128)(2,1)} %param.11, bf16[1024,4096]{1,0:T(8,128)(2,1)} %shard_map.74, f32[4096]{0:T(1024)S(1)} %copy-done.3, f32[1024]{0:T(1024)S(1)} %add_rsqrt_fusion), kind=kOutput, calls=%fused_computation.14 | convolution fusion | flops 7538475008 | bytes 21254144 | tf_op jit(solution)/shard_map/dot_general | solution.py:269
  108.9 0.0 slice-done
  108.9 0.0 slice-done.1
  108.9 18.2 %fusion.3 = f32[1024,8,2,256]{3,0,1,2:T(8,128)} fusion(bf16[896,8,2,256]{3,2,1,0:T(2,128)(2,1)S(1)} %bitcast.36, bf16[1024,896]{1,0:T(8,128)(2,1)S(1)} %multiply_convert_fusion), kind=kOutput, calls=%fused_computation.8 | convolution fusion | flops 7516192768 | bytes 25952256 | tf_op jit(solution)/shard_map/sf,fkjw->jksw/dot_general | solution.py:273
  127.1 0.0 copy-start.2
  127.1 7.1 %dynamic-slice_bitcast_fusion = f32[8,1024,256]{2,1,0:T(8,128)} fusion(f32[1024,8,2,256]{3,0,1,2:T(8,128)} %fusion.3, s32[]{:T(128)S(6)} %select_n.11), kind=kLoop, calls=%fused_computation.7 | loop fusion | bytes 16777220 | tf_op jit(solution)/shard_map/jit(dynamic_index_in_dim)/squeeze | solution.py:276
  134.3 0.4 collective-permute-start
  134.6 0.1 copy.36
  134.8 0.1 reshape.55
  134.9 0.0 copy-done.2
  134.9 0.1 copy.37
  135.1 12.7 %collective-permute-done = f32[8,1024,256]{2,1,0:T(8,128)} collective-permute-done((f32[8,1024,256]{2,1,0:T(8,128)}, f32[8,1024,256]{2,1,0:T(8,128)}, u32[]{:S(2)}, u32[]{:S(2)}) %collective-permute-start) | collective-permute-done | bytes 8388640 | tf_op jit(solution)/shard_map/ppermute | solution.py:277
  147.8 10.1 %bitcast_add_fusion.parts = f32[8,1024,256]{2,1,0:T(8,128)} fusion(f32[8,1024,256]{2,1,0:T(8,128)} %collective-permute-done, f32[1024,8,2,256]{3,0,1,2:T(8,128)} %fusion.3, s32[]{:T(128)S(6)} %select_n.10), kind=kLoop, calls=%fused_computation.6 | loop fusion | flops 2097152 | bytes 25165828 | tf_op jit(solution)/shard_map/add | solution.py:277
  157.8 0.0 copy-start.1
  157.8 57.0 %shard_map.75 = f32[1024,256]{1,0:T(8,128)S(1)} custom-call(f32[8,1024,256]{2,1,0:T(8,128)} %bitcast_add_fusion.parts), custom_call_target="tpu_custom_call" | custom-call | tf_op jit(solution)/shard_map/pallas_call | solution.py:203
  214.9 0.0 copy-start
  214.9 1.0 copy-done
  215.8 16.7 %shard_map.76 = f32[8,128,256]{2,1,0:T(8,128)} custom-call(f32[8,128,256]{2,1,0:T(8,128)} %bitcast.33), custom_call_target="tpu_custom_call" | custom-call | tf_op jit(solution)/shard_map/pallas_call | solution.py:243
  232.5 2.8 %gather_fusion = f32[512,256]{1,0:T(8,128)S(1)} fusion(f32[1024,256]{1,0:T(8,128)} %bitcast.34, s32[1024]{0:T(1024)S(1)} %pad_clamp_fusion), kind=kCustom, calls=%fused_computation | custom fusion | bytes 1050624 | tf_op jit(solution)/shard_map/gather | solution.py:38
  235.3 0.3 reshape.54
  235.7 0.7 multiply_reduce_fusion
  236.4 0.0 copy-done.1
  236.4 0.7 add_convert_fusion
  (6 shorter events, 0.1 us)
Async XLA Ops:
  69.3 12.9 %copy-start.3 = (f32[4096]{0:T(1024)S(1)}, f32[4096]{0:T(1024)}, u32[]{:S(2)}) copy-start(f32[4096]{0:T(1024)} %param.8) | copy-start | bytes 49156
  82.2 26.7 %slice-start = ((s8[7340032]{0:T(1024)(128)(4,1)}), s8[4194304]{0:T(1024)(128)(4,1)S(1)}, s32[]{:S(2)}) async-start(s8[7340032]{0:T(1024)(128)(4,1)} %bitcast.35), calls=%async_computation | async-start | bytes 8388608
  94.8 14.1 %slice-start.1 = ((s8[7340032]{0:T(1024)(128)(4,1)}), s8[3145728]{0:T(1024)(128)(4,1)S(1)}, s32[]{:S(2)}) async-start(s8[7340032]{0:T(1024)(128)(4,1)} %bitcast.35), calls=%async_computation.1 | async-start | bytes 6291456
  127.1 7.8 %copy-start.2 = (f32[256,2]{0,1:T(2,128)S(1)}, f32[256,2]{0,1:T(2,128)}, u32[]{:S(2)}) copy-start(f32[256,2]{0,1:T(2,128)} %param.10) | copy-start | bytes 6148
  134.3 13.5 %collective-permute-start = (f32[8,1024,256]{2,1,0:T(8,128)}, f32[8,1024,256]{2,1,0:T(8,128)}, u32[]{:S(2)}, u32[]{:S(2)}) collective-permute-start(f32[8,1024,256]{2,1,0:T(8,128)} %dynamic-slice_bitcast_fusion), channel_id=1, source_target_pairs={{0,1},{1,0},{2,3},{3,2},{4,5},{5,4},{6,7},{7,6},{8,9},{9,8},{10,11... | collective-permute-start | bytes 25165832 | tf_op jit(solution)/shard_map/ppermute | solution.py:277
  157.8 78.5 %copy-start.1 = (bf16[256,256]{1,0:T(8,128)(2,1)S(1)}, bf16[256,256]{1,0:T(8,128)(2,1)}, u32[]{:S(2)}) copy-start(bf16[256,256]{1,0:T(8,128)(2,1)} %param.7) | copy-start | bytes 393220
  214.9 1.0 copy-start

commit v6 on v4

--- a/solution.py
+++ b/solution.py
@@ -144,8 +144,10 @@
     lax.fori_loop(0, rows // step, one, 0)
 
 
-def scatter_kernel(parts, out, sending, landed, send_sem, recv_sem):
+def scatter_kernel(width, parts, out, mine, theirs, sending, landed, local_sem, sister_send,
+                   sister_recv, send_sem, recv_sem):
     row, me, core = lax.axis_index("row"), lax.axis_index("chip"), lax.axis_index("core")
+    sister = 1 - core
     side, y = me // 4, me % 4
     partner = lax.rem(me + 4, 8)
     up = side * 4 + lax.rem(y + 1, 4)
@@ -155,10 +157,32 @@
     def far(chip):
         return lax.rem(chip + 4, 8)
 
+    def columns(chip, half):
+        start = pl.multiple_of((chip * 2 + half) * width, width)
+        return parts.at[:, pl.ds(start, width)]
+
     barrier = pltpu.get_barrier_semaphore()
-    for chip in (partner, up, down):
-        pl.semaphore_signal(barrier, inc=1, device_id=(row, chip, core), device_id_type=MESH)
-    pl.semaphore_wait(barrier, 3)
+    for chip, half in ((partner, core), (up, core), (down, core), (me, sister)):
+        pl.semaphore_signal(barrier, inc=1, device_id=(row, chip, half), device_id_type=MESH)
+    pl.semaphore_wait(barrier, 4)
+
+    order = (far(down), across, up, far(across), down, far(up), partner, me)
+    swaps, loads = [], []
+    for slot, chip in enumerate(order):
+        swap = pltpu.make_async_remote_copy(
+            src_ref=columns(chip, sister), dst_ref=theirs.at[slot], send_sem=sister_send.at[slot],
+            recv_sem=sister_recv.at[slot], device_id=(row, me, sister), device_id_type=MESH,
+        )
+        swap.start()
+        swaps.append(swap)
+        load = pltpu.make_async_copy(columns(chip, core), mine.at[slot], local_sem.at[slot])
+        load.start()
+        loads.append(load)
+
+    def ready(slot):
+        loads[slot].wait()
+        swaps[slot].wait_recv()
+        return (mine.at[slot], theirs.at[slot])
 
     def send(tag, chip):
         copy = pltpu.make_async_remote_copy(
@@ -175,44 +199,48 @@
         ).wait_recv()
 
     sent = []
-    for tag, chip, target in ((0, down, far(down)), (1, down, across), (2, up, up),
-                              (3, up, far(across))):
-        add_blocks(sending.at[tag], parts.at[target])
+    for tag, chip in ((0, down), (1, down), (2, up), (3, up)):
+        add_blocks(sending.at[tag], *ready(tag))
         sent.append(send(tag, chip))
     arrive(1)
-    add_blocks(sending.at[4], parts.at[down], landed.at[1])
+    add_blocks(sending.at[4], *ready(4), landed.at[1])
     sent.append(send(4, down))
     arrive(3)
-    add_blocks(sending.at[5], parts.at[far(up)], landed.at[3])
+    add_blocks(sending.at[5], *ready(5), landed.at[3])
     sent.append(send(5, up))
     arrive(0)
     arrive(5)
-    add_blocks(sending.at[6], parts.at[partner], landed.at[0], landed.at[5])
+    add_blocks(sending.at[6], *ready(6), landed.at[0], landed.at[5])
     sent.append(send(6, partner))
     arrive(2)
     arrive(4)
-    add_blocks(out, parts.at[me], landed.at[2], landed.at[4])
+    add_blocks(out, *ready(7), landed.at[2], landed.at[4])
     arrive(6)
     add_blocks(out, out, landed.at[6])
-    for copy in sent:
+    for copy in sent + swaps:
         copy.wait_send()
 
 
-def scatter_chips(parts):
-    chips, slots, width = parts.shape
+def scatter_cols(parts, width):
+    slots = parts.shape[0]
     return pl.pallas_call(
-        scatter_kernel,
+        functools.partial(scatter_kernel, width),
         out_shape=jax.ShapeDtypeStruct((slots, width), jnp.float32),
-        in_specs=[pl.BlockSpec(memory_space=pltpu.VMEM)],
+        in_specs=[pl.BlockSpec(memory_space=pl.ANY)],
         out_specs=pl.BlockSpec(memory_space=pltpu.VMEM),
         scratch_shapes=[
+            pltpu.VMEM((8, slots, width), jnp.float32),
+            pltpu.VMEM((8, slots, width), jnp.float32),
             pltpu.VMEM((7, slots, width), jnp.bfloat16),
             pltpu.VMEM((7, slots, width), jnp.bfloat16),
+            pltpu.SemaphoreType.DMA((8,)),
+            pltpu.SemaphoreType.DMA((8,)),
+            pltpu.SemaphoreType.DMA((8,)),
             pltpu.SemaphoreType.DMA((7,)),
             pltpu.SemaphoreType.DMA((7,)),
         ],
         compiler_params=pltpu.CompilerParams(
-            collective_id=1, has_side_effects=True, vmem_limit_bytes=48 * 1024 * 1024
+            collective_id=1, has_side_effects=True, vmem_limit_bytes=56 * 1024 * 1024
         ),
     )(parts)
 
@@ -236,13 +264,8 @@
     gate_part = jnp.dot(normed, w_gate[0], preferred_element_type=jnp.float32)
     up_part = jnp.dot(normed, w_up[0], preferred_element_type=jnp.float32)
     hidden = (jax.nn.silu(gate_part) * up_part).astype(jnp.bfloat16)
-    down = w_down[0].reshape(w_down.shape[1], chips, 2, width)
-    split = jnp.einsum("sf,fkjw->jksw", hidden, down, preferred_element_type=jnp.float32)
-
-    keep = lax.dynamic_index_in_dim(split, core, 0, keepdims=False)
-    give = lax.dynamic_index_in_dim(split, 1 - core, 0, keepdims=False)
-    summed = keep + lax.ppermute(give, "core", perm=[(0, 1), (1, 0)])
-    shares = scatter_chips(summed)
+    outputs = jnp.dot(hidden, w_down[0], preferred_element_type=jnp.float32)
+    shares = scatter_cols(outputs, width)
     shares = shares.reshape(EXPERTS, CAP, width)
     returned = lax.all_to_all(shares, "row", split_axis=0, concat_axis=0, tiled=True)
     mixed = combine_rows(returned.reshape(-1, width), slot_index, gate_weights)

time: 225 us -> 192 us (0.85)
  local copies, waits for them, and re-layouts: 26.2 us -> 4.34 us
  blocking collectives: 0 us -> 16.3 us
  waiting for transfers between devices: 26 us -> 13.4 us
  other arithmetic: 18.9 us -> 8.85 us
  starting transfers between devices: 11.5 us -> 3.7 us
    all_to_all x0 -> x1, blocking collectives: none -> 16.3 us  [body(): lax.all_to_all(packed, 'row', split_axis=0, concat_axis=0, tiled=True)]
    ppermute x1 -> x0, waiting for transfers between devices: 13.1 us -> none  [body(): summed = keep + lax.ppermute(give, 'core', perm=[(0, 1), (1, 0)])]
    another operation x2 -> x1, local copies, waits for them, and re-layouts: 12.9 us -> 0.01 us  [the longest x1 12.8 us: body(): down = w_down[0].reshape(w_down.shape[1], chips, 2, width)]
    add x1 -> x0, other arithmetic: 10.1 us -> none  [body(): summed = keep + lax.ppermute(give, 'core', perm=[(0, 1), (1, 0)])]
    all_to_all x1 -> x0, starting transfers between devices: 6.32 us -> none  [body(): lax.all_to_all(packed, 'row', split_axis=0, concat_axis=0, tiled=True)]
    unnamed x18 -> x14, local copies, waits for them, and re-layouts: 6.35 us -> 1.47 us
    squeeze x1 -> x0, local copies, waits for them, and re-layouts: 4.11 us -> none  [body(): give = lax.dynamic_index_in_dim(split, 1 - core, 0, keepdims=False)]
    dot_general x1, matrix products: 11.6 us -> 14.3 us  [body(): outputs = jnp.dot(hidden, w_down[0], preferred_element_type=jnp.float32)]
  transfers between devices with their start and end apart: 3 -> 1, of which waited for: 2 -> 1; matrix products, arithmetic and copies ran while one was open for 6% -> 0% of each run, Pallas kernels for 0% -> 0%
where the time goes in v6:
time: 192 us; the launch traced here: 191 us
  Pallas kernels  104 us (54%)
  matrix products  40.1 us (21%)
  blocking collectives  16.3 us (8%)
  waiting for transfers between devices  13.4 us (7%)
  other arithmetic  8.85 us (5%)
  local copies, waits for them, and re-layouts  4.34 us (2%)
  starting transfers between devices  3.7 us (2%)
    pallas_call x1, Pallas kernels, scatter_cols(): pl.pallas_call(functools.partial(scatter_kernel, width), out_shape=jax.Sh...  59.4 us
    pallas_call x1, Pallas kernels, gather_cols(): pl.pallas_call(functools.partial(gather_kernel, width), out_shape=jax.Sha...  44.3 us
    all_to_all x1, blocking collectives, body(): lax.all_to_all(packed, 'row', split_axis=0, concat_axis=0, tiled=True)  16.3 us
    dot_general x1, matrix products, body(): up_part = jnp.dot(normed, w_up[0], preferred_element_type=jnp.float32)  15.4 us
    dot_general x1, matrix products, body(): outputs = jnp.dot(hidden, w_down[0], preferred_element_type=jnp.float32)  14.3 us
    all_to_all x1, waiting for transfers between devices, body(): lax.all_to_all(shares, 'row', split_axis=0, concat_axis=0, tiled=True)  13.4 us
    dot_general x1, matrix products, body(): gate_part = jnp.dot(normed, w_gate[0], preferred_element_type=jnp.float32)  9.2 us
    reduce_sum x1, other arithmetic, normalize(): jnp.mean(values * values, axis=-1, keepdims=True) + 1e-05  5.22 us
  transfers between devices with their start and end apart: 1, of which 1 were waited for; matrix products, arithmetic and copies ran while one was open for 0% of the time, Pallas kernels for 0%

profile of v6, /device:TPU:0, one launch (start us, length us, event | category | flops | bytes accessed | tf_op | source)
XLA Modules:
  0.0 190.6 jit_solution(12462449919848064332)
XLA Ops:
  0.0 0.8 copy.21
  0.8 0.1 eq.42
  1.0 0.1 eq.38
  1.1 1.1 reduce-window.6
  2.3 0.2 slice_reduce_fusion
  2.5 0.1 fusion.15
  2.6 0.1 reduce_sum.39
  2.8 0.1 copy.23
  2.8 0.7 compare_select_fusion
  3.5 0.3 convert_reduce_fusion
  3.8 1.3 convolution_convert_fusion
  5.1 16.3 %all_to_all.10 = bf16[8,128,256]{2,1,0:T(8,128)(2,1)} all-to-all(bf16[8,128,256]{2,1,0:T(8,128)(2,1)S(1)} %bitcast.29), channel_id=1, replica_groups=mesh['row'=8,'chip'=8,'core'=2] {'row'}, dimensions={0} | all-to-all | bytes 1048576 | tf_op jit(solution)/shard_map/all_to_all | solution.py:258
  21.4 0.0 copy-start.3
  21.4 44.3 %shard_map.73 = bf16[1024,4096]{1,0:T(8,128)(2,1)} custom-call(bf16[1024,256]{1,0:T(8,128)(2,1)} %bitcast.28), custom_call_target="tpu_custom_call" | custom-call | tf_op jit(solution)/shard_map/pallas_call | solution.py:118
  65.7 0.0 copy-start
  65.7 0.0 slice-start
  65.7 5.2 %fusion = f32[1024]{0:T(1024)S(1)} fusion(bf16[1024,4096]{1,0:T(8,128)(2,1)} %shard_map.73), kind=kLoop, calls=%fused_computation.3 | loop fusion | flops 12581888 | bytes 8392704 | tf_op jit(solution)/shard_map/reduce_sum | solution.py:19
  71.0 0.0 copy-done.3
  71.0 0.5 copy-done
  71.5 0.0 slice-start.1
  71.5 15.4 %fusion.5 = f32[1024,896]{1,0:T(8,128)S(1)} fusion(bf16[1,4096,896]{2,1,0:T(8,128)(2,1)} %param.12, bf16[1024,4096]{1,0:T(8,128)(2,1)S(1)} %copy-done, f32[4096]{0:T(1024)S(1)} %copy-done.3, f32[1024]{0:T(1024)S(1)} %add_rsqrt_fusion), kind=kOutput, calls=%fused_computation.8 | convolution fusion | flops 7532969984 | bytes 19419136 | tf_op jit(solution)/shard_map/dot_general | solution.py:265
  86.9 0.0 slice-done
  86.9 0.0 slice-done.1
  86.9 9.2 %multiply_convert_fusion = bf16[1024,896]{1,0:T(8,128)(2,1)S(1)} fusion(f32[1024,896]{1,0:T(8,128)S(1)} %fusion.5, bf16[1,4096,896]{2,1,0:T(8,128)(2,1)S(1)} %bitcast.31, bf16[1024,4096]{1,0:T(8,128)(2,1)S(1)} %copy-done, f32[4096]{0:T(1024)S(1)} %copy-done.3, f32[1024]{0:T(1024)S(1)} %add_rsqrt_fusion), kind=kOutput, calls=%fused_computation.12 | convolution fusion | flops 7538475008 | bytes 21254144 | tf_op jit(solution)/shard_map/dot_general | solution.py:264
  96.1 14.3 %fusion.3.parts = f32[1024,4096]{1,0:T(8,128)} fusion(bf16[1024,896]{1,0:T(8,128)(2,1)S(1)} %multiply_convert_fusion, bf16[1,896,4096]{2,1,0:T(8,128)(2,1)} %param.13), kind=kOutput, calls=%fused_computation.6 | convolution fusion | flops 7516192768 | bytes 25952256 | tf_op jit(solution)/shard_map/dot_general | solution.py:267
  110.3 0.0 copy-start.2
  110.4 59.4 %shard_map.74 = f32[1024,256]{1,0:T(8,128)} custom-call(f32[1024,4096]{1,0:T(8,128)} %fusion.3.parts), custom_call_target="tpu_custom_call" | custom-call | tf_op jit(solution)/shard_map/pallas_call | solution.py:226
  169.7 0.0 copy-start.1
  169.7 3.7 %all-to-all-start.1 = ((f32[8,128,256]{2,1,0:T(8,128)}), f32[8,128,256]{2,1,0:T(8,128)S(1)}, u32[]{:S(2)}, u32[]{:S(2)}) async-start(f32[8,128,256]{2,1,0:T(8,128)} %bitcast.27), calls=%async_computation.1 | async-start | bytes 2097152 | tf_op jit(solution)/shard_map/all_to_all | solution.py:270
  173.5 0.1 copy.24
  173.6 0.1 reshape.55
  173.7 0.0 copy-done.2
  173.8 0.1 copy.25
  173.9 13.4 %all-to-all-done.1 = f32[8,128,256]{2,1,0:T(8,128)S(1)} async-done(((f32[8,128,256]{2,1,0:T(8,128)}), f32[8,128,256]{2,1,0:T(8,128)S(1)}, u32[]{:S(2)}, u32[]{:S(2)}) %all-to-all-start.1) | async-done | bytes 1048608 | tf_op jit(solution)/shard_map/all_to_all | solution.py:270
  187.3 1.6 gather_fusion
  188.9 0.3 reshape.54
  189.2 0.7 multiply_reduce_fusion
  189.9 0.0 copy-done.1
  189.9 0.7 add_convert_fusion
  (6 shorter events, 0.1 us)
Async XLA Ops:
  21.4 49.6 %copy-start.3 = (f32[4096]{0:T(1024)S(1)}, f32[4096]{0:T(1024)}, u32[]{:S(2)}) copy-start(f32[4096]{0:T(1024)} %param.8) | copy-start | bytes 49156
  65.7 5.8 %copy-start = (bf16[1024,4096]{1,0:T(8,128)(2,1)S(1)}, bf16[1024,4096]{1,0:T(8,128)(2,1)}, u32[]{:S(2)}) copy-start(bf16[1024,4096]{1,0:T(8,128)(2,1)} %shard_map.73) | copy-start | bytes 25165828
  65.7 21.1 %slice-start = ((s8[7340032]{0:T(1024)(128)(4,1)}), s8[3145728]{0:T(1024)(128)(4,1)S(1)}, s32[]{:S(2)}) async-start(s8[7340032]{0:T(1024)(128)(4,1)} %bitcast.30), calls=%async_computation.2 | async-start | bytes 6291456
  71.5 15.4 %slice-start.1 = ((s8[7340032]{0:T(1024)(128)(4,1)}), s8[4194304]{0:T(1024)(128)(4,1)S(1)}, s32[]{:S(2)}) async-start(s8[7340032]{0:T(1024)(128)(4,1)} %bitcast.30), calls=%async_computation.3 | async-start | bytes 8388608
  110.3 63.4 %copy-start.2 = (f32[256,2]{0,1:T(2,128)S(1)}, f32[256,2]{0,1:T(2,128)}, u32[]{:S(2)}) copy-start(f32[256,2]{0,1:T(2,128)} %param.10) | copy-start | bytes 6148
  169.7 20.1 %copy-start.1 = (bf16[256,256]{1,0:T(8,128)(2,1)S(1)}, bf16[256,256]{1,0:T(8,128)(2,1)}, u32[]{:S(2)}) copy-start(bf16[256,256]{1,0:T(8,128)(2,1)} %param.7) | copy-start | bytes 393220
  169.7 17.5 %all-to-all-start.1 = ((f32[8,128,256]{2,1,0:T(8,128)}), f32[8,128,256]{2,1,0:T(8,128)S(1)}, u32[]{:S(2)}, u32[]{:S(2)}) async-start(f32[8,128,256]{2,1,0:T(8,128)} %bitcast.27), calls=%async_computation.1 | async-start | bytes 2097152 | tf_op jit(solution)/shard_map/all_to_all | solution.py:270

commit v7 on v6

--- a/solution.py
+++ b/solution.py
@@ -144,8 +144,21 @@
     lax.fori_loop(0, rows // step, one, 0)
 
 
-def scatter_kernel(width, parts, out, mine, theirs, sending, landed, local_sem, sister_send,
-                   sister_recv, send_sem, recv_sem):
+def project(dst, hidden, weights, start):
+    rows = dst.shape[0]
+    step = 256
+    cols = pl.ds(pl.multiple_of(start, 256), dst.shape[1])
+
+    def one(i, carry):
+        part = pl.ds(pl.multiple_of(i * step, step), step)
+        dst[part, :] = jnp.dot(hidden[part, :], weights[:, cols], preferred_element_type=jnp.float32)
+        return carry
+
+    lax.fori_loop(0, rows // step, one, 0)
+
+
+def scatter_kernel(width, hidden, weights, out, mine, theirs, outgoing, sending, landed,
+                   sister_send, sister_recv, send_sem, recv_sem):
     row, me, core = lax.axis_index("row"), lax.axis_index("chip"), lax.axis_index("core")
     sister = 1 - core
     side, y = me // 4, me % 4
@@ -157,30 +170,24 @@
     def far(chip):
         return lax.rem(chip + 4, 8)
 
-    def columns(chip, half):
-        start = pl.multiple_of((chip * 2 + half) * width, width)
-        return parts.at[:, pl.ds(start, width)]
-
     barrier = pltpu.get_barrier_semaphore()
     for chip, half in ((partner, core), (up, core), (down, core), (me, sister)):
         pl.semaphore_signal(barrier, inc=1, device_id=(row, chip, half), device_id_type=MESH)
     pl.semaphore_wait(barrier, 4)
 
     order = (far(down), across, up, far(across), down, far(up), partner, me)
-    swaps, loads = [], []
+    swaps = []
     for slot, chip in enumerate(order):
+        project(outgoing.at[slot], hidden, weights, (chip * 2 + sister) * width)
         swap = pltpu.make_async_remote_copy(
-            src_ref=columns(chip, sister), dst_ref=theirs.at[slot], send_sem=sister_send.at[slot],
+            src_ref=outgoing.at[slot], dst_ref=theirs.at[slot], send_sem=sister_send.at[slot],
             recv_sem=sister_recv.at[slot], device_id=(row, me, sister), device_id_type=MESH,
         )
         swap.start()
         swaps.append(swap)
-        load = pltpu.make_async_copy(columns(chip, core), mine.at[slot], local_sem.at[slot])
-        load.start()
-        loads.append(load)
+        project(mine.at[slot], hidden, weights, (chip * 2 + core) * width)
 
     def ready(slot):
-        loads[slot].wait()
         swaps[slot].wait_recv()
         return (mine.at[slot], theirs.at[slot])
 
@@ -221,28 +228,28 @@
         copy.wait_send()
 
 
-def scatter_cols(parts, width):
-    slots = parts.shape[0]
+def scatter_cols(hidden, weights, width):
+    slots = hidden.shape[0]
     return pl.pallas_call(
         functools.partial(scatter_kernel, width),
         out_shape=jax.ShapeDtypeStruct((slots, width), jnp.float32),
-        in_specs=[pl.BlockSpec(memory_space=pl.ANY)],
+        in_specs=[pl.BlockSpec(memory_space=pltpu.VMEM)] * 2,
         out_specs=pl.BlockSpec(memory_space=pltpu.VMEM),
         scratch_shapes=[
+            pltpu.VMEM((8, slots, width), jnp.float32),
             pltpu.VMEM((8, slots, width), jnp.float32),
             pltpu.VMEM((8, slots, width), jnp.float32),
             pltpu.VMEM((7, slots, width), jnp.bfloat16),
             pltpu.VMEM((7, slots, width), jnp.bfloat16),
             pltpu.SemaphoreType.DMA((8,)),
             pltpu.SemaphoreType.DMA((8,)),
-            pltpu.SemaphoreType.DMA((8,)),
             pltpu.SemaphoreType.DMA((7,)),
             pltpu.SemaphoreType.DMA((7,)),
         ],
         compiler_params=pltpu.CompilerParams(
-            collective_id=1, has_side_effects=True, vmem_limit_bytes=56 * 1024 * 1024
+            collective_id=1, has_side_effects=True, vmem_limit_bytes=60 * 1024 * 1024
         ),
-    )(parts)
+    )(hidden, weights)
 
 
 def body(tokens, norm_gain, expert_ids, gate_weights, w_gate, w_up, w_down):
@@ -264,8 +271,7 @@
     gate_part = jnp.dot(normed, w_gate[0], preferred_element_type=jnp.float32)
     up_part = jnp.dot(normed, w_up[0], preferred_element_type=jnp.float32)
     hidden = (jax.nn.silu(gate_part) * up_part).astype(jnp.bfloat16)
-    outputs = jnp.dot(hidden, w_down[0], preferred_element_type=jnp.float32)
-    shares = scatter_cols(outputs, width)
+    shares = scatter_cols(hidden, w_down[0], width)
     shares = shares.reshape(EXPERTS, CAP, width)
     returned = lax.all_to_all(shares, "row", split_axis=0, concat_axis=0, tiled=True)
     mixed = combine_rows(returned.reshape(-1, width), slot_index, gate_weights)

time: 192 us -> 197 us (1.026)
  Pallas kernels: 104 us -> 123 us
  matrix products: 40.1 us -> 27.7 us
    pallas_call x1, Pallas kernels: 59.4 us -> 78.5 us  [scatter_cols(): pl.pallas_call(functools.partial(scatter_kernel, width), out_shape=jax.Sh...]
    dot_general x1 -> x0, matrix products: 14.3 us -> none  [body(): outputs = jnp.dot(hidden, w_down[0], preferred_element_type=jnp.float32)]
where the time goes in v7:
time: 197 us
  Pallas kernels  123 us (62%)
  matrix products  27.7 us (14%)
  blocking collectives  16.3 us (8%)
  waiting for transfers between devices  13 us (7%)
  other arithmetic  8.85 us (4%)
  local copies, waits for them, and re-layouts  4.34 us (2%)
  starting transfers between devices  3.57 us (2%)
    pallas_call x1, Pallas kernels, scatter_cols(): pl.pallas_call(functools.partial(scatter_kernel, width), out_shape=jax.Sh...  78.5 us
    pallas_call x1, Pallas kernels, gather_cols(): pl.pallas_call(functools.partial(gather_kernel, width), out_shape=jax.Sha...  44.3 us
    all_to_all x1, blocking collectives, body(): lax.all_to_all(packed, 'row', split_axis=0, concat_axis=0, tiled=True)  16.3 us
    dot_general x1, matrix products, body(): up_part = jnp.dot(normed, w_up[0], preferred_element_type=jnp.float32)  15.7 us
    all_to_all x1, waiting for transfers between devices, body(): lax.all_to_all(shares, 'row', split_axis=0, concat_axis=0, tiled=True)  13 us
    dot_general x1, matrix products, body(): gate_part = jnp.dot(normed, w_gate[0], preferred_element_type=jnp.float32)  10.7 us
    reduce_sum x1, other arithmetic, normalize(): jnp.mean(values * values, axis=-1, keepdims=True) + 1e-05  5.22 us
  transfers between devices with their start and end apart: 1, of which 1 were waited for; matrix products, arithmetic and copies ran while one was open for 0% of the time, Pallas kernels for 0%

profile of v7, /device:TPU:0, one launch (start us, length us, event | category | flops | bytes accessed | tf_op | source)
XLA Modules:
  0.0 196.7 jit_solution(9517850341563589781)
XLA Ops:
  0.0 0.8 copy.21
  0.8 0.1 eq.42
  1.0 0.1 eq.38
  1.1 1.1 reduce-window.6
  2.3 0.2 slice_reduce_fusion
  2.5 0.1 fusion.13
  2.6 0.1 reduce_sum.39
  2.8 0.1 copy.23
  2.8 0.7 compare_select_fusion
  3.5 0.3 convert_reduce_fusion
  3.8 1.3 convolution_convert_fusion
  5.1 16.3 %all_to_all.10 = bf16[8,128,256]{2,1,0:T(8,128)(2,1)} all-to-all(bf16[8,128,256]{2,1,0:T(8,128)(2,1)S(1)} %bitcast.27), channel_id=1, replica_groups=mesh['row'=8,'chip'=8,'core'=2] {'row'}, dimensions={0} | all-to-all | bytes 1048576 | tf_op jit(solution)/shard_map/all_to_all | solution.py:265
  21.4 0.0 copy-start.3
  21.4 44.3 %shard_map.73 = bf16[1024,4096]{1,0:T(8,128)(2,1)} custom-call(bf16[1024,256]{1,0:T(8,128)(2,1)} %bitcast.26), custom_call_target="tpu_custom_call" | custom-call | tf_op jit(solution)/shard_map/pallas_call | solution.py:118
  65.7 0.0 copy-start
  65.7 0.0 slice-start
  65.7 5.2 %fusion = f32[1024]{0:T(1024)S(1)} fusion(bf16[1024,4096]{1,0:T(8,128)(2,1)} %shard_map.73), kind=kLoop, calls=%fused_computation.3 | loop fusion | flops 12581888 | bytes 8392704 | tf_op jit(solution)/shard_map/reduce_sum | solution.py:19
  71.0 0.0 copy-done.3
  71.0 0.5 copy-done
  71.5 0.0 slice-start.1
  71.5 15.7 %fusion.3 = f32[1024,896]{1,0:T(8,128)S(1)} fusion(bf16[1,4096,896]{2,1,0:T(8,128)(2,1)} %param.12, bf16[1024,4096]{1,0:T(8,128)(2,1)S(1)} %copy-done, f32[4096]{0:T(1024)S(1)} %copy-done.3, f32[1024]{0:T(1024)S(1)} %add_rsqrt_fusion), kind=kOutput, calls=%fused_computation.6 | convolution fusion | flops 7532969984 | bytes 19419136 | tf_op jit(solution)/shard_map/dot_general | solution.py:272
  87.2 0.0 slice-done
  87.2 0.0 slice-done.1
  87.2 10.7 %multiply_convert_fusion.hidden = bf16[1024,896]{1,0:T(8,128)(2,1)} fusion(f32[1024,896]{1,0:T(8,128)S(1)} %fusion.3, bf16[1,4096,896]{2,1,0:T(8,128)(2,1)S(1)} %bitcast.29, bf16[1024,4096]{1,0:T(8,128)(2,1)S(1)} %copy-done, f32[4096]{0:T(1024)S(1)} %copy-done.3, f32[1024]{0:T(1024)S(1)} %add_rsqrt_fusion), kind=kOutput, calls=%fused_computation.10 | convolution fusion | flops 7538475008 | bytes 21254144 | tf_op jit(solution)/shard_map/dot_general | solution.py:271
  97.9 0.0 copy-start.2
  97.9 0.0 copy-start.1
  97.9 78.5 %shard_map.74 = f32[1024,256]{1,0:T(8,128)} custom-call(bf16[1024,896]{1,0:T(8,128)(2,1)} %multiply_convert_fusion.hidden, bf16[896,4096]{1,0:T(8,128)(2,1)} %bitcast.24), custom_call_target="tpu_custom_call" | custom-call | tf_op jit(solution)/shard_map/pallas_call | solution.py:233
  176.5 3.6 %all-to-all-start.1 = ((f32[8,128,256]{2,1,0:T(8,128)}), f32[8,128,256]{2,1,0:T(8,128)S(1)}, u32[]{:S(2)}, u32[]{:S(2)}) async-start(f32[8,128,256]{2,1,0:T(8,128)} %bitcast.25), calls=%async_computation.1 | async-start | bytes 2097152 | tf_op jit(solution)/shard_map/all_to_all | solution.py:276
  180.0 0.1 copy.24
  180.2 0.1 reshape.55
  180.3 0.0 copy-done.2
  180.3 0.1 copy.25
  180.5 13.0 %all-to-all-done.1 = f32[8,128,256]{2,1,0:T(8,128)S(1)} async-done(((f32[8,128,256]{2,1,0:T(8,128)}), f32[8,128,256]{2,1,0:T(8,128)S(1)}, u32[]{:S(2)}, u32[]{:S(2)}) %all-to-all-start.1) | async-done | bytes 1048608 | tf_op jit(solution)/shard_map/all_to_all | solution.py:276
  193.5 1.6 gather_fusion
  195.0 0.3 reshape.54
  195.3 0.7 multiply_reduce_fusion
  196.1 0.0 copy-done.1
  196.1 0.7 add_convert_fusion
  (6 shorter events, 0.1 us)
Async XLA Ops:
  21.4 49.6 %copy-start.3 = (f32[4096]{0:T(1024)S(1)}, f32[4096]{0:T(1024)}, u32[]{:S(2)}) copy-start(f32[4096]{0:T(1024)} %param.8) | copy-start | bytes 49156
  65.7 5.8 %copy-start = (bf16[1024,4096]{1,0:T(8,128)(2,1)S(1)}, bf16[1024,4096]{1,0:T(8,128)(2,1)}, u32[]{:S(2)}) copy-start(bf16[1024,4096]{1,0:T(8,128)(2,1)} %shard_map.73) | copy-start | bytes 25165828
  65.7 21.5 %slice-start = ((s8[7340032]{0:T(1024)(128)(4,1)}), s8[3145728]{0:T(1024)(128)(4,1)S(1)}, s32[]{:S(2)}) async-start(s8[7340032]{0:T(1024)(128)(4,1)} %bitcast.28), calls=%async_computation.2 | async-start | bytes 6291456
  71.5 15.7 %slice-start.1 = ((s8[7340032]{0:T(1024)(128)(4,1)}), s8[4194304]{0:T(1024)(128)(4,1)S(1)}, s32[]{:S(2)}) async-start(s8[7340032]{0:T(1024)(128)(4,1)} %bitcast.28), calls=%async_computation.3 | async-start | bytes 8388608
  97.9 82.4 %copy-start.2 = (f32[256,2]{0,1:T(2,128)S(1)}, f32[256,2]{0,1:T(2,128)}, u32[]{:S(2)}) copy-start(f32[256,2]{0,1:T(2,128)} %param.10) | copy-start | bytes 6148
  97.9 98.1 %copy-start.1 = (bf16[256,256]{1,0:T(8,128)(2,1)S(1)}, bf16[256,256]{1,0:T(8,128)(2,1)}, u32[]{:S(2)}) copy-start(bf16[256,256]{1,0:T(8,128)(2,1)} %param.7) | copy-start | bytes 393220
  176.5 17.0 %all-to-all-start.1 = ((f32[8,128,256]{2,1,0:T(8,128)}), f32[8,128,256]{2,1,0:T(8,128)S(1)}, u32[]{:S(2)}, u32[]{:S(2)}) async-start(f32[8,128,256]{2,1,0:T(8,128)} %bitcast.25), calls=%async_computation.1 | async-start | bytes 2097152 | tf_op jit(solution)/shard_map/all_to_all | solution.py:276

commit v8 on v6

--- a/solution.py
+++ b/solution.py
@@ -39,7 +39,8 @@
     return jnp.sum(picked * gate_weights[:, :, None], axis=1)
 
 
-def gather_kernel(width, src, out, send_sem, recv_sem, local_sem):
+def expert_in_kernel(width, src, gain, w_gate, w_up, hidden, xs, acc_gate, acc_up, squares,
+                     send_sem, recv_sem, local_sem):
     row, me, core = lax.axis_index("row"), lax.axis_index("chip"), lax.axis_index("core")
     side, y = me // 4, me % 4
     partner = lax.rem(me + 4, 8)
@@ -47,15 +48,17 @@
     down = side * 4 + lax.rem(y + 3, 4)
     across = side * 4 + lax.rem(y + 2, 4)
     sister = 1 - core
+    slots = xs.shape[0]
+    step = 256
 
     barrier = pltpu.get_barrier_semaphore()
     for chip, half in ((partner, core), (up, core), (down, core), (me, sister)):
         pl.semaphore_signal(barrier, inc=1, device_id=(row, chip, half), device_id_type=MESH)
     pl.semaphore_wait(barrier, 4)
 
-    def window(chip):
-        start = pl.multiple_of((chip * 2 + core) * width, width)
-        return out.at[:, pl.ds(start, width)]
+    def window(chip, half=core):
+        start = pl.multiple_of((chip * 2 + half) * width, width)
+        return xs.at[:, pl.ds(start, width)]
 
     def send(tag, origin, chip, half, source=None):
         copy = pltpu.make_async_remote_copy(
@@ -66,6 +69,37 @@
         copy.start()
         return copy
 
+    def arrive(tag, origin, half=core):
+        pltpu.make_async_remote_copy(
+            src_ref=window(origin, half), dst_ref=window(origin, half), send_sem=send_sem.at[tag],
+            recv_sem=recv_sem.at[tag], device_id=(row, me, sister), device_id_type=MESH,
+        ).wait_recv()
+
+    def absorb(origin, half=core, first=False):
+        block = origin * 2 + half
+        start = pl.multiple_of(block * width, width)
+        cols = pl.ds(start, width)
+        scale = gain[:, cols]
+
+        def one(i, carry):
+            part = pl.ds(pl.multiple_of(i * step, step), step)
+            values = xs[part, cols].astype(jnp.float32)
+            total = jnp.sum(values * values, axis=1, keepdims=True)
+            scaled = (values * scale).astype(jnp.bfloat16)
+            gate_part = jnp.dot(scaled, w_gate[cols, :], preferred_element_type=jnp.float32)
+            up_part = jnp.dot(scaled, w_up[cols, :], preferred_element_type=jnp.float32)
+            if first:
+                squares[part, :] = total
+                acc_gate[part, :] = gate_part
+                acc_up[part, :] = up_part
+            else:
+                squares[part, :] += total
+                acc_gate[part, :] += gate_part
+                acc_up[part, :] += up_part
+            return carry
+
+        lax.fori_loop(0, slots // step, one, 0)
+
     sent = [
         send(0, me, partner, core, src),
         send(1, me, up, core, src),
@@ -74,59 +108,79 @@
     ]
     local = pltpu.make_async_copy(src, window(me), local_sem)
     local.start()
-
-    def arrive(tag, origin):
-        pltpu.make_async_remote_copy(
-            src_ref=window(origin), dst_ref=window(origin), send_sem=send_sem.at[tag],
-            recv_sem=recv_sem.at[tag], device_id=(row, me, sister), device_id_type=MESH,
-        ).wait_recv()
-
-    other = lax.rem(partner, 8)
-    arrive(0, other)
-    sent += [send(3, other, up, core), send(4, other, down, core), send(8, other, me, sister)]
+    local.wait()
+    absorb(me, first=True)
+
+    arrive(0, partner)
+    sent += [send(3, partner, up, core), send(4, partner, down, core),
+             send(8, partner, me, sister)]
+    absorb(partner)
     arrive(1, down)
     sent += [send(5, down, up, core), send(9, down, me, sister)]
+    absorb(down)
     arrive(2, up)
     sent.append(send(10, up, me, sister))
-    arrive(3, lax.rem(down + 4, 8))
-    sent.append(send(11, lax.rem(down + 4, 8), me, sister))
-    arrive(4, lax.rem(up + 4, 8))
-    sent += [send(6, lax.rem(up + 4, 8), down, core), send(12, lax.rem(up + 4, 8), me, sister)]
+    absorb(up)
+    arrive(3, far(down))
+    sent.append(send(11, far(down), me, sister))
+    absorb(far(down))
+    arrive(4, far(up))
+    sent += [send(6, far(up), down, core), send(12, far(up), me, sister)]
+    absorb(far(up))
     arrive(5, across)
     sent.append(send(13, across, me, sister))
-    arrive(6, lax.rem(across + 4, 8))
-    sent.append(send(14, lax.rem(across + 4, 8), me, sister))
-    local.wait()
-
-    def sister_window(origin):
-        start = pl.multiple_of((origin * 2 + sister) * width, width)
-        return out.at[:, pl.ds(start, width)]
-
-    for tag, origin in ((7, me), (8, partner), (9, down), (10, up), (11, lax.rem(down + 4, 8)),
-                        (12, lax.rem(up + 4, 8)), (13, across), (14, lax.rem(across + 4, 8))):
-        pltpu.make_async_remote_copy(
-            src_ref=sister_window(origin), dst_ref=sister_window(origin),
-            send_sem=send_sem.at[tag], recv_sem=recv_sem.at[tag],
-            device_id=(row, me, sister), device_id_type=MESH,
-        ).wait_recv()
+    absorb(across)
+    arrive(6, far(across))
+    sent.append(send(14, far(across), me, sister))
+    absorb(far(across))
+
+    for tag, origin in ((7, me), (8, partner), (9, down), (10, up), (11, far(down)),
+                        (12, far(up)), (13, across), (14, far(across))):
+        arrive(tag, origin, sister)
+        absorb(origin, sister)
+
+    features = gain.shape[1]
+
+    def finish(i, carry):
+        part = pl.ds(pl.multiple_of(i * step, step), step)
+        inverse_norm = lax.rsqrt(squares[part, :] / features + 1e-05)
+        gate_values = acc_gate[part, :] * inverse_norm
+        up_values = acc_up[part, :] * inverse_norm
+        silu = gate_values / (1.0 + jnp.exp(-gate_values))
+        hidden[part, :] = (silu * up_values).astype(hidden.dtype)
+        return carry
+
+    lax.fori_loop(0, slots // step, finish, 0)
     for copy in sent:
         copy.wait_send()
 
 
-def gather_cols(block, chips):
+def far(chip):
+    return lax.rem(chip + 4, 8)
+
+
+def expert_in(block, norm_gain, w_gate, w_up, chips):
     slots, width = block.shape
+    features = chips * 2 * width
+    hidden_units = w_gate.shape[1]
     return pl.pallas_call(
-        functools.partial(gather_kernel, width),
-        out_shape=jax.ShapeDtypeStruct((slots, chips * 2 * width), block.dtype),
-        in_specs=[pl.BlockSpec(memory_space=pl.ANY)],
-        out_specs=pl.BlockSpec(memory_space=pl.ANY),
+        functools.partial(expert_in_kernel, width),
+        out_shape=jax.ShapeDtypeStruct((slots, hidden_units), jnp.bfloat16),
+        in_specs=[pl.BlockSpec(memory_space=pltpu.VMEM)] * 4,
+        out_specs=pl.BlockSpec(memory_space=pltpu.VMEM),
         scratch_shapes=[
+            pltpu.VMEM((slots, features), jnp.bfloat16),
+            pltpu.VMEM((slots, hidden_units), jnp.float32),
+            pltpu.VMEM((slots, hidden_units), jnp.float32),
+            pltpu.VMEM((slots, 1), jnp.float32),
             pltpu.SemaphoreType.DMA((15,)),
             pltpu.SemaphoreType.DMA((15,)),
             pltpu.SemaphoreType.DMA(()),
         ],
-        compiler_params=pltpu.CompilerParams(collective_id=0, has_side_effects=True),
-    )(block)
+        compiler_params=pltpu.CompilerParams(
+            collective_id=0, has_side_effects=True, vmem_limit_bytes=60 * 1024 * 1024
+        ),
+    )(block, norm_gain.reshape(1, features), w_gate, w_up)
 
 
 def add_blocks(dst, *sources):
@@ -259,11 +313,7 @@
     arrived = arrived.reshape(EXPERTS * CAP, width)
     slots = arrived.shape[0]
 
-    widened = gather_cols(arrived, chips)
-    normed = normalize(widened, norm_gain)
-    gate_part = jnp.dot(normed, w_gate[0], preferred_element_type=jnp.float32)
-    up_part = jnp.dot(normed, w_up[0], preferred_element_type=jnp.float32)
-    hidden = (jax.nn.silu(gate_part) * up_part).astype(jnp.bfloat16)
+    hidden = expert_in(arrived, norm_gain, w_gate[0], w_up[0], chips)
     outputs = jnp.dot(hidden, w_down[0], preferred_element_type=jnp.float32)
     shares = scatter_cols(outputs, width)
     shares = shares.reshape(EXPERTS, CAP, width)

time: 192 us -> 184 us (0.958)
  matrix products: 40.1 us -> 16.1 us
  Pallas kernels: 104 us -> 125 us
  other arithmetic: 8.85 us -> 3.62 us
    dot_general x2 -> x0, matrix products: 24.6 us -> none  [the longest x1 15.4 us: body(): up_part = jnp.dot(normed, w_up[0], preferred_element_type=jnp.float32)]
    pallas_call x1, Pallas kernels: 44.3 us -> 67 us  [expert_in(): pl.pallas_call(functools.partial(expert_in_kernel, width), out_shape=jax....]
    reduce_sum x1 -> x0, other arithmetic: 5.22 us -> none  [normalize(): jnp.mean(values * values, axis=-1, keepdims=True) + 1e-05]
where the time goes in v8:
time: 184 us; the launch traced here: 183 us
  Pallas kernels  125 us (68%)
  blocking collectives  16.3 us (9%)
  matrix products  16.1 us (9%)
  waiting for transfers between devices  14.5 us (8%)
  local copies, waits for them, and re-layouts  3.82 us (2%)
  starting transfers between devices  3.7 us (2%)
  other arithmetic  3.62 us (2%)
    pallas_call x1, Pallas kernels, expert_in(): pl.pallas_call(functools.partial(expert_in_kernel, width), out_shape=jax....  67 us
    pallas_call x1, Pallas kernels, scatter_cols(): pl.pallas_call(functools.partial(scatter_kernel, width), out_shape=jax.Sh...  57.9 us
    all_to_all x1, blocking collectives, body(): lax.all_to_all(packed, 'row', split_axis=0, concat_axis=0, tiled=True)  16.3 us
    dot_general x1, matrix products, body(): outputs = jnp.dot(hidden, w_down[0], preferred_element_type=jnp.float32)  14.8 us
    all_to_all x1, waiting for transfers between devices, body(): lax.all_to_all(shares, 'row', split_axis=0, concat_axis=0, tiled=True)  14.5 us
    all_to_all x1, starting transfers between devices, body(): lax.all_to_all(shares, 'row', split_axis=0, concat_axis=0, tiled=True)  3.7 us
  transfers between devices with their start and end apart: 1, of which 1 were waited for; matrix products, arithmetic and copies ran while one was open for 0% of the time, Pallas kernels for 0%

profile of v8, /device:TPU:0, one launch (start us, length us, event | category | flops | bytes accessed | tf_op | source)
XLA Modules:
  0.0 183.0 jit_solution(11673396542472050260)
XLA Ops:
  0.0 0.8 copy.21
  0.8 0.1 eq.42
  1.0 0.1 eq.38
  1.1 1.1 reduce-window.6
  2.3 0.2 slice_reduce_fusion
  2.5 0.1 fusion.4
  2.6 0.1 reduce_sum.30
  2.8 0.1 copy.23
  2.8 0.7 compare_select_fusion
  3.5 0.3 convert_reduce_fusion
  3.8 1.3 convolution_convert_fusion
  5.1 16.3 %all_to_all.10 = bf16[8,128,256]{2,1,0:T(8,128)(2,1)} all-to-all(bf16[8,128,256]{2,1,0:T(8,128)(2,1)S(1)} %bitcast.26), channel_id=1, replica_groups=mesh['row'=8,'chip'=8,'core'=2] {'row'}, dimensions={0} | all-to-all | bytes 1048576 | tf_op jit(solution)/shard_map/all_to_all | solution.py:312
  21.4 67.0 %shard_map.73 = bf16[1024,896]{1,0:T(8,128)(2,1)} custom-call(bf16[1024,256]{1,0:T(8,128)(2,1)} %bitcast.25, f32[1,4096]{1,0:T(1,128)} %bitcast.27, bf16[4096,896]{1,0:T(8,128)(2,1)} %bitcast.22, bf16[4096,896]{1,0:T(8,128)(2,1)} %bitcast.23), custom_call_target="tpu_custom_call" | custom-call | tf_op jit(solution)/shard_map/pallas_call | solution.py:166
  88.3 14.8 %fusion.parts = f32[1024,4096]{1,0:T(8,128)} fusion(bf16[1024,896]{1,0:T(8,128)(2,1)} %shard_map.73, bf16[1,896,4096]{2,1,0:T(8,128)(2,1)} %param.13), kind=kOutput, calls=%fused_computation.1 | convolution fusion | flops 7516192768 | bytes 25952256 | tf_op jit(solution)/shard_map/dot_general | solution.py:317
  103.2 0.0 copy-start.1
  103.2 57.9 %shard_map.74 = f32[1024,256]{1,0:T(8,128)} custom-call(f32[1024,4096]{1,0:T(8,128)} %fusion.parts), custom_call_target="tpu_custom_call" | custom-call | tf_op jit(solution)/shard_map/pallas_call | solution.py:280
  161.1 0.0 copy-start
  161.1 3.7 %all-to-all-start.1 = ((f32[8,128,256]{2,1,0:T(8,128)}), f32[8,128,256]{2,1,0:T(8,128)S(1)}, u32[]{:S(2)}, u32[]{:S(2)}) async-start(f32[8,128,256]{2,1,0:T(8,128)} %bitcast.24), calls=%async_computation.1 | async-start | bytes 2097152 | tf_op jit(solution)/shard_map/all_to_all | solution.py:320
  164.8 0.1 copy.24
  164.9 0.1 reshape.50
  165.1 0.0 copy-done.1
  165.1 0.1 copy.25
  165.2 14.5 %all-to-all-done.1 = f32[8,128,256]{2,1,0:T(8,128)S(1)} async-done(((f32[8,128,256]{2,1,0:T(8,128)}), f32[8,128,256]{2,1,0:T(8,128)S(1)}, u32[]{:S(2)}, u32[]{:S(2)}) %all-to-all-start.1) | async-done | bytes 1048608 | tf_op jit(solution)/shard_map/all_to_all | solution.py:320
  179.7 1.6 gather_fusion
  181.3 0.3 reshape.49
  181.6 0.7 multiply_reduce_fusion
  182.3 0.0 copy-done
  182.3 0.7 add_convert_fusion
  (4 shorter events, 0.0 us)
Async XLA Ops:
  103.2 61.9 %copy-start.1 = (f32[256,2]{0,1:T(2,128)S(1)}, f32[256,2]{0,1:T(2,128)}, u32[]{:S(2)}) copy-start(f32[256,2]{0,1:T(2,128)} %param.10) | copy-start | bytes 6148
  161.1 21.3 %copy-start = (bf16[256,256]{1,0:T(8,128)(2,1)S(1)}, bf16[256,256]{1,0:T(8,128)(2,1)}, u32[]{:S(2)}) copy-start(bf16[256,256]{1,0:T(8,128)(2,1)} %param.7) | copy-start | bytes 393220
  161.1 18.7 %all-to-all-start.1 = ((f32[8,128,256]{2,1,0:T(8,128)}), f32[8,128,256]{2,1,0:T(8,128)S(1)}, u32[]{:S(2)}, u32[]{:S(2)}) async-start(f32[8,128,256]{2,1,0:T(8,128)} %bitcast.24), calls=%async_computation.1 | async-start | bytes 2097152 | tf_op jit(solution)/shard_map/all_to_all | solution.py:320

commit v9 on v8

--- a/solution.py
+++ b/solution.py
@@ -39,8 +39,9 @@
     return jnp.sum(picked * gate_weights[:, :, None], axis=1)
 
 
-def expert_in_kernel(width, src, gain, w_gate, w_up, hidden, xs, acc_gate, acc_up, squares,
-                     send_sem, recv_sem, local_sem):
+def expert_in_kernel(width, src, squares_part, gain, w_gate_hbm, w_up_hbm, hidden, xs, w_gate,
+                     w_up, acc_gate, acc_up, squares, send_sem, recv_sem, local_sem, weight_sem,
+                     square_send, square_recv):
     row, me, core = lax.axis_index("row"), lax.axis_index("chip"), lax.axis_index("core")
     side, y = me // 4, me % 4
     partner = lax.rem(me + 4, 8)
@@ -50,11 +51,31 @@
     sister = 1 - core
     slots = xs.shape[0]
     step = 256
+    blocks = squares.shape[0]
+    mine = me * 2 + core
+
+    loads = [pltpu.make_async_copy(w_gate_hbm, w_gate, weight_sem.at[0]),
+             pltpu.make_async_copy(w_up_hbm, w_up, weight_sem.at[1])]
+    for load in loads:
+        load.start()
 
     barrier = pltpu.get_barrier_semaphore()
-    for chip, half in ((partner, core), (up, core), (down, core), (me, sister)):
-        pl.semaphore_signal(barrier, inc=1, device_id=(row, chip, half), device_id_type=MESH)
-    pl.semaphore_wait(barrier, 4)
+    for d in range(1, blocks):
+        other = lax.rem(mine + d, blocks)
+        pl.semaphore_signal(barrier, inc=1, device_id=(row, other // 2, other % 2),
+                            device_id_type=MESH)
+    pl.semaphore_wait(barrier, blocks - 1)
+
+    square_copies = []
+    for d in range(1, blocks):
+        other = lax.rem(mine + d, blocks)
+        copy = pltpu.make_async_remote_copy(
+            src_ref=squares_part, dst_ref=squares.at[mine], send_sem=square_send.at[d],
+            recv_sem=square_recv.at[d], device_id=(row, other // 2, other % 2),
+            device_id_type=MESH,
+        )
+        copy.start()
+        square_copies.append(copy)
 
     def window(chip, half=core):
         start = pl.multiple_of((chip * 2 + half) * width, width)
@@ -75,31 +96,6 @@
             recv_sem=recv_sem.at[tag], device_id=(row, me, sister), device_id_type=MESH,
         ).wait_recv()
 
-    def absorb(origin, half=core, first=False):
-        block = origin * 2 + half
-        start = pl.multiple_of(block * width, width)
-        cols = pl.ds(start, width)
-        scale = gain[:, cols]
-
-        def one(i, carry):
-            part = pl.ds(pl.multiple_of(i * step, step), step)
-            values = xs[part, cols].astype(jnp.float32)
-            total = jnp.sum(values * values, axis=1, keepdims=True)
-            scaled = (values * scale).astype(jnp.bfloat16)
-            gate_part = jnp.dot(scaled, w_gate[cols, :], preferred_element_type=jnp.float32)
-            up_part = jnp.dot(scaled, w_up[cols, :], preferred_element_type=jnp.float32)
-            if first:
-                squares[part, :] = total
-                acc_gate[part, :] = gate_part
-                acc_up[part, :] = up_part
-            else:
-                squares[part, :] += total
-                acc_gate[part, :] += gate_part
-                acc_up[part, :] += up_part
-            return carry
-
-        lax.fori_loop(0, slots // step, one, 0)
-
     sent = [
         send(0, me, partner, core, src),
         send(1, me, up, core, src),
@@ -108,9 +104,43 @@
     ]
     local = pltpu.make_async_copy(src, window(me), local_sem)
     local.start()
+    squares[mine] = squares_part[...]
+    for copy in square_copies:
+        copy.wait_recv()
+    total = squares[0]
+    for b in range(1, blocks):
+        total = total + squares[b]
+    inverse_norm = lax.rsqrt(total / (blocks * width) + 1e-05)
+    squares[0] = inverse_norm
+    for load in loads:
+        load.wait()
     local.wait()
+
+    def absorb(origin, half=core, first=False):
+        block = origin * 2 + half
+        start = pl.multiple_of(block * width, width)
+        cols = pl.ds(start, width)
+        scale = gain[:, cols]
+
+        def one(i, carry):
+            part = pl.ds(pl.multiple_of(i * step, step), step)
+            spread = jnp.broadcast_to(squares[0, pl.ds(i, 1), :], (128, step))
+            column = jnp.transpose(spread)[:, 0:1]
+            values = xs[part, cols].astype(jnp.float32)
+            normed = (values * column * scale).astype(jnp.bfloat16)
+            gate_part = jnp.dot(normed, w_gate[cols, :], preferred_element_type=jnp.float32)
+            up_part = jnp.dot(normed, w_up[cols, :], preferred_element_type=jnp.float32)
+            if first:
+                acc_gate[part, :] = gate_part
+                acc_up[part, :] = up_part
+            else:
+                acc_gate[part, :] += gate_part
+                acc_up[part, :] += up_part
+            return carry
+
+        lax.fori_loop(0, slots // step, one, 0)
+
     absorb(me, first=True)
-
     arrive(0, partner)
     sent += [send(3, partner, up, core), send(4, partner, down, core),
              send(8, partner, me, sister)]
@@ -139,19 +169,15 @@
         arrive(tag, origin, sister)
         absorb(origin, sister)
 
-    features = gain.shape[1]
-
     def finish(i, carry):
         part = pl.ds(pl.multiple_of(i * step, step), step)
-        inverse_norm = lax.rsqrt(squares[part, :] / features + 1e-05)
-        gate_values = acc_gate[part, :] * inverse_norm
-        up_values = acc_up[part, :] * inverse_norm
+        gate_values = acc_gate[part, :]
         silu = gate_values / (1.0 + jnp.exp(-gate_values))
-        hidden[part, :] = (silu * up_values).astype(hidden.dtype)
+        hidden[part, :] = (silu * acc_up[part, :]).astype(hidden.dtype)
         return carry
 
     lax.fori_loop(0, slots // step, finish, 0)
-    for copy in sent:
+    for copy in sent + square_copies:
         copy.wait_send()
 
 
@@ -161,26 +187,35 @@
 
 def expert_in(block, norm_gain, w_gate, w_up, chips):
     slots, width = block.shape
-    features = chips * 2 * width
+    blocks = chips * 2
+    features = blocks * width
     hidden_units = w_gate.shape[1]
+    values = block.astype(jnp.float32)
+    squares_part = jnp.sum(values * values, axis=1).reshape(slots // 256, 256)
     return pl.pallas_call(
         functools.partial(expert_in_kernel, width),
         out_shape=jax.ShapeDtypeStruct((slots, hidden_units), jnp.bfloat16),
-        in_specs=[pl.BlockSpec(memory_space=pltpu.VMEM)] * 4,
+        in_specs=[pl.BlockSpec(memory_space=pltpu.VMEM)] * 3
+        + [pl.BlockSpec(memory_space=pl.ANY)] * 2,
         out_specs=pl.BlockSpec(memory_space=pltpu.VMEM),
         scratch_shapes=[
             pltpu.VMEM((slots, features), jnp.bfloat16),
+            pltpu.VMEM(w_gate.shape, w_gate.dtype),
+            pltpu.VMEM(w_up.shape, w_up.dtype),
             pltpu.VMEM((slots, hidden_units), jnp.float32),
             pltpu.VMEM((slots, hidden_units), jnp.float32),
-            pltpu.VMEM((slots, 1), jnp.float32),
+            pltpu.VMEM((blocks, slots // 256, 256), jnp.float32),
             pltpu.SemaphoreType.DMA((15,)),
             pltpu.SemaphoreType.DMA((15,)),
             pltpu.SemaphoreType.DMA(()),
+            pltpu.SemaphoreType.DMA((2,)),
+            pltpu.SemaphoreType.DMA((blocks,)),
+            pltpu.SemaphoreType.DMA((blocks,)),
         ],
         compiler_params=pltpu.CompilerParams(
             collective_id=0, has_side_effects=True, vmem_limit_bytes=60 * 1024 * 1024
         ),
-    )(block, norm_gain.reshape(1, features), w_gate, w_up)
+    )(block, squares_part, norm_gain.reshape(1, features), w_gate, w_up)
 
 
 def add_blocks(dst, *sources):

time: 184 us -> 195 us (1.060)
  Pallas kernels: 125 us -> 134 us
    pallas_call x1, Pallas kernels: 67 us -> 73.8 us  [expert_in(): pl.pallas_call(functools.partial(expert_in_kernel, width), out_shape=jax....]
    pallas_call x1, Pallas kernels: 57.9 us -> 59.8 us  [scatter_cols(): pl.pallas_call(functools.partial(scatter_kernel, width), out_shape=jax.Sh...]
where the time goes in v9:
time: 195 us; the launch traced here: 193 us
  Pallas kernels  134 us (69%)
  blocking collectives  16.2 us (8%)
  matrix products  16.1 us (8%)
  waiting for transfers between devices  14.5 us (7%)
  local copies, waits for them, and re-layouts  4.43 us (2%)
  other arithmetic  3.83 us (2%)
  starting transfers between devices  3.7 us (2%)
    pallas_call x1, Pallas kernels, expert_in(): pl.pallas_call(functools.partial(expert_in_kernel, width), out_shape=jax....  73.8 us
    pallas_call x1, Pallas kernels, scatter_cols(): pl.pallas_call(functools.partial(scatter_kernel, width), out_shape=jax.Sh...  59.8 us
    all_to_all x1, blocking collectives, body(): lax.all_to_all(packed, 'row', split_axis=0, concat_axis=0, tiled=True)  16.2 us
    dot_general x1, matrix products, body(): outputs = jnp.dot(hidden, w_down[0], preferred_element_type=jnp.float32)  14.8 us
    all_to_all x1, waiting for transfers between devices, body(): lax.all_to_all(shares, 'row', split_axis=0, concat_axis=0, tiled=True)  14.5 us
  transfers between devices with their start and end apart: 1, of which 1 were waited for; matrix products, arithmetic and copies ran while one was open for 0% of the time, Pallas kernels for 0%

profile of v9, /device:TPU:0, one launch (start us, length us, event | category | flops | bytes accessed | tf_op | source)
XLA Modules:
  0.0 192.5 jit_solution(17218833846681397186)
XLA Ops:
  0.0 0.8 copy.21
  0.8 0.1 eq.42
  1.0 0.1 eq.38
  1.1 1.1 reduce-window.6
  2.3 0.2 slice_reduce_fusion
  2.5 0.1 fusion.4
  2.6 0.1 reduce_sum.39
  2.8 0.1 copy.23
  2.8 0.7 compare_select_fusion
  3.5 0.3 convert_reduce_fusion
  3.8 1.3 convolution_convert_fusion
  5.1 16.2 %all_to_all.10 = bf16[8,128,256]{2,1,0:T(8,128)(2,1)S(1)} all-to-all(bf16[8,128,256]{2,1,0:T(8,128)(2,1)S(1)} %bitcast.26), channel_id=1, replica_groups=mesh['row'=8,'chip'=8,'core'=2] {'row'}, dimensions={0} | all-to-all | bytes 1048576 | tf_op jit(solution)/shard_map/all_to_all | solution.py:347
  21.3 0.0 copy-start
  21.3 0.2 multiply_reduce_fusion
  21.5 0.6 reshape.50.squares_part
  22.1 0.0 copy-done
  22.1 73.8 %shard_map.73 = bf16[1024,896]{1,0:T(8,128)(2,1)} custom-call(bf16[1024,256]{1,0:T(8,128)(2,1)} %bitcast.24, f32[4,256]{1,0:T(4,128)} %reshape.50.squares_part, f32[1,4096]{1,0:T(1,128)} %bitcast.27, bf16[4096,896]{1,0:T(8,128)(2,1)} %bitcast.22, bf16[4096,896]{1,0:T(8,128)(2,1)} %bitcast.23), custom_call_target="tpu_custom_call" | custom-call | tf_op jit(solution)/shard_map/pallas_call | solution.py:195
  95.9 14.8 %fusion.parts = f32[1024,4096]{1,0:T(8,128)} fusion(bf16[1024,896]{1,0:T(8,128)(2,1)} %shard_map.73, bf16[1,896,4096]{2,1,0:T(8,128)(2,1)} %param.13), kind=kOutput, calls=%fused_computation.1 | convolution fusion | flops 7516192768 | bytes 25952256 | tf_op jit(solution)/shard_map/dot_general | solution.py:352
  110.7 0.0 copy-start.2
  110.7 59.8 %shard_map.74 = f32[1024,256]{1,0:T(8,128)} custom-call(f32[1024,4096]{1,0:T(8,128)} %fusion.parts), custom_call_target="tpu_custom_call" | custom-call | tf_op jit(solution)/shard_map/pallas_call | solution.py:315
  170.6 0.0 copy-start.1
  170.6 3.7 %all-to-all-start.1 = ((f32[8,128,256]{2,1,0:T(8,128)}), f32[8,128,256]{2,1,0:T(8,128)S(1)}, u32[]{:S(2)}, u32[]{:S(2)}) async-start(f32[8,128,256]{2,1,0:T(8,128)} %bitcast.25), calls=%async_computation.1 | async-start | bytes 2097152 | tf_op jit(solution)/shard_map/all_to_all | solution.py:355
  174.3 0.1 copy.24
  174.4 0.1 reshape.56
  174.6 0.0 copy-done.2
  174.6 0.1 copy.25
  174.7 14.5 %all-to-all-done.1 = f32[8,128,256]{2,1,0:T(8,128)S(1)} async-done(((f32[8,128,256]{2,1,0:T(8,128)}), f32[8,128,256]{2,1,0:T(8,128)S(1)}, u32[]{:S(2)}, u32[]{:S(2)}) %all-to-all-start.1) | async-done | bytes 1048608 | tf_op jit(solution)/shard_map/all_to_all | solution.py:355
  189.3 1.6 gather_fusion
  190.8 0.3 reshape.55
  191.1 0.7 multiply_reduce_fusion.1
  191.8 0.0 copy-done.1
  191.9 0.7 add_convert_fusion
  (4 shorter events, 0.1 us)
Async XLA Ops:
  21.3 0.8 copy-start
  110.7 63.8 %copy-start.2 = (f32[256,2]{0,1:T(2,128)S(1)}, f32[256,2]{0,1:T(2,128)}, u32[]{:S(2)}) copy-start(f32[256,2]{0,1:T(2,128)} %param.10) | copy-start | bytes 6148
  170.6 21.3 %copy-start.1 = (bf16[256,256]{1,0:T(8,128)(2,1)S(1)}, bf16[256,256]{1,0:T(8,128)(2,1)}, u32[]{:S(2)}) copy-start(bf16[256,256]{1,0:T(8,128)(2,1)} %param.7) | copy-start | bytes 393220
  170.6 18.7 %all-to-all-start.1 = ((f32[8,128,256]{2,1,0:T(8,128)}), f32[8,128,256]{2,1,0:T(8,128)S(1)}, u32[]{:S(2)}, u32[]{:S(2)}) async-start(f32[8,128,256]{2,1,0:T(8,128)} %bitcast.25), calls=%async_computation.1 | async-start | bytes 2097152 | tf_op jit(solution)/shard_map/all_to_all | solution.py:355

commit v10 on v9

--- a/solution.py
+++ b/solution.py
@@ -144,25 +144,22 @@
     arrive(0, partner)
     sent += [send(3, partner, up, core), send(4, partner, down, core),
              send(8, partner, me, sister)]
-    absorb(partner)
     arrive(1, down)
     sent += [send(5, down, up, core), send(9, down, me, sister)]
-    absorb(down)
     arrive(2, up)
     sent.append(send(10, up, me, sister))
-    absorb(up)
+    absorb(partner)
     arrive(3, far(down))
     sent.append(send(11, far(down), me, sister))
-    absorb(far(down))
     arrive(4, far(up))
     sent += [send(6, far(up), down, core), send(12, far(up), me, sister)]
-    absorb(far(up))
+    absorb(down)
     arrive(5, across)
     sent.append(send(13, across, me, sister))
-    absorb(across)
     arrive(6, far(across))
     sent.append(send(14, far(across), me, sister))
-    absorb(far(across))
+    for origin in (up, far(down), far(up), across, far(across)):
+        absorb(origin)
 
     for tag, origin in ((7, me), (8, partner), (9, down), (10, up), (11, far(down)),
                         (12, far(up)), (13, across), (14, far(across))):

time: 195 us -> 202 us (1.036); the launches traced: 193 us -> 202 us
  Pallas kernels: 134 us -> 143 us
    pallas_call x1, Pallas kernels: 73.8 us -> 81.5 us  [expert_in(): pl.pallas_call(functools.partial(expert_in_kernel, width), out_shape=jax....]
    pallas_call x1, Pallas kernels: 59.8 us -> 61.9 us  [scatter_cols(): pl.pallas_call(functools.partial(scatter_kernel, width), out_shape=jax.Sh...]
where the time goes in v10:
time: 202 us
  Pallas kernels  143 us (71%)
  blocking collectives  16.2 us (8%)
  matrix products  16.1 us (8%)
  waiting for transfers between devices  14 us (7%)
  local copies, waits for them, and re-layouts  4.43 us (2%)
  other arithmetic  3.83 us (2%)
  starting transfers between devices  3.7 us (2%)
    pallas_call x1, Pallas kernels, expert_in(): pl.pallas_call(functools.partial(expert_in_kernel, width), out_shape=jax....  81.5 us
    pallas_call x1, Pallas kernels, scatter_cols(): pl.pallas_call(functools.partial(scatter_kernel, width), out_shape=jax.Sh...  61.9 us
    all_to_all x1, blocking collectives, body(): lax.all_to_all(packed, 'row', split_axis=0, concat_axis=0, tiled=True)  16.2 us
    dot_general x1, matrix products, body(): outputs = jnp.dot(hidden, w_down[0], preferred_element_type=jnp.float32)  14.8 us
    all_to_all x1, waiting for transfers between devices, body(): lax.all_to_all(shares, 'row', split_axis=0, concat_axis=0, tiled=True)  14 us
  transfers between devices with their start and end apart: 1, of which 1 were waited for; matrix products, arithmetic and copies ran while one was open for 0% of the time, Pallas kernels for 0%

profile of v10, /device:TPU:0, one launch (start us, length us, event | category | flops | bytes accessed | tf_op | source)
XLA Modules:
  0.0 201.8 jit_solution(8046679461526794898)
XLA Ops:
  0.0 0.8 copy.21
  0.8 0.1 eq.42
  1.0 0.1 eq.38
  1.1 1.1 reduce-window.6
  2.3 0.2 slice_reduce_fusion
  2.5 0.1 fusion.4
  2.6 0.1 reduce_sum.39
  2.8 0.1 copy.23
  2.8 0.7 compare_select_fusion
  3.5 0.3 convert_reduce_fusion
  3.8 1.3 convolution_convert_fusion
  5.1 16.2 %all_to_all.10 = bf16[8,128,256]{2,1,0:T(8,128)(2,1)S(1)} all-to-all(bf16[8,128,256]{2,1,0:T(8,128)(2,1)S(1)} %bitcast.26), channel_id=1, replica_groups=mesh['row'=8,'chip'=8,'core'=2] {'row'}, dimensions={0} | all-to-all | bytes 1048576 | tf_op jit(solution)/shard_map/all_to_all | solution.py:344
  21.3 0.0 copy-start
  21.3 0.2 multiply_reduce_fusion
  21.5 0.6 reshape.50.squares_part
  22.1 0.0 copy-done
  22.1 81.5 %shard_map.73 = bf16[1024,896]{1,0:T(8,128)(2,1)} custom-call(bf16[1024,256]{1,0:T(8,128)(2,1)} %bitcast.24, f32[4,256]{1,0:T(4,128)} %reshape.50.squares_part, f32[1,4096]{1,0:T(1,128)} %bitcast.27, bf16[4096,896]{1,0:T(8,128)(2,1)} %bitcast.22, bf16[4096,896]{1,0:T(8,128)(2,1)} %bitcast.23), custom_call_target="tpu_custom_call" | custom-call | tf_op jit(solution)/shard_map/pallas_call | solution.py:192
  103.6 14.8 %fusion.parts = f32[1024,4096]{1,0:T(8,128)} fusion(bf16[1024,896]{1,0:T(8,128)(2,1)} %shard_map.73, bf16[1,896,4096]{2,1,0:T(8,128)(2,1)} %param.13), kind=kOutput, calls=%fused_computation.1 | convolution fusion | flops 7516192768 | bytes 25952256 | tf_op jit(solution)/shard_map/dot_general | solution.py:349
  118.5 0.0 copy-start.2
  118.5 61.9 %shard_map.74 = f32[1024,256]{1,0:T(8,128)} custom-call(f32[1024,4096]{1,0:T(8,128)} %fusion.parts), custom_call_target="tpu_custom_call" | custom-call | tf_op jit(solution)/shard_map/pallas_call | solution.py:312
  180.4 0.0 copy-start.1
  180.4 3.7 %all-to-all-start.1 = ((f32[8,128,256]{2,1,0:T(8,128)}), f32[8,128,256]{2,1,0:T(8,128)S(1)}, u32[]{:S(2)}, u32[]{:S(2)}) async-start(f32[8,128,256]{2,1,0:T(8,128)} %bitcast.25), calls=%async_computation.1 | async-start | bytes 2097152 | tf_op jit(solution)/shard_map/all_to_all | solution.py:352
  184.1 0.1 copy.24
  184.3 0.1 reshape.56
  184.4 0.0 copy-done.2
  184.4 0.1 copy.25
  184.6 14.0 %all-to-all-done.1 = f32[8,128,256]{2,1,0:T(8,128)S(1)} async-done(((f32[8,128,256]{2,1,0:T(8,128)}), f32[8,128,256]{2,1,0:T(8,128)S(1)}, u32[]{:S(2)}, u32[]{:S(2)}) %all-to-all-start.1) | async-done | bytes 1048608 | tf_op jit(solution)/shard_map/all_to_all | solution.py:352
  198.5 1.6 gather_fusion
  200.1 0.3 reshape.55
  200.4 0.7 multiply_reduce_fusion.1
  201.1 0.0 copy-done.1
  201.2 0.7 add_convert_fusion
  (4 shorter events, 0.0 us)
Async XLA Ops:
  21.3 0.8 copy-start
  118.5 65.9 %copy-start.2 = (f32[256,2]{0,1:T(2,128)S(1)}, f32[256,2]{0,1:T(2,128)}, u32[]{:S(2)}) copy-start(f32[256,2]{0,1:T(2,128)} %param.10) | copy-start | bytes 6148
  180.4 20.7 %copy-start.1 = (bf16[256,256]{1,0:T(8,128)(2,1)S(1)}, bf16[256,256]{1,0:T(8,128)(2,1)}, u32[]{:S(2)}) copy-start(bf16[256,256]{1,0:T(8,128)(2,1)} %param.7) | copy-start | bytes 393220
  180.4 18.1 %all-to-all-start.1 = ((f32[8,128,256]{2,1,0:T(8,128)}), f32[8,128,256]{2,1,0:T(8,128)S(1)}, u32[]{:S(2)}, u32[]{:S(2)}) async-start(f32[8,128,256]{2,1,0:T(8,128)} %bitcast.25), calls=%async_computation.1 | async-start | bytes 2097152 | tf_op jit(solution)/shard_map/all_to_all | solution.py:352

commit v11 on v10

--- a/solution.py
+++ b/solution.py
@@ -39,9 +39,9 @@
     return jnp.sum(picked * gate_weights[:, :, None], axis=1)
 
 
-def expert_in_kernel(width, src, squares_part, gain, w_gate_hbm, w_up_hbm, hidden, xs, w_gate,
-                     w_up, acc_gate, acc_up, squares, send_sem, recv_sem, local_sem, weight_sem,
-                     square_send, square_recv):
+def expert_in_kernel(width, src, squares_part, gain_in, w_gate_hbm, w_up_hbm, hidden, xs, w_gate,
+                     w_up, gain, acc_gate, acc_up, squares, send_sem, recv_sem, local_sem,
+                     weight_sem, square_send, square_recv):
     row, me, core = lax.axis_index("row"), lax.axis_index("chip"), lax.axis_index("core")
     side, y = me // 4, me % 4
     partner = lax.rem(me + 4, 8)
@@ -53,11 +53,19 @@
     step = 256
     blocks = squares.shape[0]
     mine = me * 2 + core
-
-    loads = [pltpu.make_async_copy(w_gate_hbm, w_gate, weight_sem.at[0]),
-             pltpu.make_async_copy(w_up_hbm, w_up, weight_sem.at[1])]
-    for load in loads:
-        load.start()
+    chips = (me, partner, down, up, far(down), far(up), across, far(across))
+    features = [(chip * 2 + core) * width for chip in chips]
+    features += [(chip * 2 + sister) * width for chip in chips]
+
+    loads = []
+    for place, start in enumerate(features):
+        rows = pl.ds(pl.multiple_of(start, width), width)
+        for index, (source, target) in enumerate(((w_gate_hbm, w_gate), (w_up_hbm, w_up))):
+            load = pltpu.make_async_copy(source.at[rows, :], target.at[pl.ds(place * width, width), :],
+                                         weight_sem.at[index, place])
+            load.start()
+            loads.append(load)
+        gain[:, pl.ds(place * width, width)] = gain_in[:, rows]
 
     barrier = pltpu.get_barrier_semaphore()
     for d in range(1, blocks):
@@ -77,32 +85,30 @@
         copy.start()
         square_copies.append(copy)
 
-    def window(chip, half=core):
-        start = pl.multiple_of((chip * 2 + half) * width, width)
-        return xs.at[:, pl.ds(start, width)]
-
-    def send(tag, origin, chip, half, source=None):
+    def place(p):
+        return xs.at[:, pl.ds(p * width, width)]
+
+    def send(tag, source, target, chip, half):
         copy = pltpu.make_async_remote_copy(
-            src_ref=window(origin) if source is None else source, dst_ref=window(origin),
-            send_sem=send_sem.at[tag], recv_sem=recv_sem.at[tag],
-            device_id=(row, chip, half), device_id_type=MESH,
+            src_ref=source, dst_ref=place(target), send_sem=send_sem.at[tag],
+            recv_sem=recv_sem.at[tag], device_id=(row, chip, half), device_id_type=MESH,
         )
         copy.start()
         return copy
 
-    def arrive(tag, origin, half=core):
+    def arrive(tag, target):
         pltpu.make_async_remote_copy(
-            src_ref=window(origin, half), dst_ref=window(origin, half), send_sem=send_sem.at[tag],
+            src_ref=place(target), dst_ref=place(target), send_sem=send_sem.at[tag],
             recv_sem=recv_sem.at[tag], device_id=(row, me, sister), device_id_type=MESH,
         ).wait_recv()
 
     sent = [
-        send(0, me, partner, core, src),
-        send(1, me, up, core, src),
-        send(2, me, down, core, src),
-        send(7, me, me, sister, src),
+        send(0, src, 1, partner, core),
+        send(1, src, 2, up, core),
+        send(2, src, 3, down, core),
+        send(7, src, 8, me, sister),
     ]
-    local = pltpu.make_async_copy(src, window(me), local_sem)
+    local = pltpu.make_async_copy(src, place(0), local_sem)
     local.start()
     squares[mine] = squares_part[...]
     for copy in square_copies:
@@ -110,16 +116,21 @@
     total = squares[0]
     for b in range(1, blocks):
         total = total + squares[b]
-    inverse_norm = lax.rsqrt(total / (blocks * width) + 1e-05)
-    squares[0] = inverse_norm
+    squares[0] = lax.rsqrt(total / (blocks * width) + 1e-05)
+
+    arrive(0, 1)
+    sent += [send(3, place(1), 4, up, core), send(4, place(1), 5, down, core),
+             send(8, place(1), 9, me, sister)]
+    arrive(1, 2)
+    sent += [send(5, place(2), 6, up, core), send(9, place(2), 10, me, sister)]
+    arrive(2, 3)
+    sent.append(send(10, place(3), 11, me, sister))
     for load in loads:
         load.wait()
     local.wait()
 
-    def absorb(origin, half=core, first=False):
-        block = origin * 2 + half
-        start = pl.multiple_of(block * width, width)
-        cols = pl.ds(start, width)
+    def absorb(first_place, first=False):
+        cols = pl.ds(first_place * width, 4 * width)
         scale = gain[:, cols]
 
         def one(i, carry):
@@ -140,31 +151,22 @@
 
         lax.fori_loop(0, slots // step, one, 0)
 
-    absorb(me, first=True)
-    arrive(0, partner)
-    sent += [send(3, partner, up, core), send(4, partner, down, core),
-             send(8, partner, me, sister)]
-    arrive(1, down)
-    sent += [send(5, down, up, core), send(9, down, me, sister)]
-    arrive(2, up)
-    sent.append(send(10, up, me, sister))
-    absorb(partner)
-    arrive(3, far(down))
-    sent.append(send(11, far(down), me, sister))
-    arrive(4, far(up))
-    sent += [send(6, far(up), down, core), send(12, far(up), me, sister)]
-    absorb(down)
-    arrive(5, across)
-    sent.append(send(13, across, me, sister))
-    arrive(6, far(across))
-    sent.append(send(14, far(across), me, sister))
-    for origin in (up, far(down), far(up), across, far(across)):
-        absorb(origin)
-
-    for tag, origin in ((7, me), (8, partner), (9, down), (10, up), (11, far(down)),
-                        (12, far(up)), (13, across), (14, far(across))):
-        arrive(tag, origin, sister)
-        absorb(origin, sister)
+    absorb(0, first=True)
+    arrive(3, 4)
+    sent.append(send(11, place(4), 12, me, sister))
+    arrive(4, 5)
+    sent += [send(6, place(5), 7, down, core), send(12, place(5), 13, me, sister)]
+    arrive(5, 6)
+    sent.append(send(13, place(6), 14, me, sister))
+    arrive(6, 7)
+    sent.append(send(14, place(7), 15, me, sister))
+    absorb(4)
+    for tag in range(7, 11):
+        arrive(tag, tag + 1)
+    absorb(8)
+    for tag in range(11, 15):
+        arrive(tag, tag + 1)
+    absorb(12)
 
     def finish(i, carry):
         part = pl.ds(pl.multiple_of(i * step, step), step)
@@ -199,13 +201,14 @@
             pltpu.VMEM((slots, features), jnp.bfloat16),
             pltpu.VMEM(w_gate.shape, w_gate.dtype),
             pltpu.VMEM(w_up.shape, w_up.dtype),
+            pltpu.VMEM((1, features), jnp.float32),
             pltpu.VMEM((slots, hidden_units), jnp.float32),
             pltpu.VMEM((slots, hidden_units), jnp.float32),
             pltpu.VMEM((blocks, slots // 256, 256), jnp.float32),
             pltpu.SemaphoreType.DMA((15,)),
             pltpu.SemaphoreType.DMA((15,)),
             pltpu.SemaphoreType.DMA(()),
-            pltpu.SemaphoreType.DMA((2,)),
+            pltpu.SemaphoreType.DMA((2, blocks)),
             pltpu.SemaphoreType.DMA((blocks,)),
             pltpu.SemaphoreType.DMA((blocks,)),
         ],

time: 202 us -> 187 us (0.926)
  Pallas kernels: 143 us -> 128 us
    pallas_call x1, Pallas kernels: 81.5 us -> 65.8 us  [expert_in(): pl.pallas_call(functools.partial(expert_in_kernel, width), out_shape=jax....]
where the time goes in v11:
time: 187 us; the launch traced here: 186 us
  Pallas kernels  128 us (68%)
  blocking collectives  16.2 us (9%)
  matrix products  16.1 us (9%)
  waiting for transfers between devices  14.1 us (8%)
  local copies, waits for them, and re-layouts  4.43 us (2%)
  other arithmetic  3.83 us (2%)
  starting transfers between devices  3.7 us (2%)
    pallas_call x1, Pallas kernels, expert_in(): pl.pallas_call(functools.partial(expert_in_kernel, width), out_shape=jax....  65.8 us
    pallas_call x1, Pallas kernels, scatter_cols(): pl.pallas_call(functools.partial(scatter_kernel, width), out_shape=jax.Sh...  62.1 us
    all_to_all x1, blocking collectives, body(): lax.all_to_all(packed, 'row', split_axis=0, concat_axis=0, tiled=True)  16.2 us
    dot_general x1, matrix products, body(): outputs = jnp.dot(hidden, w_down[0], preferred_element_type=jnp.float32)  14.8 us
    all_to_all x1, waiting for transfers between devices, body(): lax.all_to_all(shares, 'row', split_axis=0, concat_axis=0, tiled=True)  14.1 us
  transfers between devices with their start and end apart: 1, of which 1 were waited for; matrix products, arithmetic and copies ran while one was open for 0% of the time, Pallas kernels for 0%

profile of v11, /device:TPU:0, one launch (start us, length us, event | category | flops | bytes accessed | tf_op | source)
XLA Modules:
  0.0 186.4 jit_solution(7433380958208563674)
XLA Ops:
  0.0 0.8 copy.21
  0.8 0.1 eq.42
  1.0 0.1 eq.38
  1.1 1.1 reduce-window.6
  2.3 0.2 slice_reduce_fusion
  2.5 0.1 fusion.4
  2.6 0.1 reduce_sum.39
  2.8 0.1 copy.23
  2.8 0.7 compare_select_fusion
  3.5 0.3 convert_reduce_fusion
  3.8 1.3 convolution_convert_fusion
  5.1 16.2 %all_to_all.10 = bf16[8,128,256]{2,1,0:T(8,128)(2,1)S(1)} all-to-all(bf16[8,128,256]{2,1,0:T(8,128)(2,1)S(1)} %bitcast.26), channel_id=1, replica_groups=mesh['row'=8,'chip'=8,'core'=2] {'row'}, dimensions={0} | all-to-all | bytes 1048576 | tf_op jit(solution)/shard_map/all_to_all | solution.py:347
  21.3 0.0 copy-start
  21.3 0.2 multiply_reduce_fusion
  21.5 0.6 reshape.50.squares_part
  22.1 0.0 copy-done
  22.1 65.8 %shard_map.73 = bf16[1024,896]{1,0:T(8,128)(2,1)} custom-call(bf16[1024,256]{1,0:T(8,128)(2,1)} %bitcast.24, f32[4,256]{1,0:T(4,128)} %reshape.50.squares_part, f32[1,4096]{1,0:T(1,128)} %bitcast.27, bf16[4096,896]{1,0:T(8,128)(2,1)} %bitcast.22, bf16[4096,896]{1,0:T(8,128)(2,1)} %bitcast.23), custom_call_target="tpu_custom_call" | custom-call | tf_op jit(solution)/shard_map/pallas_call | solution.py:194
  87.8 14.8 %fusion.parts = f32[1024,4096]{1,0:T(8,128)} fusion(bf16[1024,896]{1,0:T(8,128)(2,1)} %shard_map.73, bf16[1,896,4096]{2,1,0:T(8,128)(2,1)} %param.13), kind=kOutput, calls=%fused_computation.1 | convolution fusion | flops 7516192768 | bytes 25952256 | tf_op jit(solution)/shard_map/dot_general | solution.py:352
  102.7 0.0 copy-start.2
  102.7 62.1 %shard_map.74 = f32[1024,256]{1,0:T(8,128)} custom-call(f32[1024,4096]{1,0:T(8,128)} %fusion.parts), custom_call_target="tpu_custom_call" | custom-call | tf_op jit(solution)/shard_map/pallas_call | solution.py:315
  164.8 0.0 copy-start.1
  164.8 3.7 %all-to-all-start.1 = ((f32[8,128,256]{2,1,0:T(8,128)}), f32[8,128,256]{2,1,0:T(8,128)S(1)}, u32[]{:S(2)}, u32[]{:S(2)}) async-start(f32[8,128,256]{2,1,0:T(8,128)} %bitcast.25), calls=%async_computation.1 | async-start | bytes 2097152 | tf_op jit(solution)/shard_map/all_to_all | solution.py:355
  168.5 0.1 copy.24
  168.6 0.1 reshape.56
  168.8 0.0 copy-done.2
  168.8 0.1 copy.25
  168.9 14.1 %all-to-all-done.1 = f32[8,128,256]{2,1,0:T(8,128)S(1)} async-done(((f32[8,128,256]{2,1,0:T(8,128)}), f32[8,128,256]{2,1,0:T(8,128)S(1)}, u32[]{:S(2)}, u32[]{:S(2)}) %all-to-all-start.1) | async-done | bytes 1048608 | tf_op jit(solution)/shard_map/all_to_all | solution.py:355
  183.1 1.6 gather_fusion
  184.7 0.3 reshape.55
  185.0 0.7 multiply_reduce_fusion.1
  185.7 0.0 copy-done.1
  185.7 0.7 add_convert_fusion
  (4 shorter events, 0.1 us)
Async XLA Ops:
  21.3 0.8 copy-start
  102.7 66.1 %copy-start.2 = (f32[256,2]{0,1:T(2,128)S(1)}, f32[256,2]{0,1:T(2,128)}, u32[]{:S(2)}) copy-start(f32[256,2]{0,1:T(2,128)} %param.10) | copy-start | bytes 6148
  164.8 20.9 %copy-start.1 = (bf16[256,256]{1,0:T(8,128)(2,1)S(1)}, bf16[256,256]{1,0:T(8,128)(2,1)}, u32[]{:S(2)}) copy-start(bf16[256,256]{1,0:T(8,128)(2,1)} %param.7) | copy-start | bytes 393220
  164.8 18.3 %all-to-all-start.1 = ((f32[8,128,256]{2,1,0:T(8,128)}), f32[8,128,256]{2,1,0:T(8,128)S(1)}, u32[]{:S(2)}, u32[]{:S(2)}) async-start(f32[8,128,256]{2,1,0:T(8,128)} %bitcast.25), calls=%async_computation.1 | async-start | bytes 2097152 | tf_op jit(solution)/shard_map/all_to_all | solution.py:355

commit v12 on v11

--- a/solution.py
+++ b/solution.py
@@ -218,6 +218,19 @@
     )(block, squares_part, norm_gain.reshape(1, features), w_gate, w_up)
 
 
+def project(dst, hidden, weights, start):
+    rows = dst.shape[0]
+    step = 256
+    cols = pl.ds(pl.multiple_of(start, 256), dst.shape[1])
+
+    def one(i, carry):
+        part = pl.ds(pl.multiple_of(i * step, step), step)
+        dst[part, :] = jnp.dot(hidden[part, :], weights[:, cols], preferred_element_type=jnp.float32)
+        return carry
+
+    lax.fori_loop(0, rows // step, one, 0)
+
+
 def add_blocks(dst, *sources):
     rows = dst.shape[0]
     step = 128
@@ -233,8 +246,8 @@
     lax.fori_loop(0, rows // step, one, 0)
 
 
-def scatter_kernel(width, parts, out, mine, theirs, sending, landed, local_sem, sister_send,
-                   sister_recv, send_sem, recv_sem):
+def scatter_kernel(width, hidden, weights, out, mine, theirs, outgoing, sending, landed,
+                   sister_send, sister_recv, send_sem, recv_sem):
     row, me, core = lax.axis_index("row"), lax.axis_index("chip"), lax.axis_index("core")
     sister = 1 - core
     side, y = me // 4, me % 4
@@ -246,30 +259,29 @@
     def far(chip):
         return lax.rem(chip + 4, 8)
 
-    def columns(chip, half):
-        start = pl.multiple_of((chip * 2 + half) * width, width)
-        return parts.at[:, pl.ds(start, width)]
-
     barrier = pltpu.get_barrier_semaphore()
     for chip, half in ((partner, core), (up, core), (down, core), (me, sister)):
         pl.semaphore_signal(barrier, inc=1, device_id=(row, chip, half), device_id_type=MESH)
     pl.semaphore_wait(barrier, 4)
 
     order = (far(down), across, up, far(across), down, far(up), partner, me)
-    swaps, loads = [], []
-    for slot, chip in enumerate(order):
-        swap = pltpu.make_async_remote_copy(
-            src_ref=columns(chip, sister), dst_ref=theirs.at[slot], send_sem=sister_send.at[slot],
-            recv_sem=sister_recv.at[slot], device_id=(row, me, sister), device_id_type=MESH,
-        )
-        swap.start()
-        swaps.append(swap)
-        load = pltpu.make_async_copy(columns(chip, core), mine.at[slot], local_sem.at[slot])
-        load.start()
-        loads.append(load)
+    swaps = []
+
+    def produce(slots):
+        for slot in slots:
+            project(outgoing.at[slot], hidden, weights, (order[slot] * 2 + sister) * width)
+            swap = pltpu.make_async_remote_copy(
+                src_ref=outgoing.at[slot], dst_ref=theirs.at[slot], send_sem=sister_send.at[slot],
+                recv_sem=sister_recv.at[slot], device_id=(row, me, sister), device_id_type=MESH,
+            )
+            swap.start()
+            swaps.append(swap)
+        for slot in slots:
+            project(mine.at[slot], hidden, weights, (order[slot] * 2 + core) * width)
+
+    produce(range(4))
 
     def ready(slot):
-        loads[slot].wait()
         swaps[slot].wait_recv()
         return (mine.at[slot], theirs.at[slot])
 
@@ -291,6 +303,7 @@
     for tag, chip in ((0, down), (1, down), (2, up), (3, up)):
         add_blocks(sending.at[tag], *ready(tag))
         sent.append(send(tag, chip))
+    produce(range(4, 8))
     arrive(1)
     add_blocks(sending.at[4], *ready(4), landed.at[1])
     sent.append(send(4, down))
@@ -310,28 +323,28 @@
         copy.wait_send()
 
 
-def scatter_cols(parts, width):
-    slots = parts.shape[0]
+def scatter_cols(hidden, weights, width):
+    slots = hidden.shape[0]
     return pl.pallas_call(
         functools.partial(scatter_kernel, width),
         out_shape=jax.ShapeDtypeStruct((slots, width), jnp.float32),
-        in_specs=[pl.BlockSpec(memory_space=pl.ANY)],
+        in_specs=[pl.BlockSpec(memory_space=pltpu.VMEM)] * 2,
         out_specs=pl.BlockSpec(memory_space=pltpu.VMEM),
         scratch_shapes=[
+            pltpu.VMEM((8, slots, width), jnp.float32),
             pltpu.VMEM((8, slots, width), jnp.float32),
             pltpu.VMEM((8, slots, width), jnp.float32),
             pltpu.VMEM((7, slots, width), jnp.bfloat16),
             pltpu.VMEM((7, slots, width), jnp.bfloat16),
             pltpu.SemaphoreType.DMA((8,)),
             pltpu.SemaphoreType.DMA((8,)),
-            pltpu.SemaphoreType.DMA((8,)),
             pltpu.SemaphoreType.DMA((7,)),
             pltpu.SemaphoreType.DMA((7,)),
         ],
         compiler_params=pltpu.CompilerParams(
-            collective_id=1, has_side_effects=True, vmem_limit_bytes=56 * 1024 * 1024
+            collective_id=1, has_side_effects=True, vmem_limit_bytes=60 * 1024 * 1024
         ),
-    )(parts)
+    )(hidden, weights)
 
 
 def body(tokens, norm_gain, expert_ids, gate_weights, w_gate, w_up, w_down):
@@ -349,8 +362,7 @@
     slots = arrived.shape[0]
 
     hidden = expert_in(arrived, norm_gain, w_gate[0], w_up[0], chips)
-    outputs = jnp.dot(hidden, w_down[0], preferred_element_type=jnp.float32)
-    shares = scatter_cols(outputs, width)
+    shares = scatter_cols(hidden, w_down[0], width)
     shares = shares.reshape(EXPERTS, CAP, width)
     returned = lax.all_to_all(shares, "row", split_axis=0, concat_axis=0, tiled=True)
     mixed = combine_rows(returned.reshape(-1, width), slot_index, gate_weights)

time: 187 us -> 175 us (0.936)
  matrix products: 16.1 us -> 1.26 us
  Pallas kernels: 128 us -> 132 us
  waiting for transfers between devices: 14.1 us -> 11.9 us
    dot_general x1 -> x0, matrix products: 14.8 us -> none  [body(): outputs = jnp.dot(hidden, w_down[0], preferred_element_type=jnp.float32)]
    pallas_call x1, Pallas kernels: 62.1 us -> 66.4 us  [scatter_cols(): pl.pallas_call(functools.partial(scatter_kernel, width), out_shape=jax.Sh...]
    all_to_all x1, waiting for transfers between devices: 14.1 us -> 11.9 us  [body(): lax.all_to_all(shares, 'row', split_axis=0, concat_axis=0, tiled=True)]
where the time goes in v12:
time: 175 us; the launch traced here: 173 us
  Pallas kernels  132 us (75%)
  blocking collectives  16.2 us (9%)
  waiting for transfers between devices  11.9 us (7%)
  local copies, waits for them, and re-layouts  4.43 us (3%)
  other arithmetic  3.84 us (2%)
  starting transfers between devices  3.57 us (2%)
    pallas_call x1, Pallas kernels, scatter_cols(): pl.pallas_call(functools.partial(scatter_kernel, width), out_shape=jax.Sh...  66.4 us
    pallas_call x1, Pallas kernels, expert_in(): pl.pallas_call(functools.partial(expert_in_kernel, width), out_shape=jax....  65.7 us
    all_to_all x1, blocking collectives, body(): lax.all_to_all(packed, 'row', split_axis=0, concat_axis=0, tiled=True)  16.2 us
    all_to_all x1, waiting for transfers between devices, body(): lax.all_to_all(shares, 'row', split_axis=0, concat_axis=0, tiled=True)  11.9 us
    all_to_all x1, starting transfers between devices, body(): lax.all_to_all(shares, 'row', split_axis=0, concat_axis=0, tiled=True)  3.57 us
  transfers between devices with their start and end apart: 1, of which 1 were waited for; matrix products, arithmetic and copies ran while one was open for 0% of the time, Pallas kernels for 0%

profile of v12, /device:TPU:0, one launch (start us, length us, event | category | flops | bytes accessed | tf_op | source)
XLA Modules:
  0.0 173.5 jit_solution(2213870229837025486)
XLA Ops:
  0.0 0.8 copy.21
  0.8 0.1 eq.42
  1.0 0.1 eq.38
  1.1 1.1 reduce-window.6
  2.3 0.2 slice_reduce_fusion
  2.5 0.1 fusion.2
  2.6 0.1 reduce_sum.39
  2.8 0.1 copy.23
  2.8 0.7 compare_select_fusion
  3.5 0.3 convert_reduce_fusion
  3.8 1.3 convolution_convert_fusion
  5.1 16.2 %all_to_all.10 = bf16[8,128,256]{2,1,0:T(8,128)(2,1)S(1)} all-to-all(bf16[8,128,256]{2,1,0:T(8,128)(2,1)S(1)} %bitcast.24), channel_id=1, replica_groups=mesh['row'=8,'chip'=8,'core'=2] {'row'}, dimensions={0} | all-to-all | bytes 1048576 | tf_op jit(solution)/shard_map/all_to_all | solution.py:360
  21.3 0.0 copy-start
  21.3 0.2 multiply_reduce_fusion
  21.5 0.6 reshape.50.squares_part
  22.1 0.0 copy-done
  22.1 65.7 %shard_map.73.hidden = bf16[1024,896]{1,0:T(8,128)(2,1)} custom-call(bf16[1024,256]{1,0:T(8,128)(2,1)} %bitcast.22, f32[4,256]{1,0:T(4,128)} %reshape.50.squares_part, f32[1,4096]{1,0:T(1,128)} %bitcast.25, bf16[4096,896]{1,0:T(8,128)(2,1)} %bitcast.20, bf16[4096,896]{1,0:T(8,128)(2,1)} %bitcast.21), custom_call_target="tpu_custom_call" | custom-call | tf_op jit(solution)/shard_map/pallas_call | solution.py:194
  87.8 66.4 %shard_map.74 = f32[1024,256]{1,0:T(8,128)} custom-call(bf16[1024,896]{1,0:T(8,128)(2,1)} %shard_map.73.hidden, bf16[896,4096]{1,0:T(8,128)(2,1)} %bitcast.19), custom_call_target="tpu_custom_call" | custom-call | tf_op jit(solution)/shard_map/pallas_call | solution.py:328
  154.2 0.0 copy-start.2
  154.3 3.6 %all-to-all-start.1 = ((f32[8,128,256]{2,1,0:T(8,128)}), f32[8,128,256]{2,1,0:T(8,128)S(1)}, u32[]{:S(2)}, u32[]{:S(2)}) async-start(f32[8,128,256]{2,1,0:T(8,128)} %bitcast.23), calls=%async_computation.1 | async-start | bytes 2097152 | tf_op jit(solution)/shard_map/all_to_all | solution.py:367
  157.8 0.1 copy.24
  158.0 0.1 reshape.56
  158.1 0.0 copy-done.2
  158.1 0.1 copy.25
  158.3 11.9 %all-to-all-done.1 = f32[8,128,256]{2,1,0:T(8,128)S(1)} async-done(((f32[8,128,256]{2,1,0:T(8,128)}), f32[8,128,256]{2,1,0:T(8,128)S(1)}, u32[]{:S(2)}, u32[]{:S(2)}) %all-to-all-start.1) | async-done | bytes 1048608 | tf_op jit(solution)/shard_map/all_to_all | solution.py:367
  170.2 0.0 copy-start.1
  170.2 1.6 gather_fusion
  171.8 0.3 reshape.55
  172.1 0.7 multiply_reduce_fusion.1
  172.8 0.0 copy-done.1
  172.8 0.7 add_convert_fusion
  (4 shorter events, 0.0 us)
Async XLA Ops:
  21.3 0.8 copy-start
  154.2 3.9 %copy-start.2 = (f32[256,2]{0,1:T(2,128)S(1)}, f32[256,2]{0,1:T(2,128)}, u32[]{:S(2)}) copy-start(f32[256,2]{0,1:T(2,128)} %param.10) | copy-start | bytes 6148
  154.3 15.9 %all-to-all-start.1 = ((f32[8,128,256]{2,1,0:T(8,128)}), f32[8,128,256]{2,1,0:T(8,128)S(1)}, u32[]{:S(2)}, u32[]{:S(2)}) async-start(f32[8,128,256]{2,1,0:T(8,128)} %bitcast.23), calls=%async_computation.1 | async-start | bytes 2097152 | tf_op jit(solution)/shard_map/all_to_all | solution.py:367
  170.2 2.6 %copy-start.1 = (bf16[256,256]{1,0:T(8,128)(2,1)S(1)}, bf16[256,256]{1,0:T(8,128)(2,1)}, u32[]{:S(2)}) copy-start(bf16[256,256]{1,0:T(8,128)(2,1)} %param.7) | copy-start | bytes 393220

commit v13 on v12

--- a/solution.py
+++ b/solution.py
@@ -246,8 +246,8 @@
     lax.fori_loop(0, rows // step, one, 0)
 
 
-def scatter_kernel(width, hidden, weights, out, mine, theirs, outgoing, sending, landed,
-                   sister_send, sister_recv, send_sem, recv_sem):
+def scatter_kernel(width, hidden, weights, returned, out, mine, theirs, outgoing, sending,
+                   landed, sister_send, sister_recv, send_sem, recv_sem, back_send, back_recv):
     row, me, core = lax.axis_index("row"), lax.axis_index("chip"), lax.axis_index("core")
     sister = 1 - core
     side, y = me // 4, me % 4
@@ -259,10 +259,14 @@
     def far(chip):
         return lax.rem(chip + 4, 8)
 
+    rows = returned.shape[0]
     barrier = pltpu.get_barrier_semaphore()
     for chip, half in ((partner, core), (up, core), (down, core), (me, sister)):
         pl.semaphore_signal(barrier, inc=1, device_id=(row, chip, half), device_id_type=MESH)
-    pl.semaphore_wait(barrier, 4)
+    for d in range(1, rows):
+        pl.semaphore_signal(barrier, inc=1, device_id=(lax.rem(row + d, rows), me, core),
+                            device_id_type=MESH)
+    pl.semaphore_wait(barrier, 4 + rows - 1)
 
     order = (far(down), across, up, far(across), down, far(up), partner, me)
     swaps = []
@@ -319,18 +323,33 @@
     add_blocks(out, *ready(7), landed.at[2], landed.at[4])
     arrive(6)
     add_blocks(out, out, landed.at[6])
+    depth = returned.shape[1]
+    returned[row] = out[pl.ds(pl.multiple_of(row * depth, depth), depth), :]
+    backs = []
+    for d in range(1, rows):
+        source = lax.rem(row + d, rows)
+        back = pltpu.make_async_remote_copy(
+            src_ref=out.at[pl.ds(pl.multiple_of(source * depth, depth), depth), :],
+            dst_ref=returned.at[row], send_sem=back_send.at[d], recv_sem=back_recv.at[d],
+            device_id=(source, me, core), device_id_type=MESH,
+        )
+        back.start()
+        backs.append(back)
     for copy in sent + swaps:
         copy.wait_send()
-
-
-def scatter_cols(hidden, weights, width):
+    for back in backs:
+        back.wait()
+
+
+def scatter_cols(hidden, weights, width, rows):
     slots = hidden.shape[0]
     return pl.pallas_call(
         functools.partial(scatter_kernel, width),
-        out_shape=jax.ShapeDtypeStruct((slots, width), jnp.float32),
+        out_shape=jax.ShapeDtypeStruct((rows, slots // rows, width), jnp.float32),
         in_specs=[pl.BlockSpec(memory_space=pltpu.VMEM)] * 2,
         out_specs=pl.BlockSpec(memory_space=pltpu.VMEM),
         scratch_shapes=[
+            pltpu.VMEM((slots, width), jnp.float32),
             pltpu.VMEM((8, slots, width), jnp.float32),
             pltpu.VMEM((8, slots, width), jnp.float32),
             pltpu.VMEM((8, slots, width), jnp.float32),
@@ -340,6 +359,8 @@
             pltpu.SemaphoreType.DMA((8,)),
             pltpu.SemaphoreType.DMA((7,)),
             pltpu.SemaphoreType.DMA((7,)),
+            pltpu.SemaphoreType.DMA((rows,)),
+            pltpu.SemaphoreType.DMA((rows,)),
         ],
         compiler_params=pltpu.CompilerParams(
             collective_id=1, has_side_effects=True, vmem_limit_bytes=60 * 1024 * 1024
@@ -362,9 +383,7 @@
     slots = arrived.shape[0]
 
     hidden = expert_in(arrived, norm_gain, w_gate[0], w_up[0], chips)
-    shares = scatter_cols(hidden, w_down[0], width)
-    shares = shares.reshape(EXPERTS, CAP, width)
-    returned = lax.all_to_all(shares, "row", split_axis=0, concat_axis=0, tiled=True)
+    returned = scatter_cols(hidden, w_down[0], width, EXPERTS)
     mixed = combine_rows(returned.reshape(-1, width), slot_index, gate_weights)
     return (tokens.astype(jnp.float32) + mixed).astype(jnp.bfloat16)
 

time: 175 us -> 169 us (0.966)
  blocking collectives: 16.2 us -> 0 us
  Pallas kernels: 132 us -> 142 us
  waiting for transfers between devices: 11.9 us -> 9.13 us
  starting transfers between devices: 3.57 us -> 6.33 us
    all_to_all x1 -> x0, blocking collectives: 16.2 us -> none  [body(): lax.all_to_all(packed, 'row', split_axis=0, concat_axis=0, tiled=True)]
    pallas_call x1, Pallas kernels: 66.4 us -> 76 us  [scatter_cols(): pl.pallas_call(functools.partial(scatter_kernel, width), out_shape=jax.Sh...]
    all_to_all x1, waiting for transfers between devices: 11.9 us -> 9.13 us  [body(): lax.all_to_all(packed, 'row', split_axis=0, concat_axis=0, tiled=True)]
    all_to_all x1, starting transfers between devices: 3.57 us -> 6.33 us  [body(): lax.all_to_all(packed, 'row', split_axis=0, concat_axis=0, tiled=True)]
where the time goes in v13:
time: 169 us
  Pallas kernels  142 us (84%)
  waiting for transfers between devices  9.13 us (5%)
  starting transfers between devices  6.33 us (4%)
  local copies, waits for them, and re-layouts  5.7 us (3%)
  other arithmetic  3.84 us (2%)
  matrix products  2.05 us (1%)
    pallas_call x1, Pallas kernels, scatter_cols(): pl.pallas_call(functools.partial(scatter_kernel, width), out_shape=jax.Sh...  76 us
    pallas_call x1, Pallas kernels, expert_in(): pl.pallas_call(functools.partial(expert_in_kernel, width), out_shape=jax....  65.7 us
    all_to_all x1, waiting for transfers between devices, body(): lax.all_to_all(packed, 'row', split_axis=0, concat_axis=0, tiled=True)  9.13 us
    all_to_all x1, starting transfers between devices, body(): lax.all_to_all(packed, 'row', split_axis=0, concat_axis=0, tiled=True)  6.33 us
  transfers between devices with their start and end apart: 1, of which 1 were waited for; matrix products, arithmetic and copies ran while one was open for 0% of the time, Pallas kernels for 0%

profile of v13, /device:TPU:0, one launch (start us, length us, event | category | flops | bytes accessed | tf_op | source)
XLA Modules:
  0.0 168.9 jit_solution(1374618989973025677)
XLA Ops:
  0.0 0.0 copy-start.2
  0.0 0.8 copy.21
  0.8 0.1 eq.42
  1.0 0.1 eq.38
  1.1 1.1 reduce-window.6
  2.3 0.2 slice_reduce_fusion
  2.5 0.1 fusion.2
  2.6 0.1 reduce_sum.39
  2.8 0.1 copy.23
  2.9 0.7 compare_select_fusion
  3.6 0.3 convert_reduce_fusion
  3.8 2.0 %convolution_convert_fusion = bf16[1024,256]{1,0:T(8,128)(2,1)} fusion(bf16[256,256]{1,0:T(8,128)(2,1)} %param.7, bf16[256,1024]{1,0:T(8,128)(2,1)S(1)} %convert_reduce_fusion), kind=kOutput, calls=%fused_computation.3 | convolution fusion | flops 134479872 | bytes 1179648 | tf_op jit(solution)/shard_map/ts,td->sd/dot_general | solution.py:377
  5.9 6.3 %all-to-all-start = ((bf16[8,128,256]{2,1,0:T(8,128)(2,1)}), bf16[8,128,256]{2,1,0:T(8,128)(2,1)S(1)}, u32[]{:S(2)}, u32[]{:S(2)}) async-start(bf16[8,128,256]{2,1,0:T(8,128)(2,1)} %bitcast.2), calls=%async_computation | async-start | bytes 1048576 | tf_op jit(solution)/shard_map/all_to_all | solution.py:381
  12.2 0.1 copy.24
  12.3 0.1 reshape.52
  12.5 0.0 copy-done.2
  12.5 0.1 copy.25
  12.6 9.1 %all-to-all-done = bf16[8,128,256]{2,1,0:T(8,128)(2,1)S(1)} async-done(((bf16[8,128,256]{2,1,0:T(8,128)(2,1)}), bf16[8,128,256]{2,1,0:T(8,128)(2,1)S(1)}, u32[]{:S(2)}, u32[]{:S(2)}) %all-to-all-start) | async-done | bytes 524320 | tf_op jit(solution)/shard_map/all_to_all | solution.py:381
  21.8 0.0 copy-start
  21.8 0.2 multiply_reduce_fusion
  22.0 0.6 reshape.47.squares_part
  22.6 0.0 copy-done
  22.6 65.7 %shard_map.73.hidden = bf16[1024,896]{1,0:T(8,128)(2,1)} custom-call(bf16[1024,256]{1,0:T(8,128)(2,1)} %bitcast.21, f32[4,256]{1,0:T(4,128)} %reshape.47.squares_part, f32[1,4096]{1,0:T(1,128)} %bitcast.22, bf16[4096,896]{1,0:T(8,128)(2,1)} %bitcast.19, bf16[4096,896]{1,0:T(8,128)(2,1)} %bitcast.20), custom_call_target="tpu_custom_call" | custom-call | tf_op jit(solution)/shard_map/pallas_call | solution.py:194
  88.3 76.0 %shard_map.74 = f32[8,128,256]{2,1,0:T(8,128)} custom-call(bf16[1024,896]{1,0:T(8,128)(2,1)} %shard_map.73.hidden, bf16[896,4096]{1,0:T(8,128)(2,1)} %bitcast.18), custom_call_target="tpu_custom_call" | custom-call | tf_op jit(solution)/shard_map/pallas_call | solution.py:346
  164.4 0.0 copy-start.1
  164.4 2.8 %gather_fusion = f32[512,256]{1,0:T(8,128)S(1)} fusion(f32[1024,256]{1,0:T(8,128)} %bitcast.17, s32[1024]{0:T(1024)S(1)} %pad_clamp_fusion), kind=kCustom, calls=%fused_computation | custom fusion | bytes 1050624 | tf_op jit(solution)/shard_map/gather | solution.py:38
  167.2 0.3 reshape.51
  167.5 0.7 multiply_reduce_fusion.1
  168.2 0.0 copy-done.1
  168.3 0.7 add_convert_fusion
  (4 shorter events, 0.0 us)
Async XLA Ops:
  0.0 12.5 %copy-start.2 = (f32[256,2]{0,1:T(2,128)S(1)}, f32[256,2]{0,1:T(2,128)}, u32[]{:S(2)}) copy-start(f32[256,2]{0,1:T(2,128)} %param.10) | copy-start | bytes 6148
  5.9 15.9 %all-to-all-start = ((bf16[8,128,256]{2,1,0:T(8,128)(2,1)}), bf16[8,128,256]{2,1,0:T(8,128)(2,1)S(1)}, u32[]{:S(2)}, u32[]{:S(2)}) async-start(bf16[8,128,256]{2,1,0:T(8,128)(2,1)} %bitcast.2), calls=%async_computation | async-start | bytes 1048576 | tf_op jit(solution)/shard_map/all_to_all | solution.py:381
  21.8 0.8 copy-start
  164.4 3.9 %copy-start.1 = (bf16[256,256]{1,0:T(8,128)(2,1)S(1)}, bf16[256,256]{1,0:T(8,128)(2,1)}, u32[]{:S(2)}) copy-start(bf16[256,256]{1,0:T(8,128)(2,1)} %param.7) | copy-start | bytes 393220

commit v14 on v13

--- a/solution.py
+++ b/solution.py
@@ -39,9 +39,9 @@
     return jnp.sum(picked * gate_weights[:, :, None], axis=1)
 
 
-def expert_in_kernel(width, src, squares_part, gain_in, w_gate_hbm, w_up_hbm, hidden, xs, w_gate,
-                     w_up, gain, acc_gate, acc_up, squares, send_sem, recv_sem, local_sem,
-                     weight_sem, square_send, square_recv):
+def expert_in_kernel(width, packed, gain_in, w_gate_hbm, w_up_hbm, hidden, src, squares_part, xs,
+                     w_gate, w_up, gain, acc_gate, acc_up, squares, send_sem, recv_sem, local_sem,
+                     weight_sem, square_send, square_recv, come_send, come_recv):
     row, me, core = lax.axis_index("row"), lax.axis_index("chip"), lax.axis_index("core")
     side, y = me // 4, me % 4
     partner = lax.rem(me + 4, 8)
@@ -67,12 +67,42 @@
             loads.append(load)
         gain[:, pl.ds(place * width, width)] = gain_in[:, rows]
 
+    rows, depth = packed.shape[0], packed.shape[1]
     barrier = pltpu.get_barrier_semaphore()
     for d in range(1, blocks):
         other = lax.rem(mine + d, blocks)
         pl.semaphore_signal(barrier, inc=1, device_id=(row, other // 2, other % 2),
                             device_id_type=MESH)
-    pl.semaphore_wait(barrier, blocks - 1)
+    for d in range(1, rows):
+        pl.semaphore_signal(barrier, inc=1, device_id=(lax.rem(row + d, rows), me, core),
+                            device_id_type=MESH)
+    pl.semaphore_wait(barrier, blocks - 1 + rows - 1)
+
+    def rows_of(r):
+        return pl.ds(pl.multiple_of(r * depth, depth), depth)
+
+    comes = []
+    for d in range(1, rows):
+        target = lax.rem(row + d, rows)
+        come = pltpu.make_async_remote_copy(
+            src_ref=packed.at[target], dst_ref=src.at[rows_of(row), :],
+            send_sem=come_send.at[d], recv_sem=come_recv.at[d],
+            device_id=(target, me, core), device_id_type=MESH,
+        )
+        come.start()
+        comes.append(come)
+    src[rows_of(row), :] = packed[row]
+    for come in comes:
+        come.wait_recv()
+
+    def sum_squares(i, carry):
+        part = pl.ds(pl.multiple_of(i * step, step), step)
+        values = src[part, :].astype(jnp.float32)
+        total = jnp.sum(values * values, axis=1, keepdims=True)
+        squares_part[pl.ds(i, 1), :] = jnp.transpose(jnp.broadcast_to(total, (step, 128)))[0:1, :]
+        return carry
+
+    lax.fori_loop(0, slots // step, sum_squares, 0)
 
     square_copies = []
     for d in range(1, blocks):
@@ -176,7 +206,7 @@
         return carry
 
     lax.fori_loop(0, slots // step, finish, 0)
-    for copy in sent + square_copies:
+    for copy in sent + square_copies + comes:
         copy.wait_send()
 
 
@@ -184,20 +214,21 @@
     return lax.rem(chip + 4, 8)
 
 
-def expert_in(block, norm_gain, w_gate, w_up, chips):
-    slots, width = block.shape
+def expert_in(packed, norm_gain, w_gate, w_up, chips):
+    rows, depth, width = packed.shape
+    slots = rows * depth
     blocks = chips * 2
     features = blocks * width
     hidden_units = w_gate.shape[1]
-    values = block.astype(jnp.float32)
-    squares_part = jnp.sum(values * values, axis=1).reshape(slots // 256, 256)
     return pl.pallas_call(
         functools.partial(expert_in_kernel, width),
         out_shape=jax.ShapeDtypeStruct((slots, hidden_units), jnp.bfloat16),
-        in_specs=[pl.BlockSpec(memory_space=pltpu.VMEM)] * 3
+        in_specs=[pl.BlockSpec(memory_space=pltpu.VMEM)] * 2
         + [pl.BlockSpec(memory_space=pl.ANY)] * 2,
         out_specs=pl.BlockSpec(memory_space=pltpu.VMEM),
         scratch_shapes=[
+            pltpu.VMEM((slots, width), packed.dtype),
+            pltpu.VMEM((slots // 256, 256), jnp.float32),
             pltpu.VMEM((slots, features), jnp.bfloat16),
             pltpu.VMEM(w_gate.shape, w_gate.dtype),
             pltpu.VMEM(w_up.shape, w_up.dtype),
@@ -211,11 +242,13 @@
             pltpu.SemaphoreType.DMA((2, blocks)),
             pltpu.SemaphoreType.DMA((blocks,)),
             pltpu.SemaphoreType.DMA((blocks,)),
+            pltpu.SemaphoreType.DMA((rows,)),
+            pltpu.SemaphoreType.DMA((rows,)),
         ],
         compiler_params=pltpu.CompilerParams(
             collective_id=0, has_side_effects=True, vmem_limit_bytes=60 * 1024 * 1024
         ),
-    )(block, squares_part, norm_gain.reshape(1, features), w_gate, w_up)
+    )(packed, norm_gain.reshape(1, features), w_gate, w_up)
 
 
 def project(dst, hidden, weights, start):
@@ -378,11 +411,7 @@
         jnp.bfloat16
     )
     packed = packed.reshape(EXPERTS, CAP, width)
-    arrived = lax.all_to_all(packed, "row", split_axis=0, concat_axis=0, tiled=True)
-    arrived = arrived.reshape(EXPERTS * CAP, width)
-    slots = arrived.shape[0]
-
-    hidden = expert_in(arrived, norm_gain, w_gate[0], w_up[0], chips)
+    hidden = expert_in(packed, norm_gain, w_gate[0], w_up[0], chips)
     returned = scatter_cols(hidden, w_down[0], width, EXPERTS)
     mixed = combine_rows(returned.reshape(-1, width), slot_index, gate_weights)
     return (tokens.astype(jnp.float32) + mixed).astype(jnp.bfloat16)

time: 169 us -> 165 us (0.976)
  Pallas kernels: 142 us -> 153 us
  waiting for transfers between devices: 9.13 us -> 0 us
  starting transfers between devices: 6.33 us -> 0 us
    pallas_call x1, Pallas kernels: 65.7 us -> 75.7 us  [expert_in(): pl.pallas_call(functools.partial(expert_in_kernel, width), out_shape=jax....]
    all_to_all x1 -> x0, waiting for transfers between devices: 9.13 us -> none  [body(): lax.all_to_all(packed, 'row', split_axis=0, concat_axis=0, tiled=True)]
    all_to_all x1 -> x0, starting transfers between devices: 6.33 us -> none  [body(): lax.all_to_all(packed, 'row', split_axis=0, concat_axis=0, tiled=True)]
    pallas_call x1, Pallas kernels: 76 us -> 77.8 us  [scatter_cols(): pl.pallas_call(functools.partial(scatter_kernel, width), out_shape=jax.Sh...]
  transfers between devices with their start and end apart: 1 -> 0, of which waited for: 1 -> 0; matrix products, arithmetic and copies ran while one was open for 0% -> 0% of each run, Pallas kernels for 0% -> 0%
where the time goes in v14:
time: 165 us; the launch traced here: 164 us
  Pallas kernels  153 us (93%)
  local copies, waits for them, and re-layouts  5.06 us (3%)
  other arithmetic  3.64 us (2%)
  matrix products  2.07 us (1%)
    pallas_call x1, Pallas kernels, scatter_cols(): pl.pallas_call(functools.partial(scatter_kernel, width), out_shape=jax.Sh...  77.8 us
    pallas_call x1, Pallas kernels, expert_in(): pl.pallas_call(functools.partial(expert_in_kernel, width), out_shape=jax....  75.7 us

profile of v14, /device:TPU:0, one launch (start us, length us, event | category | flops | bytes accessed | tf_op | source)
XLA Modules:
  0.0 164.4 jit_solution(3100794395849789321)
XLA Ops:
  0.0 0.8 copy.21
  0.8 0.1 eq.42
  1.0 1.1 reduce-window.6
  2.1 0.2 slice_reduce_fusion
  2.4 0.1 eq.38
  2.5 0.1 fusion.2
  2.6 0.1 reduce_sum.30
  2.8 0.1 copy.23
  2.8 0.7 compare_select_fusion
  3.5 0.3 convert_reduce_fusion
  3.8 2.1 %convolution_convert_fusion = bf16[1024,256]{1,0:T(8,128)(2,1)} fusion(bf16[256,256]{1,0:T(8,128)(2,1)} %param.7, bf16[256,1024]{1,0:T(8,128)(2,1)S(1)} %convert_reduce_fusion), kind=kOutput, calls=%fused_computation.3 | convolution fusion | flops 134479872 | bytes 1179648 | tf_op jit(solution)/shard_map/ts,td->sd/dot_general | solution.py:410
  5.9 75.7 %shard_map.73.hidden = bf16[1024,896]{1,0:T(8,128)(2,1)} custom-call(bf16[8,128,256]{2,1,0:T(8,128)(2,1)} %bitcast.20, f32[1,4096]{1,0:T(1,128)} %bitcast.21, bf16[4096,896]{1,0:T(8,128)(2,1)} %bitcast.17, bf16[4096,896]{1,0:T(8,128)(2,1)} %bitcast.18), custom_call_target="tpu_custom_call" | custom-call | tf_op jit(solution)/shard_map/pallas_call | solution.py:223
  81.6 77.8 %shard_map.74 = f32[8,128,256]{2,1,0:T(8,128)} custom-call(bf16[1024,896]{1,0:T(8,128)(2,1)} %shard_map.73.hidden, bf16[896,4096]{1,0:T(8,128)(2,1)} %bitcast.19), custom_call_target="tpu_custom_call" | custom-call | tf_op jit(solution)/shard_map/pallas_call | solution.py:379
  159.3 0.1 copy.24
  159.5 0.1 reshape.42
  159.6 0.0 copy-start.1
  159.7 2.8 %gather_fusion = f32[512,256]{1,0:T(8,128)S(1)} fusion(f32[1024,256]{1,0:T(8,128)} %bitcast.16, s32[1024]{0:T(1024)S(1)} %pad_clamp_fusion), kind=kCustom, calls=%fused_computation | custom fusion | bytes 1050624 | tf_op jit(solution)/shard_map/gather | solution.py:38
  162.5 0.0 copy-start
  162.5 0.3 reshape.41
  162.8 0.0 copy-done.1
  162.8 0.1 copy.25
  162.9 0.7 multiply_reduce_fusion
  163.7 0.0 copy-done
  163.7 0.7 add_convert_fusion
  (4 shorter events, 0.1 us)
Async XLA Ops:
  159.6 3.1 %copy-start.1 = (f32[256,2]{0,1:T(2,128)S(1)}, f32[256,2]{0,1:T(2,128)}, u32[]{:S(2)}) copy-start(f32[256,2]{0,1:T(2,128)} %param.10) | copy-start | bytes 6148
  162.5 1.2 copy-start

commit v15 on v14

--- a/solution.py
+++ b/solution.py
@@ -279,8 +279,9 @@
     lax.fori_loop(0, rows // step, one, 0)
 
 
-def scatter_kernel(width, hidden, weights, returned, out, mine, theirs, outgoing, sending,
-                   landed, sister_send, sister_recv, send_sem, recv_sem, back_send, back_recv):
+def scatter_kernel(width, hidden, weights_hbm, returned, weights, out, mine, theirs, outgoing,
+                   sending, landed, weight_sem, sister_send, sister_recv, send_sem, recv_sem,
+                   back_send, back_recv):
     row, me, core = lax.axis_index("row"), lax.axis_index("chip"), lax.axis_index("core")
     sister = 1 - core
     side, y = me // 4, me % 4
@@ -293,6 +294,15 @@
         return lax.rem(chip + 4, 8)
 
     rows = returned.shape[0]
+    order = (far(down), across, up, far(across), down, far(up), partner, me)
+    loads = {}
+    for slot, chip in enumerate(order):
+        for index, half in enumerate((sister, core)):
+            cols = pl.ds(pl.multiple_of((chip * 2 + half) * width, width), width)
+            load = pltpu.make_async_copy(weights_hbm.at[:, cols], weights.at[:, cols],
+                                         weight_sem.at[index, slot])
+            load.start()
+            loads[(slot, index)] = load
     barrier = pltpu.get_barrier_semaphore()
     for chip, half in ((partner, core), (up, core), (down, core), (me, sister)):
         pl.semaphore_signal(barrier, inc=1, device_id=(row, chip, half), device_id_type=MESH)
@@ -301,11 +311,11 @@
                             device_id_type=MESH)
     pl.semaphore_wait(barrier, 4 + rows - 1)
 
-    order = (far(down), across, up, far(across), down, far(up), partner, me)
     swaps = []
 
-    def produce(slots):
+    def produce(slots, own=True):
         for slot in slots:
+            loads[(slot, 0)].wait()
             project(outgoing.at[slot], hidden, weights, (order[slot] * 2 + sister) * width)
             swap = pltpu.make_async_remote_copy(
                 src_ref=outgoing.at[slot], dst_ref=theirs.at[slot], send_sem=sister_send.at[slot],
@@ -313,10 +323,15 @@
             )
             swap.start()
             swaps.append(swap)
-        for slot in slots:
-            project(mine.at[slot], hidden, weights, (order[slot] * 2 + core) * width)
-
-    produce(range(4))
+        if own:
+            for slot in slots:
+                own_block(slot)
+
+    def own_block(slot):
+        loads[(slot, 1)].wait()
+        project(mine.at[slot], hidden, weights, (order[slot] * 2 + core) * width)
+
+    produce(range(4), own=False)
 
     def ready(slot):
         swaps[slot].wait_recv()
@@ -338,6 +353,7 @@
 
     sent = []
     for tag, chip in ((0, down), (1, down), (2, up), (3, up)):
+        own_block(tag)
         add_blocks(sending.at[tag], *ready(tag))
         sent.append(send(tag, chip))
     produce(range(4, 8))
@@ -379,15 +395,17 @@
     return pl.pallas_call(
         functools.partial(scatter_kernel, width),
         out_shape=jax.ShapeDtypeStruct((rows, slots // rows, width), jnp.float32),
-        in_specs=[pl.BlockSpec(memory_space=pltpu.VMEM)] * 2,
+        in_specs=[pl.BlockSpec(memory_space=pltpu.VMEM), pl.BlockSpec(memory_space=pl.ANY)],
         out_specs=pl.BlockSpec(memory_space=pltpu.VMEM),
         scratch_shapes=[
+            pltpu.VMEM(weights.shape, weights.dtype),
             pltpu.VMEM((slots, width), jnp.float32),
             pltpu.VMEM((8, slots, width), jnp.float32),
             pltpu.VMEM((8, slots, width), jnp.float32),
             pltpu.VMEM((8, slots, width), jnp.float32),
             pltpu.VMEM((7, slots, width), jnp.bfloat16),
             pltpu.VMEM((7, slots, width), jnp.bfloat16),
+            pltpu.SemaphoreType.DMA((2, 8)),
             pltpu.SemaphoreType.DMA((8,)),
             pltpu.SemaphoreType.DMA((8,)),
             pltpu.SemaphoreType.DMA((7,)),

time: 165 us -> 161 us (0.976)
  Pallas kernels: 153 us -> 150 us
    pallas_call x1, Pallas kernels: 77.8 us -> 74.5 us  [scatter_cols(): pl.pallas_call(functools.partial(scatter_kernel, width), out_shape=jax.Sh...]
where the time goes in v15:
time: 161 us
  Pallas kernels  150 us (93%)
  local copies, waits for them, and re-layouts  5.06 us (3%)
  other arithmetic  3.64 us (2%)
  matrix products  2.07 us (1%)
    pallas_call x1, Pallas kernels, expert_in(): pl.pallas_call(functools.partial(expert_in_kernel, width), out_shape=jax....  75.7 us
    pallas_call x1, Pallas kernels, scatter_cols(): pl.pallas_call(functools.partial(scatter_kernel, width), out_shape=jax.Sh...  74.5 us

profile of v15, /device:TPU:0, one launch (start us, length us, event | category | flops | bytes accessed | tf_op | source)
XLA Modules:
  0.0 161.1 jit_solution(2033853966593010851)
XLA Ops:
  0.0 0.8 copy.21
  0.8 0.1 eq.42
  1.0 1.1 reduce-window.6
  2.1 0.2 slice_reduce_fusion
  2.4 0.1 eq.38
  2.5 0.1 fusion.2
  2.6 0.1 reduce_sum.30
  2.8 0.1 copy.23
  2.8 0.7 compare_select_fusion
  3.5 0.3 convert_reduce_fusion
  3.8 2.1 %convolution_convert_fusion = bf16[1024,256]{1,0:T(8,128)(2,1)} fusion(bf16[256,256]{1,0:T(8,128)(2,1)} %param.7, bf16[256,1024]{1,0:T(8,128)(2,1)S(1)} %convert_reduce_fusion), kind=kOutput, calls=%fused_computation.3 | convolution fusion | flops 134479872 | bytes 1179648 | tf_op jit(solution)/shard_map/ts,td->sd/dot_general | solution.py:428
  5.9 75.7 %shard_map.73.hidden = bf16[1024,896]{1,0:T(8,128)(2,1)} custom-call(bf16[8,128,256]{2,1,0:T(8,128)(2,1)} %bitcast.20, f32[1,4096]{1,0:T(1,128)} %bitcast.21, bf16[4096,896]{1,0:T(8,128)(2,1)} %bitcast.17, bf16[4096,896]{1,0:T(8,128)(2,1)} %bitcast.18), custom_call_target="tpu_custom_call" | custom-call | tf_op jit(solution)/shard_map/pallas_call | solution.py:223
  81.6 74.5 %shard_map.74 = f32[8,128,256]{2,1,0:T(8,128)} custom-call(bf16[1024,896]{1,0:T(8,128)(2,1)} %shard_map.73.hidden, bf16[896,4096]{1,0:T(8,128)(2,1)} %bitcast.19), custom_call_target="tpu_custom_call" | custom-call | tf_op jit(solution)/shard_map/pallas_call | solution.py:395
  156.1 0.1 copy.24
  156.2 0.1 reshape.42
  156.4 0.0 copy-start.1
  156.4 2.8 %gather_fusion = f32[512,256]{1,0:T(8,128)S(1)} fusion(f32[1024,256]{1,0:T(8,128)} %bitcast.16, s32[1024]{0:T(1024)S(1)} %pad_clamp_fusion), kind=kCustom, calls=%fused_computation | custom fusion | bytes 1050624 | tf_op jit(solution)/shard_map/gather | solution.py:38
  159.2 0.0 copy-start
  159.2 0.3 reshape.41
  159.5 0.0 copy-done.1
  159.6 0.1 copy.25
  159.7 0.7 multiply_reduce_fusion
  160.4 0.0 copy-done
  160.4 0.7 add_convert_fusion
  (4 shorter events, 0.1 us)
Async XLA Ops:
  156.4 3.1 %copy-start.1 = (f32[256,2]{0,1:T(2,128)S(1)}, f32[256,2]{0,1:T(2,128)}, u32[]{:S(2)}) copy-start(f32[256,2]{0,1:T(2,128)} %param.10) | copy-start | bytes 6148
  159.2 1.2 copy-start

commit v16 on v15

--- a/solution.py
+++ b/solution.py
@@ -159,8 +159,8 @@
         load.wait()
     local.wait()
 
-    def absorb(first_place, first=False):
-        cols = pl.ds(first_place * width, 4 * width)
+    def absorb(first_place, count=4, first=False, last=False):
+        cols = pl.ds(first_place * width, count * width)
         scale = gain[:, cols]
 
         def one(i, carry):
@@ -174,6 +174,10 @@
             if first:
                 acc_gate[part, :] = gate_part
                 acc_up[part, :] = up_part
+            elif last:
+                gate_values = acc_gate[part, :] + gate_part
+                silu = gate_values / (1.0 + jnp.exp(-gate_values))
+                hidden[part, :] = (silu * (acc_up[part, :] + up_part)).astype(hidden.dtype)
             else:
                 acc_gate[part, :] += gate_part
                 acc_up[part, :] += up_part
@@ -194,18 +198,12 @@
     for tag in range(7, 11):
         arrive(tag, tag + 1)
     absorb(8)
-    for tag in range(11, 15):
+    for tag in range(11, 13):
         arrive(tag, tag + 1)
-    absorb(12)
-
-    def finish(i, carry):
-        part = pl.ds(pl.multiple_of(i * step, step), step)
-        gate_values = acc_gate[part, :]
-        silu = gate_values / (1.0 + jnp.exp(-gate_values))
-        hidden[part, :] = (silu * acc_up[part, :]).astype(hidden.dtype)
-        return carry
-
-    lax.fori_loop(0, slots // step, finish, 0)
+    absorb(12, count=2)
+    for tag in range(13, 15):
+        arrive(tag, tag + 1)
+    absorb(14, count=2, last=True)
     for copy in sent + square_copies + comes:
         copy.wait_send()
 

time: 161 us -> 162 us (level)
  no operation moved by 1% of the time
where the time goes in v16:
time: 162 us
  Pallas kernels  151 us (93%)
  local copies, waits for them, and re-layouts  5.06 us (3%)
  other arithmetic  3.64 us (2%)
  matrix products  2.07 us (1%)
    pallas_call x1, Pallas kernels, expert_in(): pl.pallas_call(functools.partial(expert_in_kernel, width), out_shape=jax....  76.6 us
    pallas_call x1, Pallas kernels, scatter_cols(): pl.pallas_call(functools.partial(scatter_kernel, width), out_shape=jax.Sh...  74.5 us

profile of v16, /device:TPU:0, one launch (start us, length us, event | category | flops | bytes accessed | tf_op | source)
XLA Modules:
  0.0 162.0 jit_solution(9029173595490435647)
XLA Ops:
  0.0 0.8 copy.21
  0.8 0.1 eq.42
  1.0 1.1 reduce-window.6
  2.1 0.2 slice_reduce_fusion
  2.4 0.1 eq.38
  2.5 0.1 fusion.2
  2.6 0.1 reduce_sum.30
  2.8 0.1 copy.23
  2.8 0.7 compare_select_fusion
  3.5 0.3 convert_reduce_fusion
  3.8 2.1 %convolution_convert_fusion = bf16[1024,256]{1,0:T(8,128)(2,1)} fusion(bf16[256,256]{1,0:T(8,128)(2,1)} %param.7, bf16[256,1024]{1,0:T(8,128)(2,1)S(1)} %convert_reduce_fusion), kind=kOutput, calls=%fused_computation.3 | convolution fusion | flops 134479872 | bytes 1179648 | tf_op jit(solution)/shard_map/ts,td->sd/dot_general | solution.py:426
  5.9 76.6 %shard_map.73.hidden = bf16[1024,896]{1,0:T(8,128)(2,1)} custom-call(bf16[8,128,256]{2,1,0:T(8,128)(2,1)} %bitcast.20, f32[1,4096]{1,0:T(1,128)} %bitcast.21, bf16[4096,896]{1,0:T(8,128)(2,1)} %bitcast.17, bf16[4096,896]{1,0:T(8,128)(2,1)} %bitcast.18), custom_call_target="tpu_custom_call" | custom-call | tf_op jit(solution)/shard_map/pallas_call | solution.py:221
  82.4 74.5 %shard_map.74 = f32[8,128,256]{2,1,0:T(8,128)} custom-call(bf16[1024,896]{1,0:T(8,128)(2,1)} %shard_map.73.hidden, bf16[896,4096]{1,0:T(8,128)(2,1)} %bitcast.19), custom_call_target="tpu_custom_call" | custom-call | tf_op jit(solution)/shard_map/pallas_call | solution.py:393
  157.0 0.1 copy.24
  157.1 0.1 reshape.42
  157.3 0.0 copy-start.1
  157.3 2.8 %gather_fusion = f32[512,256]{1,0:T(8,128)S(1)} fusion(f32[1024,256]{1,0:T(8,128)} %bitcast.16, s32[1024]{0:T(1024)S(1)} %pad_clamp_fusion), kind=kCustom, calls=%fused_computation | custom fusion | bytes 1050624 | tf_op jit(solution)/shard_map/gather | solution.py:38
  160.1 0.0 copy-start
  160.1 0.3 reshape.41
  160.4 0.0 copy-done.1
  160.4 0.1 copy.25
  160.6 0.7 multiply_reduce_fusion
  161.3 0.0 copy-done
  161.3 0.7 add_convert_fusion
  (4 shorter events, 0.1 us)
Async XLA Ops:
  157.3 3.1 %copy-start.1 = (f32[256,2]{0,1:T(2,128)S(1)}, f32[256,2]{0,1:T(2,128)}, u32[]{:S(2)}) copy-start(f32[256,2]{0,1:T(2,128)} %param.10) | copy-start | bytes 6148
  160.1 1.2 copy-start

commit v17 on v15

--- a/solution.py
+++ b/solution.py
@@ -115,29 +115,35 @@
         copy.start()
         square_copies.append(copy)
 
-    def place(p):
-        return xs.at[:, pl.ds(p * width, width)]
-
-    def send(tag, source, target, chip, half):
+    half_rows = slots // 2
+
+    def rows_half(h):
+        return pl.ds(h * half_rows, half_rows)
+
+    def place(p, h=None):
+        if h is None:
+            return xs.at[:, pl.ds(p * width, width)]
+        return xs.at[rows_half(h), pl.ds(p * width, width)]
+
+    def send(tag, source, target, chip, half, h):
+        origin = src.at[rows_half(h), :] if source is None else place(source, h)
         copy = pltpu.make_async_remote_copy(
-            src_ref=source, dst_ref=place(target), send_sem=send_sem.at[tag],
-            recv_sem=recv_sem.at[tag], device_id=(row, chip, half), device_id_type=MESH,
+            src_ref=origin, dst_ref=place(target, h), send_sem=send_sem.at[tag, h],
+            recv_sem=recv_sem.at[tag, h], device_id=(row, chip, half), device_id_type=MESH,
         )
         copy.start()
         return copy
 
-    def arrive(tag, target):
+    def arrive(tag, target, h):
         pltpu.make_async_remote_copy(
-            src_ref=place(target), dst_ref=place(target), send_sem=send_sem.at[tag],
-            recv_sem=recv_sem.at[tag], device_id=(row, me, sister), device_id_type=MESH,
+            src_ref=place(target, h), dst_ref=place(target, h), send_sem=send_sem.at[tag, h],
+            recv_sem=recv_sem.at[tag, h], device_id=(row, me, sister), device_id_type=MESH,
         ).wait_recv()
 
-    sent = [
-        send(0, src, 1, partner, core),
-        send(1, src, 2, up, core),
-        send(2, src, 3, down, core),
-        send(7, src, 8, me, sister),
-    ]
+    sent = []
+    for h in (0, 1):
+        sent += [send(0, None, 1, partner, core, h), send(1, None, 2, up, core, h),
+                 send(2, None, 3, down, core, h), send(7, None, 8, me, sister, h)]
     local = pltpu.make_async_copy(src, place(0), local_sem)
     local.start()
     squares[mine] = squares_part[...]
@@ -148,13 +154,14 @@
         total = total + squares[b]
     squares[0] = lax.rsqrt(total / (blocks * width) + 1e-05)
 
-    arrive(0, 1)
-    sent += [send(3, place(1), 4, up, core), send(4, place(1), 5, down, core),
-             send(8, place(1), 9, me, sister)]
-    arrive(1, 2)
-    sent += [send(5, place(2), 6, up, core), send(9, place(2), 10, me, sister)]
-    arrive(2, 3)
-    sent.append(send(10, place(3), 11, me, sister))
+    for h in (0, 1):
+        arrive(0, 1, h)
+        sent += [send(3, 1, 4, up, core, h), send(4, 1, 5, down, core, h),
+                 send(8, 1, 9, me, sister, h)]
+        arrive(1, 2, h)
+        sent += [send(5, 2, 6, up, core, h), send(9, 2, 10, me, sister, h)]
+        arrive(2, 3, h)
+        sent.append(send(10, 3, 11, me, sister, h))
     for load in loads:
         load.wait()
     local.wait()
@@ -182,20 +189,23 @@
         lax.fori_loop(0, slots // step, one, 0)
 
     absorb(0, first=True)
-    arrive(3, 4)
-    sent.append(send(11, place(4), 12, me, sister))
-    arrive(4, 5)
-    sent += [send(6, place(5), 7, down, core), send(12, place(5), 13, me, sister)]
-    arrive(5, 6)
-    sent.append(send(13, place(6), 14, me, sister))
-    arrive(6, 7)
-    sent.append(send(14, place(7), 15, me, sister))
+    for h in (0, 1):
+        arrive(3, 4, h)
+        sent.append(send(11, 4, 12, me, sister, h))
+        arrive(4, 5, h)
+        sent += [send(6, 5, 7, down, core, h), send(12, 5, 13, me, sister, h)]
+        arrive(5, 6, h)
+        sent.append(send(13, 6, 14, me, sister, h))
+        arrive(6, 7, h)
+        sent.append(send(14, 7, 15, me, sister, h))
     absorb(4)
     for tag in range(7, 11):
-        arrive(tag, tag + 1)
+        for h in (0, 1):
+            arrive(tag, tag + 1, h)
     absorb(8)
     for tag in range(11, 15):
-        arrive(tag, tag + 1)
+        for h in (0, 1):
+            arrive(tag, tag + 1, h)
     absorb(12)
 
     def finish(i, carry):
@@ -236,8 +246,8 @@
             pltpu.VMEM((slots, hidden_units), jnp.float32),
             pltpu.VMEM((slots, hidden_units), jnp.float32),
             pltpu.VMEM((blocks, slots // 256, 256), jnp.float32),
-            pltpu.SemaphoreType.DMA((15,)),
-            pltpu.SemaphoreType.DMA((15,)),
+            pltpu.SemaphoreType.DMA((15, 2)),
+            pltpu.SemaphoreType.DMA((15, 2)),
             pltpu.SemaphoreType.DMA(()),
             pltpu.SemaphoreType.DMA((2, blocks)),
             pltpu.SemaphoreType.DMA((blocks,)),

time: 161 us -> 159 us (0.988)
  Pallas kernels: 150 us -> 147 us
    pallas_call x1, Pallas kernels: 74.5 us -> 70.4 us  [scatter_cols(): pl.pallas_call(functools.partial(scatter_kernel, width), out_shape=jax.Sh...]
where the time goes in v17:
time: 159 us; the launch traced here: 158 us
  Pallas kernels  147 us (92%)
  local copies, waits for them, and re-layouts  5.06 us (3%)
  other arithmetic  3.64 us (2%)
  matrix products  2.07 us (1%)
    pallas_call x1, Pallas kernels, expert_in(): pl.pallas_call(functools.partial(expert_in_kernel, width), out_shape=jax....  76.9 us
    pallas_call x1, Pallas kernels, scatter_cols(): pl.pallas_call(functools.partial(scatter_kernel, width), out_shape=jax.Sh...  70.4 us

profile of v17, /device:TPU:0, one launch (start us, length us, event | category | flops | bytes accessed | tf_op | source)
XLA Modules:
  0.0 158.2 jit_solution(11088605728970573516)
XLA Ops:
  0.0 0.8 copy.21
  0.8 0.1 eq.42
  1.0 1.1 reduce-window.6
  2.1 0.2 slice_reduce_fusion
  2.4 0.1 eq.38
  2.5 0.1 fusion.2
  2.6 0.1 reduce_sum.30
  2.8 0.1 copy.23
  2.8 0.7 compare_select_fusion
  3.5 0.3 convert_reduce_fusion
  3.8 2.1 %convolution_convert_fusion = bf16[1024,256]{1,0:T(8,128)(2,1)} fusion(bf16[256,256]{1,0:T(8,128)(2,1)} %param.7, bf16[256,1024]{1,0:T(8,128)(2,1)S(1)} %convert_reduce_fusion), kind=kOutput, calls=%fused_computation.3 | convolution fusion | flops 134479872 | bytes 1179648 | tf_op jit(solution)/shard_map/ts,td->sd/dot_general | solution.py:438
  5.9 76.9 %shard_map.73.hidden = bf16[1024,896]{1,0:T(8,128)(2,1)} custom-call(bf16[8,128,256]{2,1,0:T(8,128)(2,1)} %bitcast.20, f32[1,4096]{1,0:T(1,128)} %bitcast.21, bf16[4096,896]{1,0:T(8,128)(2,1)} %bitcast.17, bf16[4096,896]{1,0:T(8,128)(2,1)} %bitcast.18), custom_call_target="tpu_custom_call" | custom-call | tf_op jit(solution)/shard_map/pallas_call | solution.py:233
  82.8 70.4 %shard_map.74 = f32[8,128,256]{2,1,0:T(8,128)} custom-call(bf16[1024,896]{1,0:T(8,128)(2,1)} %shard_map.73.hidden, bf16[896,4096]{1,0:T(8,128)(2,1)} %bitcast.19), custom_call_target="tpu_custom_call" | custom-call | tf_op jit(solution)/shard_map/pallas_call | solution.py:405
  153.2 0.1 copy.24
  153.3 0.1 reshape.42
  153.5 0.0 copy-start.1
  153.5 2.8 %gather_fusion = f32[512,256]{1,0:T(8,128)S(1)} fusion(f32[1024,256]{1,0:T(8,128)} %bitcast.16, s32[1024]{0:T(1024)S(1)} %pad_clamp_fusion), kind=kCustom, calls=%fused_computation | custom fusion | bytes 1050624 | tf_op jit(solution)/shard_map/gather | solution.py:38
  156.3 0.0 copy-start
  156.3 0.3 reshape.41
  156.7 0.0 copy-done.1
  156.7 0.1 copy.25
  156.8 0.7 multiply_reduce_fusion
  157.5 0.0 copy-done
  157.5 0.7 add_convert_fusion
  (4 shorter events, 0.1 us)
Async XLA Ops:
  153.5 3.1 %copy-start.1 = (f32[256,2]{0,1:T(2,128)S(1)}, f32[256,2]{0,1:T(2,128)}, u32[]{:S(2)}) copy-start(f32[256,2]{0,1:T(2,128)} %param.10) | copy-start | bytes 6148
  156.3 1.2 copy-start

commit v18 on v17

--- a/solution.py
+++ b/solution.py
@@ -347,41 +347,58 @@
         swaps[slot].wait_recv()
         return (mine.at[slot], theirs.at[slot])
 
-    def send(tag, chip):
+    half_rows = mine.shape[1] // 2
+
+    def cut(ref, h):
+        return ref.at[pl.ds(h * half_rows, half_rows), :]
+
+    def send(tag, chip, h):
         copy = pltpu.make_async_remote_copy(
-            src_ref=sending.at[tag], dst_ref=landed.at[tag], send_sem=send_sem.at[tag],
-            recv_sem=recv_sem.at[tag], device_id=(row, chip, core), device_id_type=MESH,
+            src_ref=cut(sending.at[tag], h), dst_ref=cut(landed.at[tag], h),
+            send_sem=send_sem.at[tag, h], recv_sem=recv_sem.at[tag, h],
+            device_id=(row, chip, core), device_id_type=MESH,
         )
         copy.start()
         return copy
 
-    def arrive(tag):
+    def arrive(tag, h):
         pltpu.make_async_remote_copy(
-            src_ref=sending.at[tag], dst_ref=landed.at[tag], send_sem=send_sem.at[tag],
-            recv_sem=recv_sem.at[tag], device_id=(row, me, core), device_id_type=MESH,
+            src_ref=cut(sending.at[tag], h), dst_ref=cut(landed.at[tag], h),
+            send_sem=send_sem.at[tag, h], recv_sem=recv_sem.at[tag, h],
+            device_id=(row, me, core), device_id_type=MESH,
         ).wait_recv()
+
+    def combine(dst, h, *sources):
+        add_blocks(cut(dst, h), *[cut(source, h) for source in sources])
 
     sent = []
     for tag, chip in ((0, down), (1, down), (2, up), (3, up)):
         own_block(tag)
-        add_blocks(sending.at[tag], *ready(tag))
-        sent.append(send(tag, chip))
+        pair = ready(tag)
+        for h in (0, 1):
+            combine(sending.at[tag], h, *pair)
+            sent.append(send(tag, chip, h))
     produce(range(4, 8))
-    arrive(1)
-    add_blocks(sending.at[4], *ready(4), landed.at[1])
-    sent.append(send(4, down))
-    arrive(3)
-    add_blocks(sending.at[5], *ready(5), landed.at[3])
-    sent.append(send(5, up))
-    arrive(0)
-    arrive(5)
-    add_blocks(sending.at[6], *ready(6), landed.at[0], landed.at[5])
-    sent.append(send(6, partner))
-    arrive(2)
-    arrive(4)
-    add_blocks(out, *ready(7), landed.at[2], landed.at[4])
-    arrive(6)
-    add_blocks(out, out, landed.at[6])
+    pairs = [ready(slot) for slot in range(4, 8)]
+    for h in (0, 1):
+        arrive(1, h)
+        combine(sending.at[4], h, *pairs[0], landed.at[1])
+        sent.append(send(4, down, h))
+        arrive(3, h)
+        combine(sending.at[5], h, *pairs[1], landed.at[3])
+        sent.append(send(5, up, h))
+    for h in (0, 1):
+        arrive(0, h)
+        arrive(5, h)
+        combine(sending.at[6], h, *pairs[2], landed.at[0], landed.at[5])
+        sent.append(send(6, partner, h))
+    for h in (0, 1):
+        arrive(2, h)
+        arrive(4, h)
+        combine(out, h, *pairs[3], landed.at[2], landed.at[4])
+    for h in (0, 1):
+        arrive(6, h)
+        combine(out, h, out, landed.at[6])
     depth = returned.shape[1]
     returned[row] = out[pl.ds(pl.multiple_of(row * depth, depth), depth), :]
     backs = []
@@ -418,8 +435,8 @@
             pltpu.SemaphoreType.DMA((2, 8)),
             pltpu.SemaphoreType.DMA((8,)),
             pltpu.SemaphoreType.DMA((8,)),
-            pltpu.SemaphoreType.DMA((7,)),
-            pltpu.SemaphoreType.DMA((7,)),
+            pltpu.SemaphoreType.DMA((7, 2)),
+            pltpu.SemaphoreType.DMA((7, 2)),
             pltpu.SemaphoreType.DMA((rows,)),
             pltpu.SemaphoreType.DMA((rows,)),
         ],

time: 159 us -> 158 us (level)
  no operation moved by 1% of the time
where the time goes in v18:
time: 158 us
  Pallas kernels  147 us (93%)
  local copies, waits for them, and re-layouts  5.06 us (3%)
  other arithmetic  3.64 us (2%)
  matrix products  2.07 us (1%)
    pallas_call x1, Pallas kernels, expert_in(): pl.pallas_call(functools.partial(expert_in_kernel, width), out_shape=jax....  76.9 us
    pallas_call x1, Pallas kernels, scatter_cols(): pl.pallas_call(functools.partial(scatter_kernel, width), out_shape=jax.Sh...  70.4 us

profile of v18, /device:TPU:0, one launch (start us, length us, event | category | flops | bytes accessed | tf_op | source)
XLA Modules:
  0.0 158.2 jit_solution(16099041018764726304)
XLA Ops:
  0.0 0.8 copy.21
  0.8 0.1 eq.42
  1.0 1.1 reduce-window.6
  2.1 0.2 slice_reduce_fusion
  2.4 0.1 eq.38
  2.5 0.1 fusion.2
  2.6 0.1 reduce_sum.30
  2.8 0.1 copy.23
  2.8 0.7 compare_select_fusion
  3.5 0.3 convert_reduce_fusion
  3.8 2.1 %convolution_convert_fusion = bf16[1024,256]{1,0:T(8,128)(2,1)} fusion(bf16[256,256]{1,0:T(8,128)(2,1)} %param.7, bf16[256,1024]{1,0:T(8,128)(2,1)S(1)} %convert_reduce_fusion), kind=kOutput, calls=%fused_computation.3 | convolution fusion | flops 134479872 | bytes 1179648 | tf_op jit(solution)/shard_map/ts,td->sd/dot_general | solution.py:455
  5.9 76.9 %shard_map.73.hidden = bf16[1024,896]{1,0:T(8,128)(2,1)} custom-call(bf16[8,128,256]{2,1,0:T(8,128)(2,1)} %bitcast.20, f32[1,4096]{1,0:T(1,128)} %bitcast.21, bf16[4096,896]{1,0:T(8,128)(2,1)} %bitcast.17, bf16[4096,896]{1,0:T(8,128)(2,1)} %bitcast.18), custom_call_target="tpu_custom_call" | custom-call | tf_op jit(solution)/shard_map/pallas_call | solution.py:233
  82.8 70.4 %shard_map.74 = f32[8,128,256]{2,1,0:T(8,128)} custom-call(bf16[1024,896]{1,0:T(8,128)(2,1)} %shard_map.73.hidden, bf16[896,4096]{1,0:T(8,128)(2,1)} %bitcast.19), custom_call_target="tpu_custom_call" | custom-call | tf_op jit(solution)/shard_map/pallas_call | solution.py:422
  153.1 0.1 copy.24
  153.3 0.1 reshape.42
  153.4 0.0 copy-start.1
  153.5 2.8 %gather_fusion = f32[512,256]{1,0:T(8,128)S(1)} fusion(f32[1024,256]{1,0:T(8,128)} %bitcast.16, s32[1024]{0:T(1024)S(1)} %pad_clamp_fusion), kind=kCustom, calls=%fused_computation | custom fusion | bytes 1050624 | tf_op jit(solution)/shard_map/gather | solution.py:38
  156.3 0.0 copy-start
  156.3 0.3 reshape.41
  156.6 0.0 copy-done.1
  156.6 0.1 copy.25
  156.7 0.7 multiply_reduce_fusion
  157.4 0.0 copy-done
  157.5 0.7 add_convert_fusion
  (4 shorter events, 0.1 us)
Async XLA Ops:
  153.4 3.1 %copy-start.1 = (f32[256,2]{0,1:T(2,128)S(1)}, f32[256,2]{0,1:T(2,128)}, u32[]{:S(2)}) copy-start(f32[256,2]{0,1:T(2,128)} %param.10) | copy-start | bytes 6148
  156.3 1.2 copy-start

commit v19 on v18

--- a/solution.py
+++ b/solution.py
@@ -166,7 +166,7 @@
         load.wait()
     local.wait()
 
-    def absorb(first_place, first=False):
+    def absorb(first_place, first=False, rows_part=None):
         cols = pl.ds(first_place * width, 4 * width)
         scale = gain[:, cols]
 
@@ -186,7 +186,11 @@
                 acc_up[part, :] += up_part
             return carry
 
-        lax.fori_loop(0, slots // step, one, 0)
+        chunks = slots // step
+        if rows_part is None:
+            lax.fori_loop(0, chunks, one, 0)
+        else:
+            lax.fori_loop(rows_part * chunks // 2, (rows_part + 1) * chunks // 2, one, 0)
 
     absorb(0, first=True)
     for h in (0, 1):
@@ -199,14 +203,11 @@
         arrive(6, 7, h)
         sent.append(send(14, 7, 15, me, sister, h))
     absorb(4)
-    for tag in range(7, 11):
+    for first_place in (8, 12):
         for h in (0, 1):
-            arrive(tag, tag + 1, h)
-    absorb(8)
-    for tag in range(11, 15):
-        for h in (0, 1):
-            arrive(tag, tag + 1, h)
-    absorb(12)
+            for tag in range(first_place - 1, first_place + 3):
+                arrive(tag, tag + 1, h)
+            absorb(first_place, rows_part=h)
 
     def finish(i, carry):
         part = pl.ds(pl.multiple_of(i * step, step), step)

time: 158 us -> 158 us (level)
  no operation moved by 1% of the time
where the time goes in v19:
time: 158 us
  Pallas kernels  147 us (93%)
  local copies, waits for them, and re-layouts  5.06 us (3%)
  other arithmetic  3.64 us (2%)
  matrix products  2.07 us (1%)
    pallas_call x1, Pallas kernels, expert_in(): pl.pallas_call(functools.partial(expert_in_kernel, width), out_shape=jax....  76.9 us
    pallas_call x1, Pallas kernels, scatter_cols(): pl.pallas_call(functools.partial(scatter_kernel, width), out_shape=jax.Sh...  70.4 us

profile of v19, /device:TPU:0, one launch (start us, length us, event | category | flops | bytes accessed | tf_op | source)
XLA Modules:
  0.0 158.2 jit_solution(15289018298381647245)
XLA Ops:
  0.0 0.8 copy.21
  0.8 0.1 eq.42
  1.0 1.1 reduce-window.6
  2.1 0.2 slice_reduce_fusion
  2.4 0.1 eq.38
  2.5 0.1 fusion.2
  2.6 0.1 reduce_sum.30
  2.8 0.1 copy.23
  2.8 0.7 compare_select_fusion
  3.5 0.3 convert_reduce_fusion
  3.8 2.1 %convolution_convert_fusion = bf16[1024,256]{1,0:T(8,128)(2,1)} fusion(bf16[256,256]{1,0:T(8,128)(2,1)} %param.7, bf16[256,1024]{1,0:T(8,128)(2,1)S(1)} %convert_reduce_fusion), kind=kOutput, calls=%fused_computation.3 | convolution fusion | flops 134479872 | bytes 1179648 | tf_op jit(solution)/shard_map/ts,td->sd/dot_general | solution.py:456
  5.9 76.9 %shard_map.73.hidden = bf16[1024,896]{1,0:T(8,128)(2,1)} custom-call(bf16[8,128,256]{2,1,0:T(8,128)(2,1)} %bitcast.20, f32[1,4096]{1,0:T(1,128)} %bitcast.21, bf16[4096,896]{1,0:T(8,128)(2,1)} %bitcast.17, bf16[4096,896]{1,0:T(8,128)(2,1)} %bitcast.18), custom_call_target="tpu_custom_call" | custom-call | tf_op jit(solution)/shard_map/pallas_call | solution.py:234
  82.8 70.4 %shard_map.74 = f32[8,128,256]{2,1,0:T(8,128)} custom-call(bf16[1024,896]{1,0:T(8,128)(2,1)} %shard_map.73.hidden, bf16[896,4096]{1,0:T(8,128)(2,1)} %bitcast.19), custom_call_target="tpu_custom_call" | custom-call | tf_op jit(solution)/shard_map/pallas_call | solution.py:423
  153.2 0.1 copy.24
  153.3 0.1 reshape.42
  153.5 0.0 copy-start.1
  153.5 2.8 %gather_fusion = f32[512,256]{1,0:T(8,128)S(1)} fusion(f32[1024,256]{1,0:T(8,128)} %bitcast.16, s32[1024]{0:T(1024)S(1)} %pad_clamp_fusion), kind=kCustom, calls=%fused_computation | custom fusion | bytes 1050624 | tf_op jit(solution)/shard_map/gather | solution.py:38
  156.3 0.0 copy-start
  156.3 0.3 reshape.41
  156.6 0.0 copy-done.1
  156.6 0.1 copy.25
  156.8 0.7 multiply_reduce_fusion
  157.5 0.0 copy-done
  157.5 0.7 add_convert_fusion
  (4 shorter events, 0.1 us)
Async XLA Ops:
  153.5 3.1 %copy-start.1 = (f32[256,2]{0,1:T(2,128)S(1)}, f32[256,2]{0,1:T(2,128)}, u32[]{:S(2)}) copy-start(f32[256,2]{0,1:T(2,128)} %param.10) | copy-start | bytes 6148
  156.3 1.2 copy-start

commit v20 on v19

--- a/solution.py
+++ b/solution.py
@@ -322,18 +322,21 @@
                             device_id_type=MESH)
     pl.semaphore_wait(barrier, 4 + rows - 1)
 
-    swaps = []
+    swaps = {}
 
     def produce(slots, own=True):
         for slot in slots:
             loads[(slot, 0)].wait()
             project(outgoing.at[slot], hidden, weights, (order[slot] * 2 + sister) * width)
-            swap = pltpu.make_async_remote_copy(
-                src_ref=outgoing.at[slot], dst_ref=theirs.at[slot], send_sem=sister_send.at[slot],
-                recv_sem=sister_recv.at[slot], device_id=(row, me, sister), device_id_type=MESH,
-            )
-            swap.start()
-            swaps.append(swap)
+            for h in (0, 1):
+                rows_h = pl.ds(h * (hidden.shape[0] // 2), hidden.shape[0] // 2)
+                swap = pltpu.make_async_remote_copy(
+                    src_ref=outgoing.at[slot, rows_h, :], dst_ref=theirs.at[slot, rows_h, :],
+                    send_sem=sister_send.at[slot, h], recv_sem=sister_recv.at[slot, h],
+                    device_id=(row, me, sister), device_id_type=MESH,
+                )
+                swap.start()
+                swaps[(slot, h)] = swap
         if own:
             for slot in slots:
                 own_block(slot)
@@ -344,8 +347,8 @@
 
     produce(range(4), own=False)
 
-    def ready(slot):
-        swaps[slot].wait_recv()
+    def ready(slot, h):
+        swaps[(slot, h)].wait_recv()
         return (mine.at[slot], theirs.at[slot])
 
     half_rows = mine.shape[1] // 2
@@ -375,28 +378,26 @@
     sent = []
     for tag, chip in ((0, down), (1, down), (2, up), (3, up)):
         own_block(tag)
-        pair = ready(tag)
         for h in (0, 1):
-            combine(sending.at[tag], h, *pair)
+            combine(sending.at[tag], h, *ready(tag, h))
             sent.append(send(tag, chip, h))
     produce(range(4, 8))
-    pairs = [ready(slot) for slot in range(4, 8)]
     for h in (0, 1):
         arrive(1, h)
-        combine(sending.at[4], h, *pairs[0], landed.at[1])
+        combine(sending.at[4], h, *ready(4, h), landed.at[1])
         sent.append(send(4, down, h))
         arrive(3, h)
-        combine(sending.at[5], h, *pairs[1], landed.at[3])
+        combine(sending.at[5], h, *ready(5, h), landed.at[3])
         sent.append(send(5, up, h))
     for h in (0, 1):
         arrive(0, h)
         arrive(5, h)
-        combine(sending.at[6], h, *pairs[2], landed.at[0], landed.at[5])
+        combine(sending.at[6], h, *ready(6, h), landed.at[0], landed.at[5])
         sent.append(send(6, partner, h))
     for h in (0, 1):
         arrive(2, h)
         arrive(4, h)
-        combine(out, h, *pairs[3], landed.at[2], landed.at[4])
+        combine(out, h, *ready(7, h), landed.at[2], landed.at[4])
     for h in (0, 1):
         arrive(6, h)
         combine(out, h, out, landed.at[6])
@@ -412,7 +413,7 @@
         )
         back.start()
         backs.append(back)
-    for copy in sent + swaps:
+    for copy in sent + list(swaps.values()):
         copy.wait_send()
     for back in backs:
         back.wait()
@@ -434,8 +435,8 @@
             pltpu.VMEM((7, slots, width), jnp.bfloat16),
             pltpu.VMEM((7, slots, width), jnp.bfloat16),
             pltpu.SemaphoreType.DMA((2, 8)),
-            pltpu.SemaphoreType.DMA((8,)),
-            pltpu.SemaphoreType.DMA((8,)),
+            pltpu.SemaphoreType.DMA((8, 2)),
+            pltpu.SemaphoreType.DMA((8, 2)),
             pltpu.SemaphoreType.DMA((7, 2)),
             pltpu.SemaphoreType.DMA((7, 2)),
             pltpu.SemaphoreType.DMA((rows,)),

time: 158 us -> 159 us (level)
  no operation moved by 1% of the time
where the time goes in v20:
time: 159 us; the launch traced here: 158 us
  Pallas kernels  147 us (92%)
  local copies, waits for them, and re-layouts  5.06 us (3%)
  other arithmetic  3.64 us (2%)
  matrix products  2.07 us (1%)
    pallas_call x1, Pallas kernels, expert_in(): pl.pallas_call(functools.partial(expert_in_kernel, width), out_shape=jax....  76.9 us
    pallas_call x1, Pallas kernels, scatter_cols(): pl.pallas_call(functools.partial(scatter_kernel, width), out_shape=jax.Sh...  70.6 us

profile of v20, /device:TPU:0, one launch (start us, length us, event | category | flops | bytes accessed | tf_op | source)
XLA Modules:
  0.0 158.4 jit_solution(10988871276617809106)
XLA Ops:
  0.0 0.8 copy.21
  0.8 0.1 eq.42
  1.0 1.1 reduce-window.6
  2.1 0.2 slice_reduce_fusion
  2.4 0.1 eq.38
  2.5 0.1 fusion.2
  2.6 0.1 reduce_sum.30
  2.8 0.1 copy.23
  2.8 0.7 compare_select_fusion
  3.5 0.3 convert_reduce_fusion
  3.8 2.1 %convolution_convert_fusion = bf16[1024,256]{1,0:T(8,128)(2,1)} fusion(bf16[256,256]{1,0:T(8,128)(2,1)} %param.7, bf16[256,1024]{1,0:T(8,128)(2,1)S(1)} %convert_reduce_fusion), kind=kOutput, calls=%fused_computation.3 | convolution fusion | flops 134479872 | bytes 1179648 | tf_op jit(solution)/shard_map/ts,td->sd/dot_general | solution.py:457
  5.9 76.9 %shard_map.73.hidden = bf16[1024,896]{1,0:T(8,128)(2,1)} custom-call(bf16[8,128,256]{2,1,0:T(8,128)(2,1)} %bitcast.20, f32[1,4096]{1,0:T(1,128)} %bitcast.21, bf16[4096,896]{1,0:T(8,128)(2,1)} %bitcast.17, bf16[4096,896]{1,0:T(8,128)(2,1)} %bitcast.18), custom_call_target="tpu_custom_call" | custom-call | tf_op jit(solution)/shard_map/pallas_call | solution.py:234
  82.8 70.6 %shard_map.74 = f32[8,128,256]{2,1,0:T(8,128)} custom-call(bf16[1024,896]{1,0:T(8,128)(2,1)} %shard_map.73.hidden, bf16[896,4096]{1,0:T(8,128)(2,1)} %bitcast.19), custom_call_target="tpu_custom_call" | custom-call | tf_op jit(solution)/shard_map/pallas_call | solution.py:424
  153.4 0.1 copy.24
  153.5 0.1 reshape.42
  153.7 0.0 copy-start.1
  153.7 2.8 %gather_fusion = f32[512,256]{1,0:T(8,128)S(1)} fusion(f32[1024,256]{1,0:T(8,128)} %bitcast.16, s32[1024]{0:T(1024)S(1)} %pad_clamp_fusion), kind=kCustom, calls=%fused_computation | custom fusion | bytes 1050624 | tf_op jit(solution)/shard_map/gather | solution.py:38
  156.5 0.0 copy-start
  156.5 0.3 reshape.41
  156.8 0.0 copy-done.1
  156.8 0.1 copy.25
  157.0 0.7 multiply_reduce_fusion
  157.7 0.0 copy-done
  157.7 0.7 add_convert_fusion
  (4 shorter events, 0.1 us)
Async XLA Ops:
  153.7 3.1 %copy-start.1 = (f32[256,2]{0,1:T(2,128)S(1)}, f32[256,2]{0,1:T(2,128)}, u32[]{:S(2)}) copy-start(f32[256,2]{0,1:T(2,128)} %param.10) | copy-start | bytes 6148
  156.5 1.2 copy-start

commit v21 on v19

--- a/solution.py
+++ b/solution.py
@@ -12,6 +12,7 @@
 CAP = 128
 COL = ("chip", "core")
 MESH = pl.DeviceIdType.MESH
+PIECES = 4
 
 
 def normalize(rows, norm_gain):
@@ -115,7 +116,7 @@
         copy.start()
         square_copies.append(copy)
 
-    half_rows = slots // 2
+    half_rows = slots // PIECES
 
     def rows_half(h):
         return pl.ds(h * half_rows, half_rows)
@@ -141,7 +142,7 @@
         ).wait_recv()
 
     sent = []
-    for h in (0, 1):
+    for h in range(PIECES):
         sent += [send(0, None, 1, partner, core, h), send(1, None, 2, up, core, h),
                  send(2, None, 3, down, core, h), send(7, None, 8, me, sister, h)]
     local = pltpu.make_async_copy(src, place(0), local_sem)
@@ -154,7 +155,7 @@
         total = total + squares[b]
     squares[0] = lax.rsqrt(total / (blocks * width) + 1e-05)
 
-    for h in (0, 1):
+    for h in range(PIECES):
         arrive(0, 1, h)
         sent += [send(3, 1, 4, up, core, h), send(4, 1, 5, down, core, h),
                  send(8, 1, 9, me, sister, h)]
@@ -190,10 +191,10 @@
         if rows_part is None:
             lax.fori_loop(0, chunks, one, 0)
         else:
-            lax.fori_loop(rows_part * chunks // 2, (rows_part + 1) * chunks // 2, one, 0)
+            lax.fori_loop(rows_part * chunks // PIECES, (rows_part + 1) * chunks // PIECES, one, 0)
 
     absorb(0, first=True)
-    for h in (0, 1):
+    for h in range(PIECES):
         arrive(3, 4, h)
         sent.append(send(11, 4, 12, me, sister, h))
         arrive(4, 5, h)
@@ -204,7 +205,7 @@
         sent.append(send(14, 7, 15, me, sister, h))
     absorb(4)
     for first_place in (8, 12):
-        for h in (0, 1):
+        for h in range(PIECES):
             for tag in range(first_place - 1, first_place + 3):
                 arrive(tag, tag + 1, h)
             absorb(first_place, rows_part=h)
@@ -247,8 +248,8 @@
             pltpu.VMEM((slots, hidden_units), jnp.float32),
             pltpu.VMEM((slots, hidden_units), jnp.float32),
             pltpu.VMEM((blocks, slots // 256, 256), jnp.float32),
-            pltpu.SemaphoreType.DMA((15, 2)),
-            pltpu.SemaphoreType.DMA((15, 2)),
+            pltpu.SemaphoreType.DMA((15, PIECES)),
+            pltpu.SemaphoreType.DMA((15, PIECES)),
             pltpu.SemaphoreType.DMA(()),
             pltpu.SemaphoreType.DMA((2, blocks)),
             pltpu.SemaphoreType.DMA((blocks,)),

time: 158 us -> 160 us (1.013)
    pallas_call x1, Pallas kernels: 76.9 us -> 80.8 us  [expert_in(): pl.pallas_call(functools.partial(expert_in_kernel, width), out_shape=jax....]
    pallas_call x1, Pallas kernels: 70.4 us -> 67.4 us  [scatter_cols(): pl.pallas_call(functools.partial(scatter_kernel, width), out_shape=jax.Sh...]
where the time goes in v21:
time: 160 us; the launch traced here: 159 us
  Pallas kernels  148 us (92%)
  local copies, waits for them, and re-layouts  5.06 us (3%)
  other arithmetic  3.64 us (2%)
  matrix products  2.07 us (1%)
    pallas_call x1, Pallas kernels, expert_in(): pl.pallas_call(functools.partial(expert_in_kernel, width), out_shape=jax....  80.8 us
    pallas_call x1, Pallas kernels, scatter_cols(): pl.pallas_call(functools.partial(scatter_kernel, width), out_shape=jax.Sh...  67.4 us

profile of v21, /device:TPU:0, one launch (start us, length us, event | category | flops | bytes accessed | tf_op | source)
XLA Modules:
  0.0 159.1 jit_solution(2448801265741553847)
XLA Ops:
  0.0 0.8 copy.21
  0.8 0.1 eq.42
  1.0 1.1 reduce-window.6
  2.1 0.2 slice_reduce_fusion
  2.4 0.1 eq.38
  2.5 0.1 fusion.2
  2.6 0.1 reduce_sum.30
  2.8 0.1 copy.23
  2.8 0.7 compare_select_fusion
  3.5 0.3 convert_reduce_fusion
  3.8 2.1 %convolution_convert_fusion = bf16[1024,256]{1,0:T(8,128)(2,1)} fusion(bf16[256,256]{1,0:T(8,128)(2,1)} %param.7, bf16[256,1024]{1,0:T(8,128)(2,1)S(1)} %convert_reduce_fusion), kind=kOutput, calls=%fused_computation.3 | convolution fusion | flops 134479872 | bytes 1179648 | tf_op jit(solution)/shard_map/ts,td->sd/dot_general | solution.py:457
  5.9 80.8 %shard_map.73.hidden = bf16[1024,896]{1,0:T(8,128)(2,1)} custom-call(bf16[8,128,256]{2,1,0:T(8,128)(2,1)} %bitcast.20, f32[1,4096]{1,0:T(1,128)} %bitcast.21, bf16[4096,896]{1,0:T(8,128)(2,1)} %bitcast.17, bf16[4096,896]{1,0:T(8,128)(2,1)} %bitcast.18), custom_call_target="tpu_custom_call" | custom-call | tf_op jit(solution)/shard_map/pallas_call | solution.py:235
  86.7 67.4 %shard_map.74 = f32[8,128,256]{2,1,0:T(8,128)} custom-call(bf16[1024,896]{1,0:T(8,128)(2,1)} %shard_map.73.hidden, bf16[896,4096]{1,0:T(8,128)(2,1)} %bitcast.19), custom_call_target="tpu_custom_call" | custom-call | tf_op jit(solution)/shard_map/pallas_call | solution.py:424
  154.0 0.1 copy.24
  154.2 0.1 reshape.42
  154.3 0.0 copy-start.1
  154.4 2.8 %gather_fusion = f32[512,256]{1,0:T(8,128)S(1)} fusion(f32[1024,256]{1,0:T(8,128)} %bitcast.16, s32[1024]{0:T(1024)S(1)} %pad_clamp_fusion), kind=kCustom, calls=%fused_computation | custom fusion | bytes 1050624 | tf_op jit(solution)/shard_map/gather | solution.py:39
  157.2 0.0 copy-start
  157.2 0.3 reshape.41
  157.5 0.0 copy-done.1
  157.5 0.1 copy.25
  157.6 0.7 multiply_reduce_fusion
  158.4 0.0 copy-done
  158.4 0.7 add_convert_fusion
  (4 shorter events, 0.1 us)
Async XLA Ops:
  154.3 3.1 %copy-start.1 = (f32[256,2]{0,1:T(2,128)S(1)}, f32[256,2]{0,1:T(2,128)}, u32[]{:S(2)}) copy-start(f32[256,2]{0,1:T(2,128)} %param.10) | copy-start | bytes 6148
  157.2 1.2 copy-start
